TPU v7x, 32 devices: a whole 2x2x4 slice. The times are simulated.
32 devices in a mesh: dom: 32 (over z, y, x, core).
Axes of the slice: x: 2, y: 2, z: 4, core: 2. Of those that a mesh axis runs over, the one named last changes fastest.
Arguments:
- hidden: bfloat16 [49152, 1024], P('dom'), may hold values from -6 to 6
- bases: bfloat16 [1024, 1224], replicated, may hold values from -0.1875 to 0.1875
- self_weight: bfloat16 [1024, 153], replicated, may hold values from -0.1875 to 0.1875
- coef: float32 [5, 8], replicated, may hold values from -3 to 3
- bias: float32 [153], replicated, may hold values from -3 to 3
- edge_src: int32 [196608], P('dom'), may hold values from 0 to 1535
- edge_dst: int32 [196608], P('dom'), may hold values from 0 to 1535
- edge_rel: int32 [196608], P('dom'), may hold values from 0 to 4
- send_rows: int32 [32, 32, 72], P('dom'), may hold values from 0 to 1536, as said below
- recv_rows: int32 [32, 32, 72], P('dom'), may hold values from 0 to 1536, as said below
- labels: int32 [49152], P('dom'), may hold values from 0 to 152
- train_mask: int32 [49152], P('dom'), may hold values from 0 to 1, as said below
- bnd_rows: int32 [32, 32, 8], P('dom'), may hold values from 0 to 1536, as said below
- tiles: float32 [1536, 128, 128], P('dom'), may hold values from 0 to 0.003515625
- tile_cols: int32 [1536], P('dom'), may hold values from 0 to 13, as said below
Outputs:
- smoothed: float32 [49152, 153], P('dom')
Inputs may be any that keep to these rules, and one draw needn't show every extreme that they name: `send_rows`: entries below 1536 are rows of the sending partition and come first in each block; 1536 marks an empty slot. Every row of a partition is sent exactly once over all peers, and one peer of every partition receives a full block of 72. The slot k of recv_rows[d, s] receives the row in slot k of send_rows[s, d]; its entries below 1536 are rows of d, each row of d named exactly once over all s; 1536 marks an empty slot, exactly where the matching send slot is empty. `bnd_rows`: entries below 1536 are rows of the sending partition; 1536 marks an empty slot. Every partition fills all 8 slots for one peer. `train_mask`: every partition holds at least one known label. `tile_cols`: A partition's tiles come in order of row blocks, 4 to a block; the first 2 of a block name local column blocks (below 12), the others halo column blocks; every halo column block is named in every partition.
All inputs are finite; a program needn't handle non-finite values. Where the computation divides by a largest or mean magnitude, that divisor is 1e-20 or more.
Results may differ from a plain program's by a relative error of at most 0.0003.
Values sent between devices are 32-bit elements; how exact they have to be, the bound alone decides.
No kernel may reach another device: no remote copies, remote signals or barrier semaphores. Data moves between devices by JAX's collectives and lax.ppermute only.
A program may use at most 128 MiB of HBM per device.

v0:
```python
import jax
import jax.numpy as jnp
from jax import lax
from jax.sharding import PartitionSpec as P

NB = 8
REL = 5
TB = 128
TILES_ROW = 4
LOC_ROW = 2
ITERS = 3


correct_rate = 0.8
smooth_rate = 0.75
tiny = 1e-06


def device_scores(hid, src, dst, rel, bases, self_weight, coef, bias):
    nrow = hid.shape[0]
    classes = self_weight.shape[1]
    proj = jnp.dot(hid, bases, preferred_element_type=jnp.float32).reshape(nrow, NB, classes)
    mixed = jnp.einsum("nbc,rb->rnc", proj, coef, precision=lax.Precision.HIGHEST)
    msgs = mixed[rel, src]
    segment = dst * REL + rel
    counts = jax.ops.segment_sum(jnp.ones(src.shape, jnp.float32), segment, num_segments=nrow * REL)
    weight = 1.0 / counts[segment]
    agg = jax.ops.segment_sum(msgs * weight[:, None], dst, num_segments=nrow)
    return jnp.dot(hid, self_weight, preferred_element_type=jnp.float32) + agg + bias


def propagate(state, bnd_rows, tiles, tile_cols):
    nrow, classes = state.shape
    local_blocks = nrow // TB
    padded = jnp.concatenate([state, jnp.zeros((1, classes), jnp.float32)], 0)
    outgoing = padded[bnd_rows[0]]
    blocks = tile_cols.reshape(local_blocks, TILES_ROW)
    plates = tiles.reshape(local_blocks, TILES_ROW, TB, TB)
    own_cols = state.reshape(local_blocks, TB, classes)[blocks[:, :LOC_ROW]]
    near_part = jnp.einsum(
        "rsij,rsjc->ric", plates[:, :LOC_ROW], own_cols, precision=lax.Precision.HIGHEST
    )
    arrived = lax.all_to_all(outgoing, "dom", split_axis=0, concat_axis=0, tiled=True)
    halo = arrived.reshape(-1, TB, classes)
    far_cols = halo[blocks[:, LOC_ROW:] - local_blocks]
    far_part = jnp.einsum(
        "rsij,rsjc->ric", plates[:, LOC_ROW:], far_cols, precision=lax.Precision.HIGHEST
    )
    return (near_part + far_part).reshape(nrow, classes)


def on_device(
    hidden,
    bases,
    self_weight,
    coef,
    bias,
    edge_src,
    edge_dst,
    edge_rel,
    send_rows,
    recv_rows,
    labels,
    train_mask,
    bnd_rows,
    tiles,
    tile_cols,
):
    scores = device_scores(hidden, edge_src, edge_dst, edge_rel, bases, self_weight, coef, bias)
    nrow, classes = scores.shape
    padded = jnp.concatenate([scores, jnp.zeros((1, classes), jnp.float32)], 0)
    outgoing = padded[send_rows[0]]
    arrived = lax.all_to_all(outgoing, "dom", split_axis=0, concat_axis=0, tiled=True)
    base = jnp.zeros((nrow + 1, classes), jnp.float32).at[recv_rows[0]].set(arrived)[:nrow]
    onehot = (labels[:, None] == jnp.arange(classes, dtype=jnp.int32)[None, :]).astype(jnp.float32)
    known = train_mask[:, None].astype(jnp.float32)
    error0 = known * (onehot - base)
    total, counted = lax.psum((jnp.sum(jnp.mean(jnp.abs(error0), -1)), jnp.sum(known)), "dom")
    sigma = total / counted
    carried = error0
    for step in range(ITERS):
        carried = (1.0 - correct_rate) * error0 + correct_rate * propagate(
            carried, bnd_rows, tiles, tile_cols
        )
    magnitude = jnp.mean(jnp.abs(carried), -1, keepdims=True) + tiny
    corrected = base + sigma * carried / magnitude
    start = known * onehot + (1.0 - known) * corrected
    smoothed = start
    for step in range(ITERS):
        smoothed = (1.0 - smooth_rate) * start + smooth_rate * propagate(
            smoothed, bnd_rows, tiles, tile_cols
        )
    return smoothed


def solution(mesh):
    in_specs = (
        P("dom", None),
        P(),
        P(),
        P(),
        P(),
        P("dom"),
        P("dom"),
        P("dom"),
        P("dom", None, None),
        P("dom", None, None),
        P("dom"),
        P("dom"),
        P("dom", None, None),
        P("dom", None, None),
        P("dom"),
    )
    out_specs = P("dom", None)
    return jax.shard_map(
        on_device, mesh=mesh, in_specs=in_specs, out_specs=out_specs, check_vma=False
    )
```

profile of v0, /device:TPU:0, one launch (start us, length us, event | category | flops | bytes accessed | tf_op | source)
XLA Modules:
  0.0 553.2 jit_solution(11795791018430098617)
XLA Ops:
  1.0 32.6 %scatter_custom_fusion = f32[7680]{0:T(1024)S(1)} fusion(s32[6144]{0:T(1024)S(1)} %get-tuple-element.10, f32[6144]{0:T(1024)S(1)} %broadcast.150, f32[]{:T(128)} %constant.16.clone.1), kind=kCustom, calls=%fused_computation.100 | custom fusion | flops 6144 | bytes 30724 | tf_op jit(solution)/shard_map/scatter-add | solution.py:26
  33.5 34.3 %gather_fusion = f32[6144]{0:T(1024)S(1)} fusion(f32[7680]{0:T(1024)S(1)} %scatter_custom_fusion, s32[6144]{0:T(1024)S(1)} %get-tuple-element.9), kind=kCustom, calls=%fused_computation.1 | custom fusion | bytes 73728 | tf_op jit(solution)/shard_map/gather | solution.py:27
  67.9 8.0 %fusion.50 = f32[1536,1224]{0,1:T(8,128)} fusion(bf16[1536,1024]{1,0:T(8,128)(2,1)S(1)} %copy-done, bf16[1024,1224]{0,1:T(8,128)(2,1)} %param.16), kind=kOutput, calls=%fused_computation.114 | convolution fusion | flops 3850371072 | bytes 13172736 | tf_op jit(solution)/shard_map/dot_general | solution.py:22
  75.9 7.1 %reshape.172 = f32[1536,8,153]{0,2,1:T(8,128)} reshape(f32[1536,1224]{0,1:T(8,128)} %fusion.50) | data formatting | bytes 15040512 | tf_op jit(solution)/shard_map/reshape | solution.py:22
  83.0 15.5 %fusion.4 = f32[5,1536,153]{1,0,2:T(8,128)} fusion(f32[1536,8,153]{0,2,1:T(8,128)} %reshape.172, f32[5,8]{1,0:T(8,128)S(1)} %copy-done.25), kind=kOutput, calls=%fused_computation.28 | convolution fusion | flops 112803840 | bytes 12220576 | tf_op jit(solution)/shard_map/nbc,rb->rnc/dot_general | solution.py:23
  98.5 8.6 %copy.51 = f32[5,1536,153]{2,1,0:T(8,128)} copy(f32[5,1536,153]{1,0,2:T(8,128)} %fusion.4) | data formatting | bytes 9400320 | tf_op jit(solution)/shard_map/nbc,rb->rnc/dot_general | solution.py:23
  107.1 2.1 convolution_add_fusion
  109.2 2.9 copy.52
  112.2 79.4 %scatter_custom_fusion.1 = f32[1536,153]{1,0:T(8,128)} fusion(f32[1536,153]{1,0:T(8,128)} %copy.52, s32[6144]{0:T(1024)} %param.21, f32[6144]{0:T(1024)S(1)} %broadcast_divide_fusion, f32[5,1536,153]{2,1,0:T(8,128)} %copy.51, s32[6144]{0:T(1024)S(1)} %get-tuple-element.11), kind=kCustom, calls=%fused_computation.26 | custom fusion | flops 1880064 | bytes 8853504 | tf_op jit(solution)/shard_map/scatter-add | solution.py:28
  193.2 6.5 %gather_fusion.1 = f32[2304,153]{1,0:T(8,128)} fusion(f32[1537,153]{1,0:T(8,128)S(1)} %concatenate.25, s32[3072]{0:T(1024)S(1)} %pad_clamp_fusion), kind=kCustom, calls=%fused_computation.2 | custom fusion | bytes 2829312 | tf_op jit(solution)/shard_map/gather | solution.py:72
  199.6 7.4 %all-to-all-start = ((f32[32,72,153]{2,1,0:T(8,128)}), f32[32,72,153]{2,1,0:T(8,128)S(1)}, u32[]{:S(2)}, u32[]{:S(2)}) async-start(f32[32,72,153]{2,1,0:T(8,128)} %bitcast.204), calls=%async_computation | async-start | bytes 4718592 | tf_op jit(solution)/shard_map/all_to_all | solution.py:73
  207.5 54.0 %all-to-all-done = f32[32,72,153]{2,1,0:T(8,128)S(1)} async-done(((f32[32,72,153]{2,1,0:T(8,128)}), f32[32,72,153]{2,1,0:T(8,128)S(1)}, u32[]{:S(2)}, u32[]{:S(2)}) %all-to-all-start) | async-done | bytes 1410080 | tf_op jit(solution)/shard_map/all_to_all | solution.py:73
  262.9 13.7 %scatter_custom_fusion.2 = f32[1537,153]{1,0:T(8,128)S(1)} fusion(s32[2304]{0:T(1024)S(1)} %reshape.371, f32[2304,153]{1,0:T(8,128)} %bitcast.205, f32[]{:T(128)} %constant.16.clone.1), kind=kCustom, calls=%fused_computation.84 | custom fusion | bytes 941156 | tf_op jit(solution)/shard_map/scatter | solution.py:74
  280.1 3.1 gather_fusion.3
  283.2 4.3 all-to-all-start.1
  287.8 3.8 gather_fusion.2
  291.6 6.5 %all-to-all-done.1 = f32[32,8,153]{2,1,0:T(8,128)S(1)} async-done(((f32[32,8,153]{2,1,0:T(8,128)}), f32[32,8,153]{2,1,0:T(8,128)S(1)}, u32[]{:S(2)}, u32[]{:S(2)}) %all-to-all-start.1) | async-done | bytes 156704 | tf_op jit(solution)/shard_map/all_to_all | solution.py:43
  300.7 3.6 convolution_bitcast_fusion.11
  304.4 6.1 %fusion.10 = f32[12,128,153]{1,2,0:T(8,128)} fusion(f32[12,153,128]{2,1,0:T(8,128)S(1)} %convolution_bitcast_fusion.11, f32[12,2,128,153]{3,2,1,0:T(8,128)S(1)} %bitcast.199, f32[12,4,128,128]{3,2,1,0:T(8,128)S(1)} %bitcast.175), kind=kOutput, calls=%fused_computation.56 | convolution fusion | flops 722414592 | bytes 6641664 | tf_op jit(solution)/shard_map/rsij,rsjc->ric/dot_general | solution.py:40
  310.5 2.8 copy.91
  313.3 2.4 bitcast_add_fusion.5
  318.2 3.1 gather_fusion.6
  321.3 3.7 all-to-all-start.2
  325.0 3.8 gather_fusion.5
  328.8 6.7 %all-to-all-done.2 = f32[32,8,153]{2,1,0:T(8,128)} async-done(((f32[32,8,153]{2,1,0:T(8,128)}), f32[32,8,153]{2,1,0:T(8,128)}, u32[]{:S(2)}, u32[]{:S(2)}) %all-to-all-start.2) | async-done | bytes 156704 | tf_op jit(solution)/shard_map/all_to_all | solution.py:43
  338.6 3.6 convolution_bitcast_fusion.10
  342.2 6.1 %fusion.13 = f32[12,128,153]{1,2,0:T(8,128)} fusion(f32[12,153,128]{2,1,0:T(8,128)S(1)} %convolution_bitcast_fusion.10, f32[12,2,128,153]{3,2,1,0:T(8,128)S(1)} %bitcast.200, f32[12,4,128,128]{3,2,1,0:T(8,128)S(1)} %bitcast.177), kind=kOutput, calls=%fused_computation.59 | convolution fusion | flops 722414592 | bytes 6641664 | tf_op jit(solution)/shard_map/rsij,rsjc->ric/dot_general | solution.py:40
  348.4 2.8 copy.92
  351.2 2.4 bitcast_add_fusion.4
  356.1 3.1 gather_fusion.9
  359.1 3.5 all-to-all-start.3
  363.3 3.8 gather_fusion.8
  367.1 6.1 %all-to-all-done.3 = f32[32,8,153]{2,1,0:T(8,128)} async-done(((f32[32,8,153]{2,1,0:T(8,128)}), f32[32,8,153]{2,1,0:T(8,128)}, u32[]{:S(2)}, u32[]{:S(2)}) %all-to-all-start.3) | async-done | bytes 156704 | tf_op jit(solution)/shard_map/all_to_all | solution.py:43
  376.2 3.6 convolution_bitcast_fusion.9
  379.9 6.1 %fusion.16 = f32[12,128,153]{1,2,0:T(8,128)} fusion(f32[12,153,128]{2,1,0:T(8,128)S(1)} %convolution_bitcast_fusion.9, f32[12,2,128,153]{3,2,1,0:T(8,128)S(1)} %bitcast.201, f32[12,4,128,128]{3,2,1,0:T(8,128)S(1)} %bitcast.179), kind=kOutput, calls=%fused_computation.62 | convolution fusion | flops 722414592 | bytes 6641664 | tf_op jit(solution)/shard_map/rsij,rsjc->ric/dot_general | solution.py:40
  386.0 2.8 copy.93
  388.9 2.8 abs_reduce_fusion.1
  392.3 38.8 %all-reduce.7 = (f32[]{:T(128)}, f32[]{:T(128)}) all-reduce(f32[]{:T(128)} %multiply_reduce_fusion, f32[]{:T(128)} %get-tuple-element.13), channel_id=1, replica_groups=mesh['dom'=32] {'dom'}, use_global_device_ids=true, to_apply=%region_5.0 | all-reduce | flops 2 | bytes 16 | tf_op jit(solution)/shard_map/psum | solution.py:78
  432.4 3.3 multiply_add_fusion
  438.2 3.1 gather_fusion.12
  441.2 4.3 all-to-all-start.4
  445.5 3.8 gather_fusion.11
  449.3 6.7 %all-to-all-done.4 = f32[32,8,153]{2,1,0:T(8,128)} async-done(((f32[32,8,153]{2,1,0:T(8,128)}), f32[32,8,153]{2,1,0:T(8,128)}, u32[]{:S(2)}, u32[]{:S(2)}) %all-to-all-start.4) | async-done | bytes 156704 | tf_op jit(solution)/shard_map/all_to_all | solution.py:43
  459.1 3.6 convolution_bitcast_fusion.8
  462.7 6.1 %fusion.19 = f32[12,128,153]{1,2,0:T(8,128)} fusion(f32[12,153,128]{2,1,0:T(8,128)S(1)} %convolution_bitcast_fusion.8, f32[12,2,128,153]{3,2,1,0:T(8,128)S(1)} %bitcast.203, f32[12,4,128,128]{3,2,1,0:T(8,128)S(1)} %bitcast.181), kind=kOutput, calls=%fused_computation.65 | convolution fusion | flops 722414592 | bytes 6641664 | tf_op jit(solution)/shard_map/rsij,rsjc->ric/dot_general | solution.py:40
  468.9 2.8 copy.94
  471.7 2.1 bitcast_add_fusion.2
  476.2 3.1 gather_fusion.15
  479.3 3.6 all-to-all-start.5
  482.9 3.8 gather_fusion.14
  486.7 6.7 %all-to-all-done.5 = f32[32,8,153]{2,1,0:T(8,128)} async-done(((f32[32,8,153]{2,1,0:T(8,128)}), f32[32,8,153]{2,1,0:T(8,128)}, u32[]{:S(2)}, u32[]{:S(2)}) %all-to-all-start.5) | async-done | bytes 156704 | tf_op jit(solution)/shard_map/all_to_all | solution.py:43
  496.5 3.6 convolution_bitcast_fusion.7
  500.1 6.1 %fusion.22 = f32[12,128,153]{1,2,0:T(8,128)} fusion(f32[12,153,128]{2,1,0:T(8,128)S(1)} %convolution_bitcast_fusion.7, f32[12,2,128,153]{3,2,1,0:T(8,128)S(1)} %bitcast.202, f32[12,4,128,128]{3,2,1,0:T(8,128)S(1)} %bitcast.183), kind=kOutput, calls=%fused_computation.68 | convolution fusion | flops 722414592 | bytes 6641664 | tf_op jit(solution)/shard_map/rsij,rsjc->ric/dot_general | solution.py:40
  506.2 2.8 copy.95
  509.1 2.1 bitcast_add_fusion.1
  513.6 3.1 gather_fusion.18
  516.7 2.9 all-to-all-start.6
  519.5 3.8 gather_fusion.17
  523.3 6.8 %all-to-all-done.6 = f32[32,8,153]{2,1,0:T(8,128)S(1)} async-done(((f32[32,8,153]{2,1,0:T(8,128)}), f32[32,8,153]{2,1,0:T(8,128)S(1)}, u32[]{:S(2)}, u32[]{:S(2)}) %all-to-all-start.6) | async-done | bytes 156704 | tf_op jit(solution)/shard_map/all_to_all | solution.py:43
  533.9 3.6 convolution_bitcast_fusion.6
  537.5 6.1 %fusion.25 = f32[12,128,153]{1,2,0:T(8,128)} fusion(f32[12,153,128]{2,1,0:T(8,128)S(1)} %convolution_bitcast_fusion.6, f32[12,2,128,153]{3,2,1,0:T(8,128)S(1)} %bitcast.198, f32[12,4,128,128]{3,2,1,0:T(8,128)S(1)} %bitcast.185), kind=kOutput, calls=%fused_computation.71 | convolution fusion | flops 722414592 | bytes 6641664 | tf_op jit(solution)/shard_map/rsij,rsjc->ric/dot_general | solution.py:40
  543.6 2.8 copy.96
  546.5 3.4 bitcast_add_fusion
  549.9 2.8 copy.78
  (96 shorter events, 40.1 us)
Async XLA Ops:
  0.0 67.9 %copy-start = (bf16[1536,1024]{1,0:T(8,128)(2,1)S(1)}, bf16[1536,1024]{1,0:T(8,128)(2,1)}, u32[]{:S(2)}) copy-start(bf16[1536,1024]{1,0:T(8,128)(2,1)} %param.15) | copy-start | bytes 9437188
  75.9 7.1 %copy-start.25 = (f32[5,8]{1,0:T(8,128)S(1)}, f32[5,8]{1,0:T(8,128)}, u32[]{:S(2)}) copy-start(f32[5,8]{1,0:T(8,128)} %param.18) | copy-start | bytes 484
  98.5 8.6 %copy-start.18 = (bf16[1024,153]{0,1:T(8,128)(2,1)S(1)}, bf16[1024,153]{0,1:T(8,128)(2,1)}, u32[]{:S(2)}) copy-start(bf16[1024,153]{0,1:T(8,128)(2,1)} %param.17) | copy-start | bytes 940036
  98.5 8.6 %copy-start.23 = (f32[153]{0:T(256)S(1)}, f32[153]{0:T(256)}, u32[]{:S(2)}) copy-start(f32[153]{0:T(256)} %param.19) | copy-start | bytes 1840
  191.5 1.5 copy-start.21
  199.6 7.4 %copy-start.22 = (s32[1,32,72]{2,1,0:T(8,128)S(1)}, s32[1,32,72]{2,1,0:T(8,128)}, u32[]{:S(2)}) copy-start(s32[1,32,72]{2,1,0:T(8,128)} %param.24) | copy-start | bytes 27652
  199.6 7.5 %copy-start.20 = (s32[1536]{0:T(1024)S(1)}, s32[1536]{0:T(1024)}, u32[]{:S(2)}) copy-start(s32[1536]{0:T(1024)} %param.26) | copy-start | bytes 18436
  199.6 7.5 %copy-start.24 = (s32[1,32,8]{1,2,0:T(8,128)S(1)}, s32[1,32,8]{1,2,0:T(8,128)}, u32[]{:S(2)}) copy-start(s32[1,32,8]{1,2,0:T(8,128)} %param.27) | copy-start | bytes 3076
  199.6 7.7 %copy-start.26 = (s32[48]{0:T(128)S(1)}, s32[48]{0:T(128)}, u32[]{:S(2)}) copy-start(s32[48]{0:T(128)} %param.29) | copy-start | bytes 580
  199.6 77.0 %copy-start.19 = (s32[1536]{0:T(1024)S(1)}, s32[1536]{0:T(1024)}, u32[]{:S(2)}) copy-start(s32[1536]{0:T(1024)} %param.25) | copy-start | bytes 18436
  199.6 61.8 %all-to-all-start = ((f32[32,72,153]{2,1,0:T(8,128)}), f32[32,72,153]{2,1,0:T(8,128)S(1)}, u32[]{:S(2)}, u32[]{:S(2)}) async-start(f32[32,72,153]{2,1,0:T(8,128)} %bitcast.204), calls=%async_computation | async-start | bytes 4718592 | tf_op jit(solution)/shard_map/all_to_all | solution.py:73
  261.4 1.4 copy-start.16
  276.6 3.5 copy-start.4
  277.7 1.2 copy-start.5
  283.2 14.9 %all-to-all-start.1 = ((f32[32,8,153]{2,1,0:T(8,128)}), f32[32,8,153]{2,1,0:T(8,128)S(1)}, u32[]{:S(2)}, u32[]{:S(2)}) async-start(f32[32,8,153]{2,1,0:T(8,128)} %bitcast.12), calls=%async_computation.1 | async-start | bytes 524288 | tf_op jit(solution)/shard_map/all_to_all | solution.py:43
  298.2 2.5 copy-start.2
  300.7 3.6 copy-start.11
  315.8 1.2 copy-start.8
  321.3 14.3 %all-to-all-start.2 = ((f32[32,8,153]{2,1,0:T(8,128)}), f32[32,8,153]{2,1,0:T(8,128)}, u32[]{:S(2)}, u32[]{:S(2)}) async-start(f32[32,8,153]{2,1,0:T(8,128)} %bitcast.208), calls=%async_computation.2 | async-start | bytes 524288 | tf_op jit(solution)/shard_map/all_to_all | solution.py:43
  338.6 3.6 copy-start.12
  353.6 1.2 copy-start.6
  359.1 14.0 %all-to-all-start.3 = ((f32[32,8,153]{2,1,0:T(8,128)}), f32[32,8,153]{2,1,0:T(8,128)}, u32[]{:S(2)}, u32[]{:S(2)}) async-start(f32[32,8,153]{2,1,0:T(8,128)} %bitcast.206), calls=%async_computation.3 | async-start | bytes 524288 | tf_op jit(solution)/shard_map/all_to_all | solution.py:43
  376.2 3.6 copy-start.13
  435.7 1.2 copy-start.3
  441.2 14.8 %all-to-all-start.4 = ((f32[32,8,153]{2,1,0:T(8,128)}), f32[32,8,153]{2,1,0:T(8,128)}, u32[]{:S(2)}, u32[]{:S(2)}) async-start(f32[32,8,153]{2,1,0:T(8,128)} %bitcast.210), calls=%async_computation.4 | async-start | bytes 524288 | tf_op jit(solution)/shard_map/all_to_all | solution.py:43
  459.1 3.6 copy-start.15
  473.8 1.2 copy-start.9
  479.3 14.1 %all-to-all-start.5 = ((f32[32,8,153]{2,1,0:T(8,128)}), f32[32,8,153]{2,1,0:T(8,128)}, u32[]{:S(2)}, u32[]{:S(2)}) async-start(f32[32,8,153]{2,1,0:T(8,128)} %bitcast.209), calls=%async_computation.5 | async-start | bytes 524288 | tf_op jit(solution)/shard_map/all_to_all | solution.py:43
  496.5 3.6 copy-start.14
  511.2 1.2 copy-start.7
  516.7 13.4 %all-to-all-start.6 = ((f32[32,8,153]{2,1,0:T(8,128)}), f32[32,8,153]{2,1,0:T(8,128)S(1)}, u32[]{:S(2)}, u32[]{:S(2)}) async-start(f32[32,8,153]{2,1,0:T(8,128)} %bitcast.207), calls=%async_computation.6 | async-start | bytes 524288 | tf_op jit(solution)/shard_map/all_to_all | solution.py:43
  530.1 0.7 copy-start.17
  533.9 3.6 copy-start.10
  546.5 6.2 %copy-start.1 = (bf16[1536,1024]{1,0:T(8,128)(2,1)S(1)}, bf16[1536,1024]{1,0:T(8,128)(2,1)}, u32[]{:S(2)}) copy-start(bf16[1536,1024]{1,0:T(8,128)(2,1)} %param.15) | copy-start | bytes 9437188
where the time goes:
time: 564 us; the launch traced here: 553 us
  local copies, waits for them, and re-layouts  171 us (30%)
  other arithmetic  134 us (24%)
  waiting for transfers between devices  93.6 us (17%)
  matrix products  84.2 us (15%)
  blocking collectives  38.8 us (7%)
  starting transfers between devices  29.6 us (5%)
    scatter-add x1, other arithmetic, device_scores(): agg = jax.ops.segment_sum(msgs * weight[:, None], dst, num_segments=nrow)  79.4 us
    all_to_all x1, waiting for transfers between devices, on_device(): lax.all_to_all(outgoing, 'dom', split_axis=0, concat_axis=0, tiled=True)  54 us
    all_to_all x6, waiting for transfers between devices, propagate(): lax.all_to_all(outgoing, 'dom', split_axis=0, concat_axis=0, tiled=True)  39.6 us
    psum x1, blocking collectives, on_device(): lax.psum((jnp.sum(jnp.mean(jnp.abs(error0), -1)), jnp.sum(known)), 'dom')  38.8 us
    dot_general x6, matrix products, propagate(): jnp.einsum('rsij,rsjc->ric', plates[:, :LOC_ROW], own_cols, precision=lax...  36.9 us
    gather x1, local copies, waits for them, and re-layouts, device_scores(): weight = 1.0 / counts[segment]  34.3 us
    scatter-add x1, other arithmetic, device_scores(): jax.ops.segment_sum(jnp.ones(src.shape, jnp.float32), segment, num_segmen...  32.6 us
    gather x6, local copies, waits for them, and re-layouts, propagate(): own_cols = state.reshape(local_blocks, TB, classes)[blocks[:, :LOC_ROW]]  22.8 us
  transfers between devices with their start and end apart: 7, of which 7 were waited for; matrix products, arithmetic and copies ran while one was open for 4% of the time, Pallas kernels for 0%

commit v1 on v0

v1 whole, which is shorter than its diff:
```python
import functools

import jax
import jax.numpy as jnp
from jax import lax
from jax.experimental import pallas as pl
from jax.experimental.pallas import tpu as pltpu
from jax.sharding import PartitionSpec as P

TILES_ROW = 4
LOC_ROW = 2
ITERS = 3
L = 128

correct_rate = 0.8
smooth_rate = 0.75
tiny = 1e-06

F32 = jnp.float32
BF16 = jnp.bfloat16
VM = pl.BlockSpec(memory_space=pltpu.VMEM)
SM = pl.BlockSpec(memory_space=pltpu.SMEM)
MIB = 1 << 20


def up(a, b):
    return -(-a // b)


def split(x):
    hi = x.astype(BF16)
    return hi, (x - hi.astype(F32)).astype(BF16)


def dot(a, b):
    return jnp.dot(a, b, preferred_element_type=F32)


def lanes(rows):
    return lax.broadcasted_iota(jnp.int32, (rows, L), 1)


def pair(ref, row):
    return ref.at[pl.ds(pl.multiple_of(2 * row, 2), 2), :]


def gather_rows(idx_ref, src, stg, peers, slots):
    def body(p, _):
        for k in range(slots):
            row = idx_ref[0, p, k]
            pair(stg, p * slots + k)[...] = pair(src, row)[...]
        return 0

    lax.fori_loop(0, peers, body, 0)


def scores_kernel(
    hid, bases, self_w, bias, coef, es, ed, er, send, out,
    whi, wlo, m2, s0, s1, sc2, stg, kv, ks, sem, *, classes, slots, per, blk,
):
    n, hdim = hid.shape
    rest = classes - L
    nrel, nb = coef.shape
    peers = out.shape[0]
    erows = es.shape[0]
    kv[0] = (er[...] * n + es[...]) * 2
    kv[1] = (er[...] * n + ed[...]) * 2
    copy = pltpu.make_async_copy(kv, ks, sem)
    copy.start()

    step = 32

    def mix(i, _):
        rows = pl.ds(pl.multiple_of(i * step, step), step)
        parts = [bases[rows, b * classes : (b + 1) * classes].astype(F32) for b in range(nb)]
        for r in range(nrel):
            w = coef[r, 0] * parts[0]
            for b in range(1, nb):
                w = w + coef[r, b] * parts[b]
            hi, lo = split(w)
            whi[rows, r * 2 * L : r * 2 * L + classes] = hi
            wlo[rows, r * 2 * L : r * 2 * L + classes] = lo
        whi[rows, nrel * 2 * L : nrel * 2 * L + classes] = self_w[rows, :]
        return 0

    lax.fori_loop(0, hdim // step, mix, 0)

    s0[...] = jnp.zeros_like(s0)
    s1[...] = jnp.zeros_like(s1)
    sc2[pl.ds(2 * n, 16), :] = jnp.zeros((16, L), F32)

    chunk = 256
    lane = lanes(chunk)

    def project(i, _):
        row = pl.multiple_of(i * chunk, chunk)
        h = hid[pl.ds(row, chunk), :]
        for r in range(nrel):
            cols = pl.ds(r * 2 * L, 2 * L)
            a = dot(h, whi[:, cols]) + dot(h, wlo[:, cols])
            at = 2 * (r * n + row)
            m2[pl.ds(at, chunk, stride=2), :] = a[:, :L]
            tail = jnp.where(lane < rest, a[:, L:], jnp.where(lane == rest, 1.0, 0.0))
            m2[pl.ds(at + 1, chunk, stride=2), :] = tail
        a = dot(h, whi[:, pl.ds(nrel * 2 * L, 2 * L)])
        sc2[pl.ds(2 * row, chunk, stride=2), :] = a[:, :L] + bias[0:1, :]
        tail = jnp.where(lane < rest, a[:, L:] + bias[1:2, :], 0.0)
        sc2[pl.ds(2 * row + 1, chunk, stride=2), :] = tail
        return 0

    lax.fori_loop(0, n // chunk, project, 0)
    copy.wait()

    half = erows // 2

    def edges(t, _):
        for l in range(L):
            for c, s in enumerate((s0, s1)):
                j = ks[0, t + c * half, l]
                d = ks[1, t + c * half, l]
                src = m2[pl.ds(pl.multiple_of(j, 2), 2), :]
                at = pl.ds(pl.multiple_of(d, 2), 2)
                s[at, :] = s[at, :] + src
        return 0

    lax.fori_loop(0, half, edges, 0)

    fin = 64
    flane = lanes(fin)

    def finish(i, _):
        row = i * fin
        a0 = sc2[pl.ds(2 * row, fin, stride=2), :]
        a1 = sc2[pl.ds(2 * row + 1, fin, stride=2), :]
        for r in range(nrel):
            at = 2 * (r * n + row)
            m = s0[pl.ds(at, fin, stride=2), :] + s1[pl.ds(at, fin, stride=2), :]
            t = s0[pl.ds(at + 1, fin, stride=2), :] + s1[pl.ds(at + 1, fin, stride=2), :]
            inv = 1.0 / jnp.maximum(t[:, rest : rest + 1], 1.0)
            a0 = a0 + m * inv
            a1 = a1 + t * inv
        sc2[pl.ds(2 * row, fin, stride=2), :] = a0
        sc2[pl.ds(2 * row + 1, fin, stride=2), :] = jnp.where(flane < rest, a1, 0.0)
        return 0

    lax.fori_loop(0, n // fin, finish, 0)

    gather_rows(send, sc2, stg, peers, slots)
    ntail = up(slots, per)

    def put(p, _):
        at = p * 2 * slots
        out[p, 0:slots, :] = stg[pl.ds(at, slots, stride=2), :]
        tail = stg[pl.ds(at + 1, ntail, stride=2 * per), :]
        for q in range(1, per):
            x = stg[pl.ds(at + 2 * q + 1, ntail, stride=2 * per), :]
            tail = tail + pltpu.roll(x, q * rest, axis=1)
        out[p, slots : slots + ntail, :] = tail
        return 0

    lax.fori_loop(0, peers, put, 0)


def pack(bnd, v2, stg, out, extra, *, peers, slots, per, rest):
    gather_rows(bnd, v2, stg, peers, slots)
    ntail = up(slots, per)
    blk = slots + ntail
    for k in range(slots):
        out[pl.ds(k, peers, stride=blk), :] = stg[pl.ds(2 * k, peers, stride=2 * slots), :]
    for j in range(ntail):
        tail = None
        for q in range(min(per, slots - j * per)):
            x = stg[pl.ds(2 * (j * per + q) + 1, peers, stride=2 * slots), :]
            x = pltpu.roll(x, q * rest, axis=1) if q else x
            tail = x if tail is None else tail + x
        if j == 0 and extra is not None:
            tail = tail + extra
        out[pl.ds(slots + j, peers, stride=blk), :] = tail


def errors_kernel(arr, recv, bnd, labk, base, e0, eh, el, out, stg, base2, v2, stgb, *, classes, per):
    n = base.shape[0]
    rest = classes - L
    peers, blk, _ = arr.shape
    slots = recv.shape[2]
    ntail = up(slots, per)
    tlane = lanes(ntail)

    def unpack(p, _):
        at = p * 2 * slots
        tail = arr[p, slots : slots + ntail, :]
        for q in range(per):
            x = pltpu.roll(tail, (L - q * rest) % L, axis=1) if q else tail
            x = jnp.where(tlane < rest, x, 0.0)
            stg[pl.ds(at + 2 * q + 1, ntail, stride=2 * per), :] = x
        stg[pl.ds(at, slots, stride=2), :] = arr[p, 0:slots, :]
        return 0

    lax.fori_loop(0, peers, unpack, 0)

    def spread(p, _):
        for k in range(slots):
            row = recv[0, p, k]
            pair(base2, row)[...] = pair(stg, p * slots + k)[...]
        return 0

    lax.fori_loop(0, peers, spread, 0)

    chunk = 128
    lane = lanes(chunk)

    def error(i, _):
        row = pl.multiple_of(i * chunk, chunk)
        rows = pl.ds(row, chunk)
        lab = labk[rows, :]
        known = lab >= 0.0
        for h in range(2):
            cols = slice(h * L, (h + 1) * L)
            b = base2[pl.ds(2 * row + h, chunk, stride=2), :]
            onehot = jnp.where(lab == (lane + h * L).astype(F32), 1.0, 0.0)
            e = jnp.where(known, onehot - b, 0.0)
            base[rows, cols] = b
            e0[rows, cols] = e
            hi, lo = split(e)
            eh[rows, cols] = hi
            el[rows, cols] = lo
            v2[pl.ds(2 * row + h, chunk, stride=2), :] = e
        return 0

    lax.fori_loop(0, n // chunk, error, 0)
    v2[pl.ds(2 * n, 16), :] = jnp.zeros((16, L), F32)
    pack(bnd, v2, stgb, out, None, peers=peers, slots=bnd.shape[2], per=per, rest=rest)


def tiles_kernel(tiles, cols, labels, mask, nh, nl, fh, fl, labk, cnt):
    blocks = labels.shape[0]
    halo = fh.shape[1] // L

    def body(b, _):
        rows = pl.ds(pl.multiple_of(b * L, L), L)
        for j in range(LOC_ROW):
            hi, lo = split(tiles[b * TILES_ROW + j])
            nh[rows, j * L : (j + 1) * L] = hi
            nl[rows, j * L : (j + 1) * L] = lo
        for q in range(halo):
            acc = jnp.zeros((L, L), F32)
            for j in range(LOC_ROW, TILES_ROW):
                hit = cols[b * TILES_ROW + j] == blocks + q
                acc = acc + jnp.where(hit, tiles[b * TILES_ROW + j], 0.0)
            hi, lo = split(acc)
            fh[rows, q * L : (q + 1) * L] = hi
            fl[rows, q * L : (q + 1) * L] = lo
        lab = jnp.where(mask[pl.ds(b, 1), :] > 0, labels[pl.ds(b, 1), :], -1).astype(F32)
        labk[rows, :] = jnp.broadcast_to(lab, (L, L)).T
        return 0

    lax.fori_loop(0, blocks, body, 0)
    cnt[...] = jnp.zeros(cnt.shape, F32) + jnp.sum(mask[...].astype(F32))


def near_kernel(vh, vl, e, nh, nl, cols, *rest_refs, rate, classes, sums):
    if sums:
        cnt, part, tot = rest_refs
    else:
        (part,) = rest_refs
    blocks = vh.shape[0] // L

    def body(b, acc):
        rows = pl.ds(pl.multiple_of(b * L, L), L)
        at = [pl.ds(pl.multiple_of(cols[b * TILES_ROW + j] * L, L), L) for j in range(LOC_ROW)]
        bh = jnp.concatenate([vh[a, :] for a in at], 0)
        bl = jnp.concatenate([vl[a, :] for a in at], 0)
        a2 = dot(jnp.concatenate([nh[rows, :], nl[rows, :]], 0), bh)
        near = a2[:L] + a2[L:] + dot(nh[rows, :], bl)
        ev = e[rows, :]
        part[rows, :] = (1.0 - rate) * ev + rate * near
        if sums:
            mag = jnp.abs(ev)
            mag = mag[:, :L] + mag[:, L:]
            acc = acc + jnp.sum(mag.reshape(L // 8, 8, L), 0)
        return acc

    acc = lax.fori_loop(0, blocks, body, jnp.zeros((8, L), F32))
    if sums:
        total = jnp.sum(acc) * (1.0 / classes)
        lane = lanes(8)
        tot[...] = jnp.where(lane == L - 2, total, jnp.where(lane == L - 1, cnt[...], 0.0))


def far_kernel(*refs, rate, classes, per, mode, peers, slots, n):
    rest = classes - L
    refs = list(refs)
    arr, fh, fl, part = refs[:4]
    refs = refs[4:]
    if mode != "last":
        bnd = refs.pop(0)
    if mode == "sums":
        tot = refs.pop(0)
    if mode == "turn":
        base, labk, start = refs.pop(0), refs.pop(0), refs.pop(2)
    if mode == "last":
        out, hm, hr = refs
    else:
        vh, vl, out, hm, hr, v2, stgb = refs
    ntail = up(slots, per)
    blk = slots + ntail
    tlane = lanes(peers)
    for k in range(slots):
        hm[pl.ds(k, peers, stride=slots), :] = arr[pl.ds(k, peers, stride=blk), :]
    for j in range(ntail):
        tail = arr[pl.ds(slots + j, peers, stride=blk), :]
        if j == 0 and mode == "turn":
            sums = jnp.sum(tail, axis=0, keepdims=True)
            sigma = sums[:, L - 2 : L - 1] / sums[:, L - 1 : L]
        for q in range(min(per, slots - j * per)):
            x = pltpu.roll(tail, (L - q * rest) % L, axis=1) if q else tail
            x = jnp.where(tlane < rest, x, 0.0)
            hr[pl.ds(j * per + q, peers, stride=slots), :] = x
    hh, hl = split(jnp.concatenate([hm[...], hr[...]], 1))

    chunk = 256
    lane = lanes(chunk)

    def body(i, _):
        row = pl.multiple_of(i * chunk, chunk)
        rows = pl.ds(row, chunk)
        a2 = dot(jnp.concatenate([fh[rows, :], fl[rows, :]], 0), hh)
        far = a2[:chunk] + a2[chunk:] + dot(fh[rows, :], hl)
        v = part[rows, :] + rate * far
        if mode == "last":
            out[rows, :] = v[:, :classes]
            return 0
        if mode == "turn":
            mag = jnp.abs(v)
            mag = jnp.sum(mag[:, :L] + mag[:, L:], -1, keepdims=True) * (1.0 / classes) + tiny
            scale = sigma / mag
            lab = labk[rows, :]
        for h in range(2):
            cols = slice(h * L, (h + 1) * L)
            x = v[:, cols]
            if mode == "turn":
                onehot = jnp.where(lab == (lane + h * L).astype(F32), 1.0, 0.0)
                x = jnp.where(lab >= 0.0, onehot, base[rows, cols] + scale * x)
                start[rows, cols] = x
            hi, lo = split(x)
            vh[rows, cols] = hi
            vl[rows, cols] = lo
            v2[pl.ds(2 * row + h, chunk, stride=2), :] = x
        return 0

    lax.fori_loop(0, n // chunk, body, 0)
    if mode != "last":
        v2[pl.ds(2 * n, 16), :] = jnp.zeros((16, L), F32)
        extra = tot[0:1, :] if mode == "sums" else None
        pack(bnd, v2, stgb, out, extra, peers=peers, slots=slots, per=per, rest=rest)


def call(kernel, outs, ins, args, scratch=(), vmem=0, flops=0, size=0, name=None):
    return pl.pallas_call(
        kernel,
        out_shape=outs,
        in_specs=ins,
        out_specs=jax.tree.map(lambda _: VM, outs),
        scratch_shapes=list(scratch),
        compiler_params=pltpu.CompilerParams(vmem_limit_bytes=vmem),
        cost_estimate=pl.CostEstimate(flops=flops, bytes_accessed=size, transcendentals=0),
        name=name,
    )(*args)


def swap(x):
    return lax.all_to_all(x, "dom", split_axis=0, concat_axis=0, tiled=True)


def on_device(
    peers, hidden, bases, self_weight, coef, bias, edge_src, edge_dst, edge_rel, send_rows, recv_rows, labels,
    train_mask, bnd_rows, tiles, tile_cols,
):
    n, hdim = hidden.shape
    classes = self_weight.shape[1]
    nrel, nb = coef.shape
    rest = classes - L
    per = (L - 2) // rest
    slots = send_rows.shape[2]
    bnd = bnd_rows.shape[2]
    ne = edge_src.shape[0]
    halo = peers * bnd
    sds = jax.ShapeDtypeStruct
    state = sds((n, 2 * L), F32)
    half = sds((n, 2 * L), BF16)
    blocks = n // L

    blk = up(slots + up(slots, per), 8) * 8
    bias2 = jnp.pad(bias, (0, 2 * L - classes)).reshape(2, L)
    square = lambda x: x.reshape(-1, L)
    stage = pltpu.VMEM((2 * (peers * slots + 16), L), F32)
    rows2 = pltpu.VMEM((2 * n + 16, L), F32)
    sent = call(
        functools.partial(scores_kernel, classes=classes, slots=slots, per=per, blk=blk),
        sds((peers, blk, L), F32),
        [VM, VM, VM, VM, SM, VM, VM, VM, SM],
        (hidden, bases, self_weight, bias2, coef, square(edge_src), square(edge_dst), square(edge_rel), send_rows),
        [
            pltpu.VMEM((hdim, (nrel + 1) * 2 * L), BF16),
            pltpu.VMEM((hdim, nrel * 2 * L), BF16),
            pltpu.VMEM((2 * nrel * n, L), F32),
            pltpu.VMEM((2 * nrel * n, L), F32),
            pltpu.VMEM((2 * nrel * n, L), F32),
            rows2,
            stage,
            pltpu.VMEM((2, ne // L, L), jnp.int32),
            pltpu.SMEM((2, ne // L, L), jnp.int32),
            pltpu.SemaphoreType.DMA,
        ],
        vmem=56 * MIB,
        name="scores",
    )
    arrived = swap(sent)
    nh, nl, fh, fl, labk, cnt = call(
        tiles_kernel,
        (half, half, sds((n, halo), BF16), sds((n, halo), BF16), sds((n, L), F32), sds((8, L), F32)),
        [VM, SM, VM, VM],
        (tiles, tile_cols, square(labels), square(train_mask)),
        vmem=28 * MIB,
        flops=10**7,
        size=8 * 10**6,
        name="tiles",
    )
    lines = peers * (bnd + up(bnd, per))
    packed = sds((lines, L), F32)
    stageb = pltpu.VMEM((2 * halo, L), F32)
    base, e, vh, vl, out = call(
        functools.partial(errors_kernel, classes=classes, per=per),
        (state, state, half, half, packed),
        [VM, SM, SM, VM],
        (arrived, recv_rows, bnd_rows, labk),
        [stage, rows2, rows2, stageb],
        vmem=28 * MIB,
        name="errors",
    )
    hscr = [pltpu.VMEM((halo, L), F32)] * 2
    for step in range(2 * ITERS):
        rate = correct_rate if step < ITERS else smooth_rate
        halos = swap(out.reshape(peers, 1, -1)).reshape(lines, L)
        sums = step == 0
        mode = "last" if step == 2 * ITERS - 1 else "turn" if step == ITERS - 1 else "sums" if step == ITERS - 2 else "step"
        got = call(
            functools.partial(near_kernel, rate=rate, classes=classes, sums=sums),
            (state, sds((8, L), F32)) if sums else (state,),
            [VM, VM, VM, VM, VM, SM] + [VM] * sums,
            (vh, vl, e, nh, nl, tile_cols) + ((cnt,) if sums else ()),
            vmem=16 * MIB,
            flops=10**9,
            size=8 * 10**6,
            name="near",
        )
        part = got[0]
        if sums:
            tot = got[1]
        far = functools.partial(
            far_kernel, rate=rate, classes=classes, per=per, mode=mode, peers=peers, slots=bnd, n=n
        )
        args, ins = (halos, fh, fl, part), [VM] * 4
        if mode == "last":
            return call(far, sds((n, classes), F32), ins, args, hscr, vmem=24 * MIB, name="far_last")
        args, ins = args + (bnd_rows,), ins + [SM]
        outs = (half, half, packed)
        if mode == "sums":
            args, ins = args + (tot,), ins + [VM]
        if mode == "turn":
            args, ins = args + (base, labk), ins + [VM, VM]
            outs = (half, half, state, packed)
        got = call(far, outs, ins, args, hscr + [rows2, stageb], vmem=24 * MIB, name="far_" + mode)
        if mode == "turn":
            vh, vl, e, out = got
        else:
            vh, vl, out = got


def solution(mesh):
    row = P("dom")
    in_specs = (
        P("dom", None), P(), P(), P(), P(), row, row, row, P("dom", None, None), P("dom", None, None), row, row,
        P("dom", None, None), P("dom", None, None), row,
    )
    return jax.shard_map(
        functools.partial(on_device, mesh.shape["dom"]),
        mesh=mesh,
        in_specs=in_specs,
        out_specs=P("dom", None),
        check_vma=False,
    )
```

time: 564 us -> 244 us (0.43); the launches traced: 553 us -> 242 us
  other arithmetic: 134 us -> 0 us
  Pallas kernels: 0 us -> 104 us
  local copies, waits for them, and re-layouts: 171 us -> 67.2 us
  matrix products: 84.2 us -> 0 us
  waiting for transfers between devices: 93.6 us -> 32.5 us
  blocking collectives: 38.8 us -> 0 us
  starting transfers between devices: 29.6 us -> 37.9 us
    scatter-add x2 -> x0, other arithmetic: 112 us -> none  [the longest x1 79.4 us: device_scores(): agg = jax.ops.segment_sum(msgs * weight[:, None], dst, num_segments=nrow)]
    pallas_call x0 -> x15, Pallas kernels: none -> 104 us  [call(): pl.pallas_call(kernel, out_shape=outs, in_specs=ins, out_specs=jax.tree.m...]
    gather x20 -> x0, local copies, waits for them, and re-layouts: 93.8 us -> none  [the longest x1 34.3 us: device_scores(): weight = 1.0 / counts[segment]]
    dot_general x15 -> x0, matrix products: 84.2 us -> none  [the longest x6 36.9 us: propagate(): jnp.einsum('rsij,rsjc->ric', plates[:, :LOC_ROW], own_cols, precision=lax...]
    all_to_all x7, waiting for transfers between devices: 93.6 us -> 32.5 us  [swap(): return lax.all_to_all(x, 'dom', split_axis=0, concat_axis=0, tiled=True)]
    unnamed x54 -> x113, local copies, waits for them, and re-layouts: 9.7 us -> 64.5 us
    psum x1 -> x0, blocking collectives: 38.8 us -> none  [on_device(): lax.psum((jnp.sum(jnp.mean(jnp.abs(error0), -1)), jnp.sum(known)), 'dom')]
    mul x6 -> x0, local copies, waits for them, and re-layouts: 17 us -> none  [the longest x3 8.5 us: on_device(): correct_rate * propagate(carried, bnd_rows, tiles, tile_cols)]
  transfers between devices with their start and end apart: 7 -> 7, of which waited for: 7 -> 7; matrix products, arithmetic and copies ran while one was open for 4% -> 0% of each run, Pallas kernels for 0% -> 9%
where the time goes in v1:
time: 244 us; the launch traced here: 242 us
  Pallas kernels  104 us (43%)
  local copies, waits for them, and re-layouts  67.2 us (28%)
  starting transfers between devices  37.9 us (16%)
  waiting for transfers between devices  32.5 us (13%)
    pallas_call x15, Pallas kernels, call(): pl.pallas_call(kernel, out_shape=outs, in_specs=ins, out_specs=jax.tree.m...  104 us
    unnamed x113, local copies, waits for them, and re-layouts  64.5 us
    all_to_all x7, starting transfers between devices, swap(): return lax.all_to_all(x, 'dom', split_axis=0, concat_axis=0, tiled=True)  37.9 us
    all_to_all x7, waiting for transfers between devices, swap(): return lax.all_to_all(x, 'dom', split_axis=0, concat_axis=0, tiled=True)  32.5 us
  transfers between devices with their start and end apart: 7, of which 7 were waited for; matrix products, arithmetic and copies ran while one was open for 0% of the time, Pallas kernels for 9%

profile of v1, /device:TPU:0, one launch (start us, length us, event | category | flops | bytes accessed | tf_op | source)
XLA Modules:
  0.0 242.1 jit_solution(17085477359518827667)
XLA Ops:
  0.0 1.2 pad_bitcast_fusion.bias
  1.2 2.0 copy.26.self_w
  3.2 4.4 %copy.25.bases = bf16[1024,1224]{1,0:T(8,128)(2,1)} copy(bf16[1024,1224]{0,1:T(8,128)(2,1)} %param.16) | data formatting | bytes 5013504 | tf_op args[1]
  7.6 51.7 %scores.1 = f32[32,88,128]{2,1,0:T(8,128)} custom-call(bf16[1536,1024]{1,0:T(8,128)(2,1)} %hid.1, bf16[1024,1224]{1,0:T(8,128)(2,1)} %copy.25.bases, bf16[1024,153]{1,0:T(8,128)(2,1)} %copy.26.self_w, f32[2,128]{1,0:T(2,128)} %pad_bitcast_fusion.bias, f32[5,8]{1,0:T(8,128)} %coef.1, s32[48,128]{1,0:T(8,128)} %bitcast.27, s32[48,128]{1,0:T(8,128)} %bitcast.28, ...), custom_call_target="tpu_custom_call" | custom-call | tf_op jit(solution)/shard_map/scores/pallas_call | solution.py:359
  59.4 7.4 %all-to-all-start = ((f32[32,88,128]{2,1,0:T(8,128)}), f32[32,88,128]{2,1,0:T(8,128)}, u32[]{:S(2)}, u32[]{:S(2)}) async-start(f32[32,88,128]{2,1,0:T(8,128)} %scores.1), calls=%async_computation | async-start | bytes 2883584 | tf_op jit(solution)/shard_map/all_to_all | solution.py:372
  67.0 1.9 copy-done.18
  68.9 2.3 tiles.2
  72.1 29.6 %all-to-all-done.arr = f32[32,88,128]{2,1,0:T(8,128)} async-done(((f32[32,88,128]{2,1,0:T(8,128)}), f32[32,88,128]{2,1,0:T(8,128)}, u32[]{:S(2)}, u32[]{:S(2)}) %all-to-all-start) | async-done | bytes 1441824 | tf_op jit(solution)/shard_map/all_to_all | solution.py:372
  101.7 1.1 copy-done.20
  102.8 8.3 %errors.1 = (f32[1536,256]{1,0:T(8,128)S(1)}, f32[1536,256]{1,0:T(8,128)S(1)}, bf16[1536,256]{1,0:T(8,128)(2,1)S(1)}, bf16[1536,256]{1,0:T(8,128)(2,1)S(1)}, f32[320,128]{1,0:T(8,128)}) custom-call(f32[32,88,128]{2,1,0:T(8,128)} %all-to-all-done.arr, s32[1,32,72]{2,1,0:T(8,128)S(1)} %copy-done.51, s32[1,32,8]{2,1,0:T(8,128)S(1)} %copy.27.bnd.refs_4_, ...), custom_call_target="tpu_custom_call" | custom-call | tf_op jit(solution)/shard_map/errors/pallas_call | solution.py:359
  111.1 1.2 copy-done
  112.3 1.2 copy-done.24
  115.2 3.6 %all-to-all-start.1 = ((f32[32,1,1280]{2,1,0:T(1,128)}), f32[32,1,1280]{2,1,0:T(1,128)S(1)}, u32[]{:S(2)}, u32[]{:S(2)}) async-start(f32[32,1,1280]{2,1,0:T(1,128)} %bitcast.6), calls=%async_computation.1 | async-start | bytes 327680 | tf_op jit(solution)/shard_map/all_to_all | solution.py:372
  118.9 1.4 copy-done.1
  120.3 1.1 copy-done.47
  121.4 1.1 copy-done.49
  122.6 3.4 %near.6 = (f32[1536,256]{1,0:T(8,128)S(1)}, f32[8,128]{1,0:T(8,128)S(1)}) custom-call(bf16[1536,256]{1,0:T(8,128)(2,1)S(1)} %copy-done.47, bf16[1536,256]{1,0:T(8,128)(2,1)S(1)} %copy-done.49, f32[1536,256]{1,0:T(8,128)S(1)} %copy-done.1, bf16[1536,256]{1,0:T(8,128)(2,1)S(1)} %get-tuple-element.41.nh, bf16[1536,256]{1,0:T(8,128)(2,1)S(1)} %get-tuple-element.42.nl, ...), custom_call_target="tpu_custom_call" | custom-call | flops 1000000000 | bytes 8000000 | tf_op jit(solution)/shard_map/near/pallas_call | solution.py:359
  126.0 1.2 copy-done.22
  127.5 1.4 copy-done.23
  128.9 3.9 %far_step.3 = (bf16[1536,256]{1,0:T(8,128)(2,1)S(1)}, bf16[1536,256]{1,0:T(8,128)(2,1)S(1)}, f32[320,128]{1,0:T(8,128)}) custom-call(f32[320,128]{1,0:T(8,128)S(1)} %bitcast.20, bf16[1536,256]{1,0:T(8,128)(2,1)S(1)} %get-tuple-element.36.refs_1_, bf16[1536,256]{1,0:T(8,128)(2,1)S(1)} %get-tuple-element.37.refs_2_, f32[1536,256]{1,0:T(8,128)S(1)} %copy-done.23, ...), custom_call_target="tpu_custom_call" | custom-call | tf_op jit(solution)/shard_map/far_step/pallas_call | solution.py:359
  134.6 5.4 %all-to-all-start.2 = ((f32[32,1,1280]{2,1,0:T(1,128)}), f32[32,1,1280]{2,1,0:T(1,128)S(1)}, u32[]{:S(2)}, u32[]{:S(2)}) async-start(f32[32,1,1280]{2,1,0:T(1,128)} %bitcast.8), calls=%async_computation.2 | async-start | bytes 327680 | tf_op jit(solution)/shard_map/all_to_all | solution.py:372
  140.0 1.4 copy-done.2
  141.4 1.1 copy-done.39
  142.6 1.1 copy-done.41
  143.7 3.3 %near.7.refs_3_ = f32[1536,256]{1,0:T(8,128)S(1)} custom-call(bf16[1536,256]{1,0:T(8,128)(2,1)S(1)} %copy-done.39, bf16[1536,256]{1,0:T(8,128)(2,1)S(1)} %copy-done.41, f32[1536,256]{1,0:T(8,128)S(1)} %copy-done.2, bf16[1536,256]{1,0:T(8,128)(2,1)S(1)} %get-tuple-element.41.nh, bf16[1536,256]{1,0:T(8,128)(2,1)S(1)} %get-tuple-element.42.nl, s32[48]{0:T(128)S(1)} %copy-done.50), custom_call_target="tpu_custom_call" | custom-call | flops 1000000000 | bytes 8000000 | tf_op jit(solution)/shard_map/near/pallas_call | solution.py:359
  147.0 1.2 copy-done.8
  148.7 1.4 copy-done.9
  150.1 3.8 %far_sums.1 = (bf16[1536,256]{1,0:T(8,128)(2,1)S(1)}, bf16[1536,256]{1,0:T(8,128)(2,1)S(1)}, f32[320,128]{1,0:T(8,128)}) custom-call(f32[320,128]{1,0:T(8,128)S(1)} %bitcast.21, bf16[1536,256]{1,0:T(8,128)(2,1)S(1)} %get-tuple-element.36.refs_1_, bf16[1536,256]{1,0:T(8,128)(2,1)S(1)} %get-tuple-element.37.refs_2_, f32[1536,256]{1,0:T(8,128)S(1)} %copy-done.9, ...), custom_call_target="tpu_custom_call" | custom-call | tf_op jit(solution)/shard_map/far_sums/pallas_call | solution.py:359
  155.7 5.4 %all-to-all-start.3 = ((f32[32,1,1280]{2,1,0:T(1,128)}), f32[32,1,1280]{2,1,0:T(1,128)S(1)}, u32[]{:S(2)}, u32[]{:S(2)}) async-start(f32[32,1,1280]{2,1,0:T(1,128)} %bitcast.10), calls=%async_computation.3 | async-start | bytes 327680 | tf_op jit(solution)/shard_map/all_to_all | solution.py:372
  161.1 1.4 copy-done.3
  162.5 1.1 copy-done.35
  163.6 1.1 copy-done.37
  164.8 3.3 %near.8.refs_3_ = f32[1536,256]{1,0:T(8,128)S(1)} custom-call(bf16[1536,256]{1,0:T(8,128)(2,1)S(1)} %copy-done.35, bf16[1536,256]{1,0:T(8,128)(2,1)S(1)} %copy-done.37, f32[1536,256]{1,0:T(8,128)S(1)} %copy-done.3, bf16[1536,256]{1,0:T(8,128)(2,1)S(1)} %get-tuple-element.41.nh, bf16[1536,256]{1,0:T(8,128)(2,1)S(1)} %get-tuple-element.42.nl, s32[48]{0:T(128)S(1)} %copy-done.50), custom_call_target="tpu_custom_call" | custom-call | flops 1000000000 | bytes 8000000 | tf_op jit(solution)/shard_map/near/pallas_call | solution.py:359
  168.0 1.1 copy-done.14
  169.7 1.4 copy-done.15
  171.1 1.1 copy-done.21
  172.2 1.4 copy-done.25
  173.7 5.0 %far_turn.1 = (bf16[1536,256]{1,0:T(8,128)(2,1)S(1)}, bf16[1536,256]{1,0:T(8,128)(2,1)S(1)}, f32[1536,256]{1,0:T(8,128)S(1)}, f32[320,128]{1,0:T(8,128)}) custom-call(f32[320,128]{1,0:T(8,128)S(1)} %bitcast.19, bf16[1536,256]{1,0:T(8,128)(2,1)S(1)} %get-tuple-element.36.refs_1_, bf16[1536,256]{1,0:T(8,128)(2,1)S(1)} %get-tuple-element.37.refs_2_, ...), custom_call_target="tpu_custom_call" | custom-call | tf_op jit(solution)/shard_map/far_turn/pallas_call | solution.py:359
  178.6 1.2 copy-done.4
  181.6 5.3 %all-to-all-start.4 = ((f32[32,1,1280]{2,1,0:T(1,128)}), f32[32,1,1280]{2,1,0:T(1,128)S(1)}, u32[]{:S(2)}, u32[]{:S(2)}) async-start(f32[32,1,1280]{2,1,0:T(1,128)} %bitcast.12), calls=%async_computation.4 | async-start | bytes 327680 | tf_op jit(solution)/shard_map/all_to_all | solution.py:372
  186.9 1.4 copy-done.5
  188.3 1.1 copy-done.31
  189.5 1.1 copy-done.33
  190.6 3.3 %near.9.refs_3_ = f32[1536,256]{1,0:T(8,128)S(1)} custom-call(bf16[1536,256]{1,0:T(8,128)(2,1)S(1)} %copy-done.31, bf16[1536,256]{1,0:T(8,128)(2,1)S(1)} %copy-done.33, f32[1536,256]{1,0:T(8,128)S(1)} %copy-done.5, bf16[1536,256]{1,0:T(8,128)(2,1)S(1)} %get-tuple-element.41.nh, bf16[1536,256]{1,0:T(8,128)(2,1)S(1)} %get-tuple-element.42.nl, s32[48]{0:T(128)S(1)} %copy-done.50), custom_call_target="tpu_custom_call" | custom-call | flops 1000000000 | bytes 8000000 | tf_op jit(solution)/shard_map/near/pallas_call | solution.py:359
  193.9 1.1 copy-done.12
  195.5 1.4 copy-done.13
  196.9 3.8 %far_step.4 = (bf16[1536,256]{1,0:T(8,128)(2,1)S(1)}, bf16[1536,256]{1,0:T(8,128)(2,1)S(1)}, f32[320,128]{1,0:T(8,128)}) custom-call(f32[320,128]{1,0:T(8,128)S(1)} %bitcast.24, bf16[1536,256]{1,0:T(8,128)(2,1)S(1)} %get-tuple-element.36.refs_1_, bf16[1536,256]{1,0:T(8,128)(2,1)S(1)} %get-tuple-element.37.refs_2_, f32[1536,256]{1,0:T(8,128)S(1)} %copy-done.13, ...), custom_call_target="tpu_custom_call" | custom-call | tf_op jit(solution)/shard_map/far_step/pallas_call | solution.py:359
  202.6 5.3 %all-to-all-start.5 = ((f32[32,1,1280]{2,1,0:T(1,128)}), f32[32,1,1280]{2,1,0:T(1,128)S(1)}, u32[]{:S(2)}, u32[]{:S(2)}) async-start(f32[32,1,1280]{2,1,0:T(1,128)} %bitcast.14), calls=%async_computation.5 | async-start | bytes 327680 | tf_op jit(solution)/shard_map/all_to_all | solution.py:372
  207.9 1.4 copy-done.6
  209.3 1.1 copy-done.43
  210.4 1.1 copy-done.45
  211.6 3.3 %near.10.refs_3_ = f32[1536,256]{1,0:T(8,128)S(1)} custom-call(bf16[1536,256]{1,0:T(8,128)(2,1)S(1)} %copy-done.43, bf16[1536,256]{1,0:T(8,128)(2,1)S(1)} %copy-done.45, f32[1536,256]{1,0:T(8,128)S(1)} %copy-done.6, bf16[1536,256]{1,0:T(8,128)(2,1)S(1)} %get-tuple-element.41.nh, bf16[1536,256]{1,0:T(8,128)(2,1)S(1)} %get-tuple-element.42.nl, s32[48]{0:T(128)S(1)} %copy-done.50), custom_call_target="tpu_custom_call" | custom-call | flops 1000000000 | bytes 8000000 | tf_op jit(solution)/shard_map/near/pallas_call | solution.py:359
  214.9 1.1 copy-done.10
  216.5 1.4 copy-done.11
  217.9 3.8 %far_step.5 = (bf16[1536,256]{1,0:T(8,128)(2,1)S(1)}, bf16[1536,256]{1,0:T(8,128)(2,1)S(1)}, f32[320,128]{1,0:T(8,128)}) custom-call(f32[320,128]{1,0:T(8,128)S(1)} %bitcast.23, bf16[1536,256]{1,0:T(8,128)(2,1)S(1)} %get-tuple-element.36.refs_1_, bf16[1536,256]{1,0:T(8,128)(2,1)S(1)} %get-tuple-element.37.refs_2_, f32[1536,256]{1,0:T(8,128)S(1)} %copy-done.11, ...), custom_call_target="tpu_custom_call" | custom-call | tf_op jit(solution)/shard_map/far_step/pallas_call | solution.py:359
  223.5 5.3 %all-to-all-start.6 = ((f32[32,1,1280]{2,1,0:T(1,128)}), f32[32,1,1280]{2,1,0:T(1,128)S(1)}, u32[]{:S(2)}, u32[]{:S(2)}) async-start(f32[32,1,1280]{2,1,0:T(1,128)} %bitcast.16), calls=%async_computation.6 | async-start | bytes 327680 | tf_op jit(solution)/shard_map/all_to_all | solution.py:372
  228.9 1.4 copy-done.7
  230.3 1.1 copy-done.27
  231.4 1.1 copy-done.29
  232.5 3.3 %near.11.refs_3_ = f32[1536,256]{1,0:T(8,128)S(1)} custom-call(bf16[1536,256]{1,0:T(8,128)(2,1)S(1)} %copy-done.27, bf16[1536,256]{1,0:T(8,128)(2,1)S(1)} %copy-done.29, f32[1536,256]{1,0:T(8,128)S(1)} %copy-done.7, bf16[1536,256]{1,0:T(8,128)(2,1)S(1)} %get-tuple-element.41.nh, bf16[1536,256]{1,0:T(8,128)(2,1)S(1)} %get-tuple-element.42.nl, s32[48]{0:T(128)S(1)} %copy-done.50), custom_call_target="tpu_custom_call" | custom-call | flops 1000000000 | bytes 8000000 | tf_op jit(solution)/shard_map/near/pallas_call | solution.py:359
  235.8 1.2 copy-done.16
  237.5 1.4 copy-done.17
  238.9 1.8 far_last.1
  240.7 1.4 copy.39
  (80 shorter events, 14.7 us)
Async XLA Ops:
  59.4 7.5 %copy-start.54 = (s32[1,32,8]{1,2,0:T(8,128)S(1)}, s32[1,32,8]{1,2,0:T(8,128)}, u32[]{:S(2)}) copy-start(s32[1,32,8]{1,2,0:T(8,128)} %param.27) | copy-start | bytes 3076
  59.4 7.6 %copy-start.50 = (s32[48]{0:T(128)S(1)}, s32[48]{0:T(128)}, u32[]{:S(2)}) copy-start(s32[48]{0:T(128)} %cols.13) | copy-start | bytes 580
  59.4 7.6 %copy-start.52 = (s32[1536]{0:T(1024)S(1)}, s32[1536]{0:T(1024)}, u32[]{:S(2)}) copy-start(s32[1536]{0:T(1024)} %param.25) | copy-start | bytes 18436
  59.4 7.6 %copy-start.53 = (s32[1536]{0:T(1024)S(1)}, s32[1536]{0:T(1024)}, u32[]{:S(2)}) copy-start(s32[1536]{0:T(1024)} %param.26) | copy-start | bytes 18436
  59.4 42.3 %all-to-all-start = ((f32[32,88,128]{2,1,0:T(8,128)}), f32[32,88,128]{2,1,0:T(8,128)}, u32[]{:S(2)}, u32[]{:S(2)}) async-start(f32[32,88,128]{2,1,0:T(8,128)} %scores.1), calls=%async_computation | async-start | bytes 2883584 | tf_op jit(solution)/shard_map/all_to_all | solution.py:372
  67.0 1.9 copy-start.18
  68.8 32.8 %copy-start.51 = (s32[1,32,72]{2,1,0:T(8,128)S(1)}, s32[1,32,72]{2,1,0:T(8,128)}, u32[]{:S(2)}) copy-start(s32[1,32,72]{2,1,0:T(8,128)} %recv.1) | copy-start | bytes 27652
  71.2 0.9 copy-start.19
  101.7 1.1 copy-start.20
  111.1 1.2 copy-start
  112.3 1.2 copy-start.24
  113.4 0.9 copy-start.46
  114.3 0.9 copy-start.48
  115.2 12.3 %all-to-all-start.1 = ((f32[32,1,1280]{2,1,0:T(1,128)}), f32[32,1,1280]{2,1,0:T(1,128)S(1)}, u32[]{:S(2)}, u32[]{:S(2)}) async-start(f32[32,1,1280]{2,1,0:T(1,128)} %bitcast.6), calls=%async_computation.1 | async-start | bytes 327680 | tf_op jit(solution)/shard_map/all_to_all | solution.py:372
  118.9 1.4 copy-start.1
  120.3 1.1 copy-start.47
  121.4 1.1 copy-start.49
  126.0 1.2 copy-start.22
  127.5 1.4 copy-start.23
  132.8 0.9 copy-start.38
  133.7 0.9 copy-start.40
  134.6 14.1 %all-to-all-start.2 = ((f32[32,1,1280]{2,1,0:T(1,128)}), f32[32,1,1280]{2,1,0:T(1,128)S(1)}, u32[]{:S(2)}, u32[]{:S(2)}) async-start(f32[32,1,1280]{2,1,0:T(1,128)} %bitcast.8), calls=%async_computation.2 | async-start | bytes 327680 | tf_op jit(solution)/shard_map/all_to_all | solution.py:372
  140.0 1.4 copy-start.2
  141.4 1.1 copy-start.39
  142.6 1.1 copy-start.41
  147.0 1.2 copy-start.8
  148.7 1.4 copy-start.9
  153.9 0.9 copy-start.34
  154.8 0.9 copy-start.36
  155.7 14.0 %all-to-all-start.3 = ((f32[32,1,1280]{2,1,0:T(1,128)}), f32[32,1,1280]{2,1,0:T(1,128)S(1)}, u32[]{:S(2)}, u32[]{:S(2)}) async-start(f32[32,1,1280]{2,1,0:T(1,128)} %bitcast.10), calls=%async_computation.3 | async-start | bytes 327680 | tf_op jit(solution)/shard_map/all_to_all | solution.py:372
  161.1 1.4 copy-start.3
  162.5 1.1 copy-start.35
  163.6 1.1 copy-start.37
  168.0 1.2 copy-start.14
  169.7 1.4 copy-start.15
  171.1 1.1 copy-start.21
  172.2 1.4 copy-start.25
  178.6 1.2 copy-start.4
  179.8 0.9 copy-start.30
  180.7 0.9 copy-start.32
  181.6 14.0 %all-to-all-start.4 = ((f32[32,1,1280]{2,1,0:T(1,128)}), f32[32,1,1280]{2,1,0:T(1,128)S(1)}, u32[]{:S(2)}, u32[]{:S(2)}) async-start(f32[32,1,1280]{2,1,0:T(1,128)} %bitcast.12), calls=%async_computation.4 | async-start | bytes 327680 | tf_op jit(solution)/shard_map/all_to_all | solution.py:372
  186.9 1.4 copy-start.5
  188.3 1.1 copy-start.31
  189.5 1.1 copy-start.33
  193.9 1.2 copy-start.12
  195.5 1.4 copy-start.13
  200.8 0.9 copy-start.42
  201.7 0.9 copy-start.44
  202.6 14.0 %all-to-all-start.5 = ((f32[32,1,1280]{2,1,0:T(1,128)}), f32[32,1,1280]{2,1,0:T(1,128)S(1)}, u32[]{:S(2)}, u32[]{:S(2)}) async-start(f32[32,1,1280]{2,1,0:T(1,128)} %bitcast.14), calls=%async_computation.5 | async-start | bytes 327680 | tf_op jit(solution)/shard_map/all_to_all | solution.py:372
  207.9 1.4 copy-start.6
  209.3 1.1 copy-start.43
  210.4 1.1 copy-start.45
  214.9 1.2 copy-start.10
  216.5 1.4 copy-start.11
  221.8 0.9 copy-start.26
  222.6 0.9 copy-start.28
  223.5 14.0 %all-to-all-start.6 = ((f32[32,1,1280]{2,1,0:T(1,128)}), f32[32,1,1280]{2,1,0:T(1,128)S(1)}, u32[]{:S(2)}, u32[]{:S(2)}) async-start(f32[32,1,1280]{2,1,0:T(1,128)} %bitcast.16), calls=%async_computation.6 | async-start | bytes 327680 | tf_op jit(solution)/shard_map/all_to_all | solution.py:372
  228.9 1.4 copy-start.7
  230.3 1.1 copy-start.27
  231.4 1.1 copy-start.29
  235.8 1.2 copy-start.16
  237.5 1.4 copy-start.17

commit v2 on v1

--- a/solution.py
+++ b/solution.py
@@ -20,6 +20,7 @@
 BF16 = jnp.bfloat16
 VM = pl.BlockSpec(memory_space=pltpu.VMEM)
 SM = pl.BlockSpec(memory_space=pltpu.SMEM)
+HB = pl.BlockSpec(memory_space=pltpu.HBM)
 MIB = 1 << 20
 
 
@@ -178,13 +179,16 @@
         out[pl.ds(slots + j, peers, stride=blk), :] = tail
 
 
-def errors_kernel(arr, recv, bnd, labk, base, e0, eh, el, out, stg, base2, v2, stgb, *, classes, per):
-    n = base.shape[0]
+def errors_kernel(
+    arr, recv, bnd, labk_hbm, base_hbm, e_hbm, out, stg, base2, v2, stgb, labk, sems, *, classes, per, n
+):
     rest = classes - L
     peers, blk, _ = arr.shape
     slots = recv.shape[2]
     ntail = up(slots, per)
     tlane = lanes(ntail)
+    load = pltpu.make_async_copy(labk_hbm, labk, sems.at[0])
+    load.start()
 
     def unpack(p, _):
         at = p * 2 * slots
@@ -205,34 +209,33 @@
         return 0
 
     lax.fori_loop(0, peers, spread, 0)
+    keep = pltpu.make_async_copy(base2, base_hbm, sems.at[1])
+    keep.start()
+    load.wait()
 
     chunk = 128
     lane = lanes(chunk)
 
     def error(i, _):
         row = pl.multiple_of(i * chunk, chunk)
-        rows = pl.ds(row, chunk)
-        lab = labk[rows, :]
+        lab = labk[pl.ds(row, chunk), :]
         known = lab >= 0.0
         for h in range(2):
-            cols = slice(h * L, (h + 1) * L)
-            b = base2[pl.ds(2 * row + h, chunk, stride=2), :]
+            rows = pl.ds(2 * row + h, chunk, stride=2)
             onehot = jnp.where(lab == (lane + h * L).astype(F32), 1.0, 0.0)
-            e = jnp.where(known, onehot - b, 0.0)
-            base[rows, cols] = b
-            e0[rows, cols] = e
-            hi, lo = split(e)
-            eh[rows, cols] = hi
-            el[rows, cols] = lo
-            v2[pl.ds(2 * row + h, chunk, stride=2), :] = e
+            v2[rows, :] = jnp.where(known, onehot - base2[rows, :], 0.0)
         return 0
 
     lax.fori_loop(0, n // chunk, error, 0)
     v2[pl.ds(2 * n, 16), :] = jnp.zeros((16, L), F32)
+    save = pltpu.make_async_copy(v2, e_hbm, sems.at[2])
+    save.start()
     pack(bnd, v2, stgb, out, None, peers=peers, slots=bnd.shape[2], per=per, rest=rest)
-
-
-def tiles_kernel(tiles, cols, labels, mask, nh, nl, fh, fl, labk, cnt):
+    keep.wait()
+    save.wait()
+
+
+def tiles_kernel(tiles, cols, labels, mask, nh_hbm, nl_hbm, fh, fl, lab_hbm, cnt, nh, nl, labk, sems):
     blocks = labels.shape[0]
     halo = fh.shape[1] // L
 
@@ -255,15 +258,38 @@
         return 0
 
     lax.fori_loop(0, blocks, body, 0)
+    pairs = ((nh, nh_hbm), (nl, nl_hbm), (labk, lab_hbm))
+    saves = [pltpu.make_async_copy(a, b, sems.at[i]) for i, (a, b) in enumerate(pairs)]
+    for c in saves:
+        c.start()
     cnt[...] = jnp.zeros(cnt.shape, F32) + jnp.sum(mask[...].astype(F32))
-
-
-def near_kernel(vh, vl, e, nh, nl, cols, *rest_refs, rate, classes, sums):
+    for c in saves:
+        c.wait()
+
+
+def near_kernel(v_hbm, e_hbm, nh_hbm, nl_hbm, cols, *refs, rate, classes, sums):
     if sums:
-        cnt, part, tot = rest_refs
+        cnt, part, tot, v2, e2, nh, nl, vh, vl, sems = refs
     else:
-        (part,) = rest_refs
-    blocks = vh.shape[0] // L
+        part, v2, e2, nh, nl, vh, vl, sems = refs
+    pairs = ((v_hbm, v2), (nh_hbm, nh), (nl_hbm, nl), (e_hbm, e2))
+    loads = [pltpu.make_async_copy(a, b, sems.at[i]) for i, (a, b) in enumerate(pairs)]
+    for c in loads:
+        c.start()
+    blocks = part.shape[0] // L
+    loads[0].wait()
+
+    def halve(b, _):
+        rows = pl.ds(pl.multiple_of(b * L, L), L)
+        for h in range(2):
+            hi, lo = split(v2[pl.ds(b * 2 * L + h, L, stride=2), :])
+            vh[rows, h * L : (h + 1) * L] = hi
+            vl[rows, h * L : (h + 1) * L] = lo
+        return 0
+
+    lax.fori_loop(0, blocks, halve, 0)
+    for c in loads[1:]:
+        c.wait()
 
     def body(b, acc):
         rows = pl.ds(pl.multiple_of(b * L, L), L)
@@ -272,12 +298,11 @@
         bl = jnp.concatenate([vl[a, :] for a in at], 0)
         a2 = dot(jnp.concatenate([nh[rows, :], nl[rows, :]], 0), bh)
         near = a2[:L] + a2[L:] + dot(nh[rows, :], bl)
-        ev = e[rows, :]
-        part[rows, :] = (1.0 - rate) * ev + rate * near
-        if sums:
-            mag = jnp.abs(ev)
-            mag = mag[:, :L] + mag[:, L:]
-            acc = acc + jnp.sum(mag.reshape(L // 8, 8, L), 0)
+        for h in range(2):
+            ev = e2[pl.ds(b * 2 * L + h, L, stride=2), :]
+            part[rows, h * L : (h + 1) * L] = (1.0 - rate) * ev + rate * near[:, h * L : (h + 1) * L]
+            if sums:
+                acc = acc + jnp.sum(jnp.abs(ev).reshape(L // 8, 8, L), 0)
         return acc
 
     acc = lax.fori_loop(0, blocks, body, jnp.zeros((8, L), F32))
@@ -297,11 +322,17 @@
     if mode == "sums":
         tot = refs.pop(0)
     if mode == "turn":
-        base, labk, start = refs.pop(0), refs.pop(0), refs.pop(2)
+        base_hbm, lab_hbm, base2, labk, sems = refs.pop(0), refs.pop(0), refs.pop(), refs.pop(), refs.pop()
+        loads = [
+            pltpu.make_async_copy(base_hbm, base2, sems.at[0]),
+            pltpu.make_async_copy(lab_hbm, labk, sems.at[1]),
+        ]
+        for c in loads:
+            c.start()
     if mode == "last":
         out, hm, hr = refs
     else:
-        vh, vl, out, hm, hr, v2, stgb = refs
+        v_hbm, out, hm, hr, v2, stgb, vsem = refs
     ntail = up(slots, per)
     blk = slots + ntail
     tlane = lanes(peers)
@@ -317,6 +348,9 @@
             x = jnp.where(tlane < rest, x, 0.0)
             hr[pl.ds(j * per + q, peers, stride=slots), :] = x
     hh, hl = split(jnp.concatenate([hm[...], hr[...]], 1))
+    if mode == "turn":
+        for c in loads:
+            c.wait()
 
     chunk = 256
     lane = lanes(chunk)
@@ -328,7 +362,8 @@
         far = a2[:chunk] + a2[chunk:] + dot(fh[rows, :], hl)
         v = part[rows, :] + rate * far
         if mode == "last":
-            out[rows, :] = v[:, :classes]
+            out[0:L, rows] = v[:, :L].T
+            out[L:classes, rows] = v[:, L:].T[:rest]
             return 0
         if mode == "turn":
             mag = jnp.abs(v)
@@ -336,31 +371,33 @@
             scale = sigma / mag
             lab = labk[rows, :]
         for h in range(2):
-            cols = slice(h * L, (h + 1) * L)
-            x = v[:, cols]
+            x = v[:, h * L : (h + 1) * L]
+            rows2 = pl.ds(2 * row + h, chunk, stride=2)
             if mode == "turn":
                 onehot = jnp.where(lab == (lane + h * L).astype(F32), 1.0, 0.0)
-                x = jnp.where(lab >= 0.0, onehot, base[rows, cols] + scale * x)
-                start[rows, cols] = x
-            hi, lo = split(x)
-            vh[rows, cols] = hi
-            vl[rows, cols] = lo
-            v2[pl.ds(2 * row + h, chunk, stride=2), :] = x
+                x = jnp.where(lab >= 0.0, onehot, base2[rows2, :] + scale * x)
+            v2[rows2, :] = x
         return 0
 
     lax.fori_loop(0, n // chunk, body, 0)
     if mode != "last":
         v2[pl.ds(2 * n, 16), :] = jnp.zeros((16, L), F32)
+        save = pltpu.make_async_copy(v2, v_hbm, vsem)
+        save.start()
         extra = tot[0:1, :] if mode == "sums" else None
         pack(bnd, v2, stgb, out, extra, peers=peers, slots=slots, per=per, rest=rest)
-
-
-def call(kernel, outs, ins, args, scratch=(), vmem=0, flops=0, size=0, name=None):
+        save.wait()
+
+
+def call(kernel, outs, ins, args, scratch=(), vmem=0, flops=0, size=0, name=None, specs=None):
+    if specs:
+        outs = tuple(pltpu.HBM(o.shape, o.dtype) if p is HB else o for o, p in zip(outs, specs))
+    args = [pltpu.with_memory_space_constraint(a, pltpu.HBM) if p is HB else a for a, p in zip(args, ins)]
     return pl.pallas_call(
         kernel,
         out_shape=outs,
         in_specs=ins,
-        out_specs=jax.tree.map(lambda _: VM, outs),
+        out_specs=specs or jax.tree.map(lambda _: VM, outs),
         scratch_shapes=list(scratch),
         compiler_params=pltpu.CompilerParams(vmem_limit_bytes=vmem),
         cost_estimate=pl.CostEstimate(flops=flops, bytes_accessed=size, transcendentals=0),
@@ -416,28 +453,36 @@
         name="scores",
     )
     arrived = swap(sent)
+    dma = lambda k: pltpu.SemaphoreType.DMA((k,))
+    spread = sds((2 * n + 16, L), F32)
+    labv = pltpu.VMEM((n, L), F32)
+    halfv = pltpu.VMEM((n, 2 * L), BF16)
     nh, nl, fh, fl, labk, cnt = call(
         tiles_kernel,
         (half, half, sds((n, halo), BF16), sds((n, halo), BF16), sds((n, L), F32), sds((8, L), F32)),
         [VM, SM, VM, VM],
         (tiles, tile_cols, square(labels), square(train_mask)),
+        [halfv, halfv, labv, dma(3)],
         vmem=28 * MIB,
         flops=10**7,
         size=8 * 10**6,
         name="tiles",
+        specs=(HB, HB, VM, VM, HB, VM),
     )
     lines = peers * (bnd + up(bnd, per))
     packed = sds((lines, L), F32)
     stageb = pltpu.VMEM((2 * halo, L), F32)
-    base, e, vh, vl, out = call(
-        functools.partial(errors_kernel, classes=classes, per=per),
-        (state, state, half, half, packed),
-        [VM, SM, SM, VM],
+    base, v, out = call(
+        functools.partial(errors_kernel, classes=classes, per=per, n=n),
+        (spread, spread, packed),
+        [VM, SM, SM, HB],
         (arrived, recv_rows, bnd_rows, labk),
-        [stage, rows2, rows2, stageb],
+        [stage, rows2, rows2, stageb, labv, dma(3)],
         vmem=28 * MIB,
         name="errors",
+        specs=(HB, HB, VM),
     )
+    e = v
     hscr = [pltpu.VMEM((halo, L), F32)] * 2
     for step in range(2 * ITERS):
         rate = correct_rate if step < ITERS else smooth_rate
@@ -447,9 +492,10 @@
         got = call(
             functools.partial(near_kernel, rate=rate, classes=classes, sums=sums),
             (state, sds((8, L), F32)) if sums else (state,),
-            [VM, VM, VM, VM, VM, SM] + [VM] * sums,
-            (vh, vl, e, nh, nl, tile_cols) + ((cnt,) if sums else ()),
-            vmem=16 * MIB,
+            [HB, HB, HB, HB, SM] + [VM] * sums,
+            (v, e, nh, nl, tile_cols) + ((cnt,) if sums else ()),
+            [rows2, rows2, halfv, halfv, halfv, halfv, dma(4)],
+            vmem=24 * MIB,
             flops=10**9,
             size=8 * 10**6,
             name="near",
@@ -462,19 +508,19 @@
         )
         args, ins = (halos, fh, fl, part), [VM] * 4
         if mode == "last":
-            return call(far, sds((n, classes), F32), ins, args, hscr, vmem=24 * MIB, name="far_last")
+            return call(far, sds((classes, n), F32), ins, args, hscr, vmem=24 * MIB, name="far_last").T
         args, ins = args + (bnd_rows,), ins + [SM]
-        outs = (half, half, packed)
+        scratch = hscr + [rows2, stageb, pltpu.SemaphoreType.DMA]
         if mode == "sums":
             args, ins = args + (tot,), ins + [VM]
         if mode == "turn":
-            args, ins = args + (base, labk), ins + [VM, VM]
-            outs = (half, half, state, packed)
-        got = call(far, outs, ins, args, hscr + [rows2, stageb], vmem=24 * MIB, name="far_" + mode)
+            args, ins = args + (base, labk), ins + [HB, HB]
+            scratch = scratch + [dma(2), labv, rows2]
+        v, out = call(
+            far, (spread, packed), ins, args, scratch, vmem=24 * MIB, name="far_" + mode, specs=(HB, VM)
+        )
         if mode == "turn":
-            vh, vl, e, out = got
-        else:
-            vh, vl, out = got
+            e = v
 
 
 def solution(mesh):

time: 244 us -> 209 us (0.86)
  local copies, waits for them, and re-layouts: 67.2 us -> 9.58 us
  Pallas kernels: 104 us -> 126 us
  waiting for transfers between devices: 32.5 us -> 46.8 us
  starting transfers between devices: 37.9 us -> 25.6 us
    unnamed x113 -> x15, local copies, waits for them, and re-layouts: 64.5 us -> 8.33 us
    pallas_call x15, Pallas kernels: 104 us -> 126 us  [call(): pl.pallas_call(kernel, out_shape=outs, in_specs=ins, out_specs=specs or j...]
    all_to_all x7, waiting for transfers between devices: 32.5 us -> 46.8 us  [swap(): return lax.all_to_all(x, 'dom', split_axis=0, concat_axis=0, tiled=True)]
    all_to_all x7, starting transfers between devices: 37.9 us -> 25.6 us  [swap(): return lax.all_to_all(x, 'dom', split_axis=0, concat_axis=0, tiled=True)]
  transfers between devices with their start and end apart: 7 -> 7, of which waited for: 7 -> 7; matrix products, arithmetic and copies ran while one was open for 0% -> 0% of each run, Pallas kernels for 9% -> 18%
where the time goes in v2:
time: 209 us; the launch traced here: 208 us
  Pallas kernels  126 us (60%)
  waiting for transfers between devices  46.8 us (22%)
  starting transfers between devices  25.6 us (12%)
  local copies, waits for them, and re-layouts  9.58 us (5%)
    pallas_call x15, Pallas kernels, call(): pl.pallas_call(kernel, out_shape=outs, in_specs=ins, out_specs=specs or j...  126 us
    all_to_all x7, waiting for transfers between devices, swap(): return lax.all_to_all(x, 'dom', split_axis=0, concat_axis=0, tiled=True)  46.8 us
    all_to_all x7, starting transfers between devices, swap(): return lax.all_to_all(x, 'dom', split_axis=0, concat_axis=0, tiled=True)  25.6 us
    unnamed x15, local copies, waits for them, and re-layouts  8.33 us
  transfers between devices with their start and end apart: 7, of which 7 were waited for; matrix products, arithmetic and copies ran while one was open for 0% of the time, Pallas kernels for 18%

profile of v2, /device:TPU:0, one launch (start us, length us, event | category | flops | bytes accessed | tf_op | source)
XLA Modules:
  0.0 207.8 jit_solution(6890722952929283701)
XLA Ops:
  0.0 1.3 pad_bitcast_fusion.bias
  1.3 2.0 copy.25.self_w
  3.2 4.4 %copy.24.bases = bf16[1024,1224]{1,0:T(8,128)(2,1)} copy(bf16[1024,1224]{0,1:T(8,128)(2,1)} %param.16) | data formatting | bytes 5013504 | tf_op args[1]
  7.6 51.8 %scores.1 = f32[32,88,128]{2,1,0:T(8,128)} custom-call(bf16[1536,1024]{1,0:T(8,128)(2,1)} %hid.1, bf16[1024,1224]{1,0:T(8,128)(2,1)} %copy.24.bases, bf16[1024,153]{1,0:T(8,128)(2,1)} %copy.25.self_w, f32[2,128]{1,0:T(2,128)} %pad_bitcast_fusion.bias, f32[5,8]{1,0:T(8,128)} %coef.1, s32[48,128]{1,0:T(8,128)} %bitcast.28, s32[48,128]{1,0:T(8,128)} %bitcast.29, ...), custom_call_target="tpu_custom_call" | custom-call | tf_op jit(solution)/shard_map/scores/pallas_call | solution.py:396
  59.4 0.0 copy-start.5
  59.4 0.0 copy-start.1
  59.4 0.0 copy-start.3
  59.4 0.0 copy-start.4
  59.4 7.3 %all-to-all-start = ((f32[32,88,128]{2,1,0:T(8,128)}), f32[32,88,128]{2,1,0:T(8,128)S(1)}, u32[]{:S(2)}, u32[]{:S(2)}) async-start(f32[32,88,128]{2,1,0:T(8,128)} %scores.1), calls=%async_computation | async-start | bytes 2883584 | tf_op jit(solution)/shard_map/all_to_all | solution.py:409
  66.7 0.0 copy-done.5
  66.7 0.1 copy.26.bnd.refs_4_
  66.8 0.0 copy-done.1
  66.8 0.0 copy-done.3
  66.8 0.0 copy-done.4
  66.8 0.0 copy-start
  66.8 1.9 copy-done
  68.7 0.0 copy-start.2
  68.7 3.6 %tiles.2 = (bf16[1536,256]{1,0:T(8,128)(2,1)}, bf16[1536,256]{1,0:T(8,128)(2,1)}, bf16[1536,256]{1,0:T(8,128)(2,1)S(1)}, bf16[1536,256]{1,0:T(8,128)(2,1)S(1)}, ...) custom-call(f32[48,128,128]{2,1,0:T(8,128)S(1)} %copy-done, s32[48]{0:T(128)S(1)} %copy-done.1, s32[12,128]{1,0:T(8,128)S(1)} %bitcast.26, ...), custom_call_target="tpu_custom_call" | custom-call | flops 10000000 | bytes 8000000 | tf_op jit(solution)/shard_map/tiles/pallas_call | solution.py:396
  72.3 29.2 %all-to-all-done.arr = f32[32,88,128]{2,1,0:T(8,128)S(1)} async-done(((f32[32,88,128]{2,1,0:T(8,128)}), f32[32,88,128]{2,1,0:T(8,128)S(1)}, u32[]{:S(2)}, u32[]{:S(2)}) %all-to-all-start) | async-done | bytes 1441824 | tf_op jit(solution)/shard_map/all_to_all | solution.py:409
  101.6 0.0 copy-done.2
  101.6 8.4 %errors.1 = (f32[3088,128]{1,0:T(8,128)}, f32[3088,128]{1,0:T(8,128)}, f32[320,128]{1,0:T(8,128)}) custom-call(f32[32,88,128]{2,1,0:T(8,128)S(1)} %all-to-all-done.arr, s32[1,32,72]{2,1,0:T(8,128)S(1)} %copy-done.2, s32[1,32,8]{2,1,0:T(8,128)S(1)} %copy.26.bnd.refs_4_, f32[1536,128]{1,0:T(8,128)} %get-tuple-element.26.labk_hbm.refs_6_), custom_call_target="tpu_custom_call" | custom-call | tf_op jit(solution)/shard_map/errors/pallas_call | solution.py:396
  110.0 3.6 %all-to-all-start.1 = ((f32[32,1,1280]{2,1,0:T(1,128)}), f32[32,1,1280]{2,1,0:T(1,128)S(1)}, u32[]{:S(2)}, u32[]{:S(2)}) async-start(f32[32,1,1280]{2,1,0:T(1,128)} %bitcast.6), calls=%async_computation.1 | async-start | bytes 327680 | tf_op jit(solution)/shard_map/all_to_all | solution.py:409
  113.6 5.8 %near.6 = (f32[1536,256]{1,0:T(8,128)S(1)}, f32[8,128]{1,0:T(8,128)S(1)}) custom-call(f32[3088,128]{1,0:T(8,128)} %get-tuple-element.30.v_hbm.e_hbm, f32[3088,128]{1,0:T(8,128)} %get-tuple-element.30.v_hbm.e_hbm, bf16[1536,256]{1,0:T(8,128)(2,1)} %get-tuple-element.31.nh_hbm, bf16[1536,256]{1,0:T(8,128)(2,1)} %get-tuple-element.32.nl_hbm, s32[48]{0:T(128)S(1)} %copy-done.1, ...), custom_call_target="tpu_custom_call" | custom-call | flops 1000000000 | bytes 8000000 | tf_op jit(solution)/shard_map/near/pallas_call | solution.py:396
  119.5 2.8 %all-to-all-done.1 = f32[32,1,1280]{2,1,0:T(1,128)S(1)} async-done(((f32[32,1,1280]{2,1,0:T(1,128)}), f32[32,1,1280]{2,1,0:T(1,128)S(1)}, u32[]{:S(2)}, u32[]{:S(2)}) %all-to-all-start.1) | async-done | bytes 163872 | tf_op jit(solution)/shard_map/all_to_all | solution.py:409
  122.3 4.4 %far_step.3 = (f32[3088,128]{1,0:T(8,128)}, f32[320,128]{1,0:T(8,128)}) custom-call(f32[320,128]{1,0:T(8,128)S(1)} %bitcast.22, bf16[1536,256]{1,0:T(8,128)(2,1)S(1)} %get-tuple-element.28.refs_1_, bf16[1536,256]{1,0:T(8,128)(2,1)S(1)} %get-tuple-element.29.refs_2_, f32[1536,256]{1,0:T(8,128)S(1)} %get-tuple-element.34.refs_3_, s32[1,32,8]{2,1,0:T(8,128)S(1)} %copy.26.bnd.refs_4_), custom_call_target="tpu_custom_call" | custom-call | tf_op jit(solution)/shard_map/far_step/pallas_call | solution.py:396
  126.7 3.1 %all-to-all-start.2 = ((f32[32,1,1280]{2,1,0:T(1,128)}), f32[32,1,1280]{2,1,0:T(1,128)S(1)}, u32[]{:S(2)}, u32[]{:S(2)}) async-start(f32[32,1,1280]{2,1,0:T(1,128)} %bitcast.8), calls=%async_computation.2 | async-start | bytes 327680 | tf_op jit(solution)/shard_map/all_to_all | solution.py:409
  129.7 5.7 %near.7.refs_3_ = f32[1536,256]{1,0:T(8,128)S(1)} custom-call(f32[3088,128]{1,0:T(8,128)} %get-tuple-element.36.v_hbm, f32[3088,128]{1,0:T(8,128)} %get-tuple-element.30.v_hbm.e_hbm, bf16[1536,256]{1,0:T(8,128)(2,1)} %get-tuple-element.31.nh_hbm, bf16[1536,256]{1,0:T(8,128)(2,1)} %get-tuple-element.32.nl_hbm, s32[48]{0:T(128)S(1)} %copy-done.1), custom_call_target="tpu_custom_call" | custom-call | flops 1000000000 | bytes 8000000 | tf_op jit(solution)/shard_map/near/pallas_call | solution.py:396
  135.4 2.9 %all-to-all-done.2 = f32[32,1,1280]{2,1,0:T(1,128)S(1)} async-done(((f32[32,1,1280]{2,1,0:T(1,128)}), f32[32,1,1280]{2,1,0:T(1,128)S(1)}, u32[]{:S(2)}, u32[]{:S(2)}) %all-to-all-start.2) | async-done | bytes 163872 | tf_op jit(solution)/shard_map/all_to_all | solution.py:409
  138.4 4.4 %far_sums.1 = (f32[3088,128]{1,0:T(8,128)}, f32[320,128]{1,0:T(8,128)}) custom-call(f32[320,128]{1,0:T(8,128)S(1)} %bitcast.23, bf16[1536,256]{1,0:T(8,128)(2,1)S(1)} %get-tuple-element.28.refs_1_, bf16[1536,256]{1,0:T(8,128)(2,1)S(1)} %get-tuple-element.29.refs_2_, f32[1536,256]{1,0:T(8,128)S(1)} %near.7.refs_3_, s32[1,32,8]{2,1,0:T(8,128)S(1)} %copy.26.bnd.refs_4_, ...), custom_call_target="tpu_custom_call" | custom-call | tf_op jit(solution)/shard_map/far_sums/pallas_call | solution.py:396
  142.8 2.9 %all-to-all-start.3 = ((f32[32,1,1280]{2,1,0:T(1,128)}), f32[32,1,1280]{2,1,0:T(1,128)S(1)}, u32[]{:S(2)}, u32[]{:S(2)}) async-start(f32[32,1,1280]{2,1,0:T(1,128)} %bitcast.10), calls=%async_computation.3 | async-start | bytes 327680 | tf_op jit(solution)/shard_map/all_to_all | solution.py:409
  145.7 5.7 %near.8.refs_3_ = f32[1536,256]{1,0:T(8,128)S(1)} custom-call(f32[3088,128]{1,0:T(8,128)} %get-tuple-element.39.v_hbm, f32[3088,128]{1,0:T(8,128)} %get-tuple-element.30.v_hbm.e_hbm, bf16[1536,256]{1,0:T(8,128)(2,1)} %get-tuple-element.31.nh_hbm, bf16[1536,256]{1,0:T(8,128)(2,1)} %get-tuple-element.32.nl_hbm, s32[48]{0:T(128)S(1)} %copy-done.1), custom_call_target="tpu_custom_call" | custom-call | flops 1000000000 | bytes 8000000 | tf_op jit(solution)/shard_map/near/pallas_call | solution.py:396
  151.4 2.9 %all-to-all-done.3 = f32[32,1,1280]{2,1,0:T(1,128)S(1)} async-done(((f32[32,1,1280]{2,1,0:T(1,128)}), f32[32,1,1280]{2,1,0:T(1,128)S(1)}, u32[]{:S(2)}, u32[]{:S(2)}) %all-to-all-start.3) | async-done | bytes 163872 | tf_op jit(solution)/shard_map/all_to_all | solution.py:409
  154.3 7.0 %far_turn.1 = (f32[3088,128]{1,0:T(8,128)}, f32[320,128]{1,0:T(8,128)}) custom-call(f32[320,128]{1,0:T(8,128)S(1)} %bitcast.20, bf16[1536,256]{1,0:T(8,128)(2,1)S(1)} %get-tuple-element.28.refs_1_, bf16[1536,256]{1,0:T(8,128)(2,1)S(1)} %get-tuple-element.29.refs_2_, f32[1536,256]{1,0:T(8,128)S(1)} %near.8.refs_3_, s32[1,32,8]{2,1,0:T(8,128)S(1)} %copy.26.bnd.refs_4_, ...), custom_call_target="tpu_custom_call" | custom-call | tf_op jit(solution)/shard_map/far_turn/pallas_call | solution.py:396
  161.3 2.9 %all-to-all-start.4 = ((f32[32,1,1280]{2,1,0:T(1,128)}), f32[32,1,1280]{2,1,0:T(1,128)S(1)}, u32[]{:S(2)}, u32[]{:S(2)}) async-start(f32[32,1,1280]{2,1,0:T(1,128)} %bitcast.12), calls=%async_computation.4 | async-start | bytes 327680 | tf_op jit(solution)/shard_map/all_to_all | solution.py:409
  164.2 5.7 %near.9.refs_3_ = f32[1536,256]{1,0:T(8,128)S(1)} custom-call(f32[3088,128]{1,0:T(8,128)} %get-tuple-element.42.v_hbm.e_hbm, f32[3088,128]{1,0:T(8,128)} %get-tuple-element.42.v_hbm.e_hbm, bf16[1536,256]{1,0:T(8,128)(2,1)} %get-tuple-element.31.nh_hbm, bf16[1536,256]{1,0:T(8,128)(2,1)} %get-tuple-element.32.nl_hbm, s32[48]{0:T(128)S(1)} %copy-done.1), custom_call_target="tpu_custom_call" | custom-call | flops 1000000000 | bytes 8000000 | tf_op jit(solution)/shard_map/near/pallas_call | solution.py:396
  169.9 2.9 %all-to-all-done.4 = f32[32,1,1280]{2,1,0:T(1,128)S(1)} async-done(((f32[32,1,1280]{2,1,0:T(1,128)}), f32[32,1,1280]{2,1,0:T(1,128)S(1)}, u32[]{:S(2)}, u32[]{:S(2)}) %all-to-all-start.4) | async-done | bytes 163872 | tf_op jit(solution)/shard_map/all_to_all | solution.py:409
  172.9 4.4 %far_step.4 = (f32[3088,128]{1,0:T(8,128)}, f32[320,128]{1,0:T(8,128)}) custom-call(f32[320,128]{1,0:T(8,128)S(1)} %bitcast.25, bf16[1536,256]{1,0:T(8,128)(2,1)S(1)} %get-tuple-element.28.refs_1_, bf16[1536,256]{1,0:T(8,128)(2,1)S(1)} %get-tuple-element.29.refs_2_, f32[1536,256]{1,0:T(8,128)S(1)} %near.9.refs_3_, s32[1,32,8]{2,1,0:T(8,128)S(1)} %copy.26.bnd.refs_4_), custom_call_target="tpu_custom_call" | custom-call | tf_op jit(solution)/shard_map/far_step/pallas_call | solution.py:396
  177.2 2.9 %all-to-all-start.5 = ((f32[32,1,1280]{2,1,0:T(1,128)}), f32[32,1,1280]{2,1,0:T(1,128)S(1)}, u32[]{:S(2)}, u32[]{:S(2)}) async-start(f32[32,1,1280]{2,1,0:T(1,128)} %bitcast.14), calls=%async_computation.5 | async-start | bytes 327680 | tf_op jit(solution)/shard_map/all_to_all | solution.py:409
  180.1 5.7 %near.10.refs_3_ = f32[1536,256]{1,0:T(8,128)S(1)} custom-call(f32[3088,128]{1,0:T(8,128)} %get-tuple-element.44.v_hbm, f32[3088,128]{1,0:T(8,128)} %get-tuple-element.42.v_hbm.e_hbm, bf16[1536,256]{1,0:T(8,128)(2,1)} %get-tuple-element.31.nh_hbm, bf16[1536,256]{1,0:T(8,128)(2,1)} %get-tuple-element.32.nl_hbm, s32[48]{0:T(128)S(1)} %copy-done.1), custom_call_target="tpu_custom_call" | custom-call | flops 1000000000 | bytes 8000000 | tf_op jit(solution)/shard_map/near/pallas_call | solution.py:396
  185.8 3.0 %all-to-all-done.5 = f32[32,1,1280]{2,1,0:T(1,128)S(1)} async-done(((f32[32,1,1280]{2,1,0:T(1,128)}), f32[32,1,1280]{2,1,0:T(1,128)S(1)}, u32[]{:S(2)}, u32[]{:S(2)}) %all-to-all-start.5) | async-done | bytes 163872 | tf_op jit(solution)/shard_map/all_to_all | solution.py:409
  188.8 4.4 %far_step.5 = (f32[3088,128]{1,0:T(8,128)}, f32[320,128]{1,0:T(8,128)}) custom-call(f32[320,128]{1,0:T(8,128)S(1)} %bitcast.24, bf16[1536,256]{1,0:T(8,128)(2,1)S(1)} %get-tuple-element.28.refs_1_, bf16[1536,256]{1,0:T(8,128)(2,1)S(1)} %get-tuple-element.29.refs_2_, f32[1536,256]{1,0:T(8,128)S(1)} %near.10.refs_3_, s32[1,32,8]{2,1,0:T(8,128)S(1)} %copy.26.bnd.refs_4_), custom_call_target="tpu_custom_call" | custom-call | tf_op jit(solution)/shard_map/far_step/pallas_call | solution.py:396
  193.2 2.9 %all-to-all-start.6 = ((f32[32,1,1280]{2,1,0:T(1,128)}), f32[32,1,1280]{2,1,0:T(1,128)S(1)}, u32[]{:S(2)}, u32[]{:S(2)}) async-start(f32[32,1,1280]{2,1,0:T(1,128)} %bitcast.16), calls=%async_computation.6 | async-start | bytes 327680 | tf_op jit(solution)/shard_map/all_to_all | solution.py:409
  196.1 5.7 %near.11.refs_3_ = f32[1536,256]{1,0:T(8,128)S(1)} custom-call(f32[3088,128]{1,0:T(8,128)} %get-tuple-element.46.v_hbm, f32[3088,128]{1,0:T(8,128)} %get-tuple-element.42.v_hbm.e_hbm, bf16[1536,256]{1,0:T(8,128)(2,1)} %get-tuple-element.31.nh_hbm, bf16[1536,256]{1,0:T(8,128)(2,1)} %get-tuple-element.32.nl_hbm, s32[48]{0:T(128)S(1)} %copy-done.1), custom_call_target="tpu_custom_call" | custom-call | flops 1000000000 | bytes 8000000 | tf_op jit(solution)/shard_map/near/pallas_call | solution.py:396
  201.7 3.0 %all-to-all-done.6 = f32[32,1,1280]{2,1,0:T(1,128)S(1)} async-done(((f32[32,1,1280]{2,1,0:T(1,128)}), f32[32,1,1280]{2,1,0:T(1,128)S(1)}, u32[]{:S(2)}, u32[]{:S(2)}) %all-to-all-start.6) | async-done | bytes 163872 | tf_op jit(solution)/shard_map/all_to_all | solution.py:409
  204.7 3.1 %far_last.1 = f32[153,1536]{1,0:T(8,128)} custom-call(f32[320,128]{1,0:T(8,128)S(1)} %bitcast.21, bf16[1536,256]{1,0:T(8,128)(2,1)S(1)} %get-tuple-element.28.refs_1_, bf16[1536,256]{1,0:T(8,128)(2,1)S(1)} %get-tuple-element.29.refs_2_, f32[1536,256]{1,0:T(8,128)S(1)} %near.11.refs_3_), custom_call_target="tpu_custom_call" | custom-call | tf_op jit(solution)/shard_map/far_last/pallas_call | solution.py:396
Async XLA Ops:
  59.4 7.4 %copy-start.5 = (s32[1,32,8]{1,2,0:T(8,128)S(1)}, s32[1,32,8]{1,2,0:T(8,128)}, u32[]{:S(2)}) copy-start(s32[1,32,8]{1,2,0:T(8,128)} %param.27) | copy-start | bytes 3076
  59.4 7.5 %copy-start.1 = (s32[48]{0:T(128)S(1)}, s32[48]{0:T(128)}, u32[]{:S(2)}) copy-start(s32[48]{0:T(128)} %cols.13) | copy-start | bytes 580
  59.4 7.4 %copy-start.3 = (s32[1536]{0:T(1024)S(1)}, s32[1536]{0:T(1024)}, u32[]{:S(2)}) copy-start(s32[1536]{0:T(1024)} %param.25) | copy-start | bytes 18436
  59.4 7.4 %copy-start.4 = (s32[1536]{0:T(1024)S(1)}, s32[1536]{0:T(1024)}, u32[]{:S(2)}) copy-start(s32[1536]{0:T(1024)} %param.26) | copy-start | bytes 18436
  59.4 42.2 %all-to-all-start = ((f32[32,88,128]{2,1,0:T(8,128)}), f32[32,88,128]{2,1,0:T(8,128)S(1)}, u32[]{:S(2)}, u32[]{:S(2)}) async-start(f32[32,88,128]{2,1,0:T(8,128)} %scores.1), calls=%async_computation | async-start | bytes 2883584 | tf_op jit(solution)/shard_map/all_to_all | solution.py:409
  66.8 1.9 copy-start
  68.7 32.9 %copy-start.2 = (s32[1,32,72]{2,1,0:T(8,128)S(1)}, s32[1,32,72]{2,1,0:T(8,128)}, u32[]{:S(2)}) copy-start(s32[1,32,72]{2,1,0:T(8,128)} %recv.1) | copy-start | bytes 27652
  110.0 12.3 %all-to-all-start.1 = ((f32[32,1,1280]{2,1,0:T(1,128)}), f32[32,1,1280]{2,1,0:T(1,128)S(1)}, u32[]{:S(2)}, u32[]{:S(2)}) async-start(f32[32,1,1280]{2,1,0:T(1,128)} %bitcast.6), calls=%async_computation.1 | async-start | bytes 327680 | tf_op jit(solution)/shard_map/all_to_all | solution.py:409
  126.7 11.7 %all-to-all-start.2 = ((f32[32,1,1280]{2,1,0:T(1,128)}), f32[32,1,1280]{2,1,0:T(1,128)S(1)}, u32[]{:S(2)}, u32[]{:S(2)}) async-start(f32[32,1,1280]{2,1,0:T(1,128)} %bitcast.8), calls=%async_computation.2 | async-start | bytes 327680 | tf_op jit(solution)/shard_map/all_to_all | solution.py:409
  142.8 11.6 %all-to-all-start.3 = ((f32[32,1,1280]{2,1,0:T(1,128)}), f32[32,1,1280]{2,1,0:T(1,128)S(1)}, u32[]{:S(2)}, u32[]{:S(2)}) async-start(f32[32,1,1280]{2,1,0:T(1,128)} %bitcast.10), calls=%async_computation.3 | async-start | bytes 327680 | tf_op jit(solution)/shard_map/all_to_all | solution.py:409
  161.3 11.5 %all-to-all-start.4 = ((f32[32,1,1280]{2,1,0:T(1,128)}), f32[32,1,1280]{2,1,0:T(1,128)S(1)}, u32[]{:S(2)}, u32[]{:S(2)}) async-start(f32[32,1,1280]{2,1,0:T(1,128)} %bitcast.12), calls=%async_computation.4 | async-start | bytes 327680 | tf_op jit(solution)/shard_map/all_to_all | solution.py:409
  177.2 11.5 %all-to-all-start.5 = ((f32[32,1,1280]{2,1,0:T(1,128)}), f32[32,1,1280]{2,1,0:T(1,128)S(1)}, u32[]{:S(2)}, u32[]{:S(2)}) async-start(f32[32,1,1280]{2,1,0:T(1,128)} %bitcast.14), calls=%async_computation.5 | async-start | bytes 327680 | tf_op jit(solution)/shard_map/all_to_all | solution.py:409
  193.2 11.5 %all-to-all-start.6 = ((f32[32,1,1280]{2,1,0:T(1,128)}), f32[32,1,1280]{2,1,0:T(1,128)S(1)}, u32[]{:S(2)}, u32[]{:S(2)}) async-start(f32[32,1,1280]{2,1,0:T(1,128)} %bitcast.16), calls=%async_computation.6 | async-start | bytes 327680 | tf_op jit(solution)/shard_map/all_to_all | solution.py:409

commit v3 on v2

--- a/solution.py
+++ b/solution.py
@@ -46,85 +46,140 @@
 
 
 def gather_rows(idx_ref, src, stg, peers, slots):
-    def body(p, _):
+    for p in range(peers):
         for k in range(slots):
-            row = idx_ref[0, p, k]
-            pair(stg, p * slots + k)[...] = pair(src, row)[...]
-        return 0
-
-    lax.fori_loop(0, peers, body, 0)
+            at = pl.ds(pl.multiple_of(idx_ref[0, p, k], 2), 2)
+            stg[pl.ds(2 * (p * slots + k), 2), :] = src[at, :]
+
+
+def fetch(src, rows, refs, sems):
+    copies = [pltpu.make_async_copy(src.at[pl.ds(i, 1), :], r, sems.at[i]) for i, r in zip(rows, refs)]
+    for c in copies:
+        c.start()
+    return copies
 
 
 def scores_kernel(
-    hid, bases, self_w, bias, coef, es, ed, er, send, out,
-    whi, wlo, m2, s0, s1, sc2, stg, kv, ks, sem, *, classes, slots, per, blk,
+    hid, bt, st, bias, coef, es, ed, er, send, out,
+    pt, p0, p1, m2, s0, s1, s2, s3, sc2, stg, kj, kd, kp, sj, sd, sp, *ks, classes, slots, per,
 ):
     n, hdim = hid.shape
     rest = classes - L
     nrel, nb = coef.shape
     peers = out.shape[0]
     erows = es.shape[0]
-    kv[0] = (er[...] * n + es[...]) * 2
-    kv[1] = (er[...] * n + ed[...]) * 2
-    copy = pltpu.make_async_copy(kv, ks, sem)
-    copy.start()
-
-    step = 32
-
-    def mix(i, _):
-        rows = pl.ds(pl.multiple_of(i * step, step), step)
-        parts = [bases[rows, b * classes : (b + 1) * classes].astype(F32) for b in range(nb)]
-        for r in range(nrel):
-            w = coef[r, 0] * parts[0]
-            for b in range(1, nb):
-                w = w + coef[r, b] * parts[b]
-            hi, lo = split(w)
-            whi[rows, r * 2 * L : r * 2 * L + classes] = hi
-            wlo[rows, r * 2 * L : r * 2 * L + classes] = lo
-        whi[rows, nrel * 2 * L : nrel * 2 * L + classes] = self_w[rows, :]
-        return 0
-
-    lax.fori_loop(0, hdim // step, mix, 0)
-
-    s0[...] = jnp.zeros_like(s0)
-    s1[...] = jnp.zeros_like(s1)
+    acc = (s0, s1, s2, s3)
+    ksj, ksd, ksp = ks[:erows], ks[erows : 2 * erows], ks[2 * erows :]
+    kj[...] = (er[...] * n + es[...]) * 2
+    kd[...] = (er[...] * n + ed[...]) * 2
+    kp[:, 0:slots] = send[0] * 2
+    copies = fetch(kj, range(erows), ksj, sj) + fetch(kd, range(erows), ksd, sd) + fetch(kp, range(peers), ksp, sp)
+
+    base_r = nb * L
+    base_s = base_r + 2 * L
+    gap = 2 * L // nb
+    step = 2 * L
+
+    def arrange(i, _):
+        cols = pl.ds(pl.multiple_of(i * step, step), step)
+        for b in range(nb):
+            x = bt[b * classes : (b + 1) * classes, cols].astype(F32)
+            pt[b * L : (b + 1) * L, cols] = x[:L].astype(BF16)
+            tail = jnp.concatenate([x[L:], jnp.zeros((gap - rest, step), F32)], 0)
+            pt[base_r + b * gap : base_r + (b + 1) * gap, cols] = tail.astype(BF16)
+        x = st[:, cols].astype(F32)
+        pt[base_s : base_s + L, cols] = x[:L].astype(BF16)
+        tail = jnp.concatenate([x[L:], jnp.zeros((L - rest, step), F32)], 0)
+        pt[base_s + L : base_s + 2 * L, cols] = tail.astype(BF16)
+        return 0
+
+    lax.fori_loop(0, hdim // step, arrange, 0)
+
+    chunk = 256
+    sub = 32
+    zrows = 2 * nrel * chunk
+    lane = lanes(sub)
+    one = jnp.where(lane == rest, 1.0, 0.0)
+    lane8 = lanes(8)
+    gains = []
+    for r in range(nrel):
+        for h in range(2):
+            g = jnp.zeros((8, L), F32)
+            for b in range(nb // 2):
+                g = jnp.where(lane8 // gap == b, coef[r, h * (nb // 2) + b], g)
+            gains.append(g[0:1])
+    bias0 = bias[0:1, 0:L]
+    bias1 = jnp.concatenate([bias[0:1, L:classes], jnp.zeros((1, L - rest), F32)], 1)
+
+    def project(i, dst):
+        h = hid[pl.ds(pl.multiple_of(i * chunk, chunk), chunk), :]
+        for j in range(0, base_s + 2 * L, 2 * L):
+            dst[:, j : j + 2 * L] = lax.dot_general(
+                h, pt[j : j + 2 * L, :], (((1,), (1,)), ((), ())), preferred_element_type=F32
+            )
+            yield
+
+    def mix(i, src):
+        row0 = i * chunk
+        for u in range(0, chunk, sub):
+            for z in acc:
+                piece = zrows * sub // chunk
+                at = pl.multiple_of(i * zrows + u * piece // sub, piece)
+                z[pl.ds(at, piece), :] = jnp.zeros((piece, L), F32)
+            rows = slice(u, u + sub)
+            mains = [src[rows, b * L : (b + 1) * L] for b in range(nb)]
+            q = [src[rows, base_r + h * L : base_r + (h + 1) * L] for h in range(2)]
+            for r in range(nrel):
+                x = coef[r, 0] * mains[0]
+                for b in range(1, nb):
+                    x = x + coef[r, b] * mains[b]
+                t = gains[2 * r] * q[0] + gains[2 * r + 1] * q[1]
+                turn = L // 2
+                while turn >= gap:
+                    t = t + pltpu.roll(t, turn, axis=1)
+                    turn //= 2
+                at = 2 * (r * n + row0 + u)
+                m2[pl.ds(at, sub, stride=2), :] = x
+                m2[pl.ds(at + 1, sub, stride=2), :] = jnp.where(lane < rest, t, one)
+            at = 2 * (row0 + u)
+            sc2[pl.ds(at, sub, stride=2), :] = src[rows, base_s : base_s + L] + bias0
+            sc2[pl.ds(at + 1, sub, stride=2), :] = src[rows, base_s + L : base_s + 2 * L] + bias1
+            yield
+
+    def weave(*works):
+        works = list(works)
+        while works:
+            for w in list(works):
+                if next(w, 0) == 0:
+                    works.remove(w)
+
     sc2[pl.ds(2 * n, 16), :] = jnp.zeros((16, L), F32)
-
-    chunk = 256
-    lane = lanes(chunk)
-
-    def project(i, _):
-        row = pl.multiple_of(i * chunk, chunk)
-        h = hid[pl.ds(row, chunk), :]
-        for r in range(nrel):
-            cols = pl.ds(r * 2 * L, 2 * L)
-            a = dot(h, whi[:, cols]) + dot(h, wlo[:, cols])
-            at = 2 * (r * n + row)
-            m2[pl.ds(at, chunk, stride=2), :] = a[:, :L]
-            tail = jnp.where(lane < rest, a[:, L:], jnp.where(lane == rest, 1.0, 0.0))
-            m2[pl.ds(at + 1, chunk, stride=2), :] = tail
-        a = dot(h, whi[:, pl.ds(nrel * 2 * L, 2 * L)])
-        sc2[pl.ds(2 * row, chunk, stride=2), :] = a[:, :L] + bias[0:1, :]
-        tail = jnp.where(lane < rest, a[:, L:] + bias[1:2, :], 0.0)
-        sc2[pl.ds(2 * row + 1, chunk, stride=2), :] = tail
-        return 0
-
-    lax.fori_loop(0, n // chunk, project, 0)
-    copy.wait()
-
-    half = erows // 2
+    count = n // chunk
+    weave(project(0, p0))
+
+    def pipe(t, _):
+        weave(project(2 * t + 1, p1), mix(2 * t, p0))
+        weave(project(2 * t + 2, p0), mix(2 * t + 1, p1))
+        return 0
+
+    lax.fori_loop(0, count // 2 - 1, pipe, 0)
+    weave(project(count - 1, p1), mix(count - 2, p0))
+    weave(mix(count - 1, p1))
+    for c in copies:
+        c.wait()
 
     def edges(t, _):
-        for l in range(L):
-            for c, s in enumerate((s0, s1)):
-                j = ks[0, t + c * half, l]
-                d = ks[1, t + c * half, l]
+        for v in range(2):
+            for e in range(erows):
+                s = acc[e % 4]
+                j = ksj[e][0, 2 * t + v]
+                d = ksd[e][0, 2 * t + v]
                 src = m2[pl.ds(pl.multiple_of(j, 2), 2), :]
                 at = pl.ds(pl.multiple_of(d, 2), 2)
                 s[at, :] = s[at, :] + src
         return 0
 
-    lax.fori_loop(0, half, edges, 0)
+    lax.fori_loop(0, L // 2, edges, 0)
 
     fin = 64
     flane = lanes(fin)
@@ -134,9 +189,8 @@
         a0 = sc2[pl.ds(2 * row, fin, stride=2), :]
         a1 = sc2[pl.ds(2 * row + 1, fin, stride=2), :]
         for r in range(nrel):
-            at = 2 * (r * n + row)
-            m = s0[pl.ds(at, fin, stride=2), :] + s1[pl.ds(at, fin, stride=2), :]
-            t = s0[pl.ds(at + 1, fin, stride=2), :] + s1[pl.ds(at + 1, fin, stride=2), :]
+            rows = [pl.ds(2 * (r * n + row) + h, fin, stride=2) for h in range(2)]
+            m, t = [(s0[w, :] + s1[w, :]) + (s2[w, :] + s3[w, :]) for w in rows]
             inv = 1.0 / jnp.maximum(t[:, rest : rest + 1], 1.0)
             a0 = a0 + m * inv
             a1 = a1 + t * inv
@@ -146,7 +200,13 @@
 
     lax.fori_loop(0, n // fin, finish, 0)
 
-    gather_rows(send, sc2, stg, peers, slots)
+    def collect(k, _):
+        for p in range(peers):
+            at = pl.ds(pl.multiple_of(ksp[p][0, k], 2), 2)
+            pair(stg, p * slots + k)[...] = sc2[at, :]
+        return 0
+
+    lax.fori_loop(0, slots, collect, 0)
     ntail = up(slots, per)
 
     def put(p, _):
@@ -427,33 +487,32 @@
     half = sds((n, 2 * L), BF16)
     blocks = n // L
 
+    dma = lambda k: pltpu.SemaphoreType.DMA((k,))
     blk = up(slots + up(slots, per), 8) * 8
-    bias2 = jnp.pad(bias, (0, 2 * L - classes)).reshape(2, L)
     square = lambda x: x.reshape(-1, L)
     stage = pltpu.VMEM((2 * (peers * slots + 16), L), F32)
     rows2 = pltpu.VMEM((2 * n + 16, L), F32)
+    sums = pltpu.VMEM((2 * nrel * n, L), F32)
+    wide = (nb + 4) * L
+    erows = ne // L
+    bnd_rows = 2 * bnd_rows
     sent = call(
-        functools.partial(scores_kernel, classes=classes, slots=slots, per=per, blk=blk),
+        functools.partial(scores_kernel, classes=classes, slots=slots, per=per),
         sds((peers, blk, L), F32),
-        [VM, VM, VM, VM, SM, VM, VM, VM, SM],
-        (hidden, bases, self_weight, bias2, coef, square(edge_src), square(edge_dst), square(edge_rel), send_rows),
-        [
-            pltpu.VMEM((hdim, (nrel + 1) * 2 * L), BF16),
-            pltpu.VMEM((hdim, nrel * 2 * L), BF16),
-            pltpu.VMEM((2 * nrel * n, L), F32),
-            pltpu.VMEM((2 * nrel * n, L), F32),
-            pltpu.VMEM((2 * nrel * n, L), F32),
-            rows2,
-            stage,
-            pltpu.VMEM((2, ne // L, L), jnp.int32),
-            pltpu.SMEM((2, ne // L, L), jnp.int32),
-            pltpu.SemaphoreType.DMA,
-        ],
-        vmem=56 * MIB,
+        [VM, VM, VM, VM, SM, VM, VM, VM, VM],
+        (hidden, bases.T, self_weight.T, bias.reshape(1, -1), coef)
+        + (square(edge_src), square(edge_dst), square(edge_rel), send_rows),
+        [pltpu.VMEM((wide, hdim), BF16)]
+        + [pltpu.VMEM((256, wide), F32)] * 2
+        + [sums] * 5
+        + [rows2, stage]
+        + [pltpu.VMEM((erows, L), jnp.int32)] * 2
+        + [pltpu.VMEM((peers, L), jnp.int32), dma(erows), dma(erows), dma(peers)]
+        + [pltpu.SMEM((1, L), jnp.int32)] * (2 * erows + peers),
+        vmem=60 * MIB,
         name="scores",
     )
     arrived = swap(sent)
-    dma = lambda k: pltpu.SemaphoreType.DMA((k,))
     spread = sds((2 * n + 16, L), F32)
     labv = pltpu.VMEM((n, L), F32)
     halfv = pltpu.VMEM((n, 2 * L), BF16)

time: 209 us -> 185 us (0.89)
  Pallas kernels: 126 us -> 110 us
  local copies, waits for them, and re-layouts: 9.58 us -> 1.99 us
    pallas_call x15, Pallas kernels: 126 us -> 110 us  [call(): pl.pallas_call(kernel, out_shape=outs, in_specs=ins, out_specs=specs or j...]
    unnamed x15 -> x13, local copies, waits for them, and re-layouts: 8.33 us -> 1.99 us
  transfers between devices with their start and end apart: 7 -> 7, of which waited for: 7 -> 7; matrix products, arithmetic and copies ran while one was open for 0% -> 0% of each run, Pallas kernels for 18% -> 20%
where the time goes in v3:
time: 185 us
  Pallas kernels  110 us (59%)
  waiting for transfers between devices  46.7 us (25%)
  starting transfers between devices  25.7 us (14%)
  local copies, waits for them, and re-layouts  1.99 us (1%)
    pallas_call x15, Pallas kernels, call(): pl.pallas_call(kernel, out_shape=outs, in_specs=ins, out_specs=specs or j...  110 us
    all_to_all x7, waiting for transfers between devices, swap(): return lax.all_to_all(x, 'dom', split_axis=0, concat_axis=0, tiled=True)  46.7 us
    all_to_all x7, starting transfers between devices, swap(): return lax.all_to_all(x, 'dom', split_axis=0, concat_axis=0, tiled=True)  25.7 us
  transfers between devices with their start and end apart: 7, of which 7 were waited for; matrix products, arithmetic and copies ran while one was open for 0% of the time, Pallas kernels for 20%

profile of v3, /device:TPU:0, one launch (start us, length us, event | category | flops | bytes accessed | tf_op | source)
XLA Modules:
  0.0 184.7 jit_solution(956000320963427199)
XLA Ops:
  0.0 34.7 %scores.1 = f32[32,88,128]{2,1,0:T(8,128)} custom-call(bf16[1536,1024]{1,0:T(8,128)(2,1)} %hid.1, bf16[1224,1024]{1,0:T(8,128)(2,1)} %bitcast.29, bf16[153,1024]{1,0:T(8,128)(2,1)} %bitcast.30, f32[1,153]{1,0:T(1,128)} %bitcast.34, f32[5,8]{1,0:T(8,128)} %coef.1, s32[48,128]{1,0:T(8,128)} %bitcast.31, s32[48,128]{1,0:T(8,128)} %bitcast.32, ...), custom_call_target="tpu_custom_call" | custom-call | tf_op jit(solution)/shard_map/scores/pallas_call | solution.py:456
  34.7 0.0 copy-start.5
  34.8 0.0 copy-start.1
  34.8 0.0 copy-start.3
  34.8 0.0 copy-start.4
  34.8 7.4 %all-to-all-start = ((f32[32,88,128]{2,1,0:T(8,128)}), f32[32,88,128]{2,1,0:T(8,128)S(1)}, u32[]{:S(2)}, u32[]{:S(2)}) async-start(f32[32,88,128]{2,1,0:T(8,128)} %scores.1), calls=%async_computation | async-start | bytes 2883584 | tf_op jit(solution)/shard_map/all_to_all | solution.py:469
  42.2 0.0 copy-done.5
  42.2 0.1 copy.17
  42.2 0.0 copy-done.1
  42.2 0.0 copy-done.3
  42.2 0.0 copy-done.4
  42.3 0.0 copy-start
  42.3 1.9 %copy-done = f32[48,128,128]{2,1,0:T(8,128)S(1)} copy-done((f32[48,128,128]{2,1,0:T(8,128)S(1)}, f32[48,128,128]{2,1,0:T(8,128)}, u32[]{:S(2)}) %copy-start) | copy-done | bytes 3145752
  44.1 0.0 copy-start.2
  44.1 3.6 %tiles.2 = (bf16[1536,256]{1,0:T(8,128)(2,1)}, bf16[1536,256]{1,0:T(8,128)(2,1)}, bf16[1536,256]{1,0:T(8,128)(2,1)S(1)}, bf16[1536,256]{1,0:T(8,128)(2,1)S(1)}, ...) custom-call(f32[48,128,128]{2,1,0:T(8,128)S(1)} %copy-done, s32[48]{0:T(128)S(1)} %copy-done.1, s32[12,128]{1,0:T(8,128)S(1)} %bitcast.27, ...), custom_call_target="tpu_custom_call" | custom-call | flops 10000000 | bytes 8000000 | tf_op jit(solution)/shard_map/tiles/pallas_call | solution.py:456
  47.8 29.2 %all-to-all-done.arr = f32[32,88,128]{2,1,0:T(8,128)S(1)} async-done(((f32[32,88,128]{2,1,0:T(8,128)}), f32[32,88,128]{2,1,0:T(8,128)S(1)}, u32[]{:S(2)}, u32[]{:S(2)}) %all-to-all-start) | async-done | bytes 1441824 | tf_op jit(solution)/shard_map/all_to_all | solution.py:469
  77.0 0.0 copy-done.2
  77.0 8.5 %errors.1 = (f32[3088,128]{1,0:T(8,128)}, f32[3088,128]{1,0:T(8,128)}, f32[320,128]{1,0:T(8,128)}) custom-call(f32[32,88,128]{2,1,0:T(8,128)S(1)} %all-to-all-done.arr, s32[1,32,72]{2,1,0:T(8,128)S(1)} %copy-done.2, s32[1,32,8]{2,1,0:T(8,128)S(1)} %broadcast_multiply_fusion.bnd.refs_4_, f32[1536,128]{1,0:T(8,128)} %get-tuple-element.26.labk_hbm.refs_6_), custom_call_target="tpu_custom_call" | custom-call | tf_op jit(solution)/shard_map/errors/pallas_call | solution.py:456
  85.5 3.6 %all-to-all-start.1 = ((f32[32,1,1280]{2,1,0:T(1,128)}), f32[32,1,1280]{2,1,0:T(1,128)S(1)}, u32[]{:S(2)}, u32[]{:S(2)}) async-start(f32[32,1,1280]{2,1,0:T(1,128)} %bitcast.8), calls=%async_computation.1 | async-start | bytes 327680 | tf_op jit(solution)/shard_map/all_to_all | solution.py:469
  89.1 5.8 %near.6 = (f32[1536,256]{1,0:T(8,128)S(1)}, f32[8,128]{1,0:T(8,128)S(1)}) custom-call(f32[3088,128]{1,0:T(8,128)} %get-tuple-element.30.v_hbm.e_hbm, f32[3088,128]{1,0:T(8,128)} %get-tuple-element.30.v_hbm.e_hbm, bf16[1536,256]{1,0:T(8,128)(2,1)} %get-tuple-element.31.nh_hbm, bf16[1536,256]{1,0:T(8,128)(2,1)} %get-tuple-element.32.nl_hbm, s32[48]{0:T(128)S(1)} %copy-done.1, ...), custom_call_target="tpu_custom_call" | custom-call | flops 1000000000 | bytes 8000000 | tf_op jit(solution)/shard_map/near/pallas_call | solution.py:456
  95.0 2.8 %all-to-all-done.1 = f32[32,1,1280]{2,1,0:T(1,128)S(1)} async-done(((f32[32,1,1280]{2,1,0:T(1,128)}), f32[32,1,1280]{2,1,0:T(1,128)S(1)}, u32[]{:S(2)}, u32[]{:S(2)}) %all-to-all-start.1) | async-done | bytes 163872 | tf_op jit(solution)/shard_map/all_to_all | solution.py:469
  97.8 4.7 %far_step.3 = (f32[3088,128]{1,0:T(8,128)}, f32[320,128]{1,0:T(8,128)}) custom-call(f32[320,128]{1,0:T(8,128)S(1)} %bitcast.23, bf16[1536,256]{1,0:T(8,128)(2,1)S(1)} %get-tuple-element.28.refs_1_, bf16[1536,256]{1,0:T(8,128)(2,1)S(1)} %get-tuple-element.29.refs_2_, f32[1536,256]{1,0:T(8,128)S(1)} %get-tuple-element.34.refs_3_, ...), custom_call_target="tpu_custom_call" | custom-call | tf_op jit(solution)/shard_map/far_step/pallas_call | solution.py:456
  102.4 3.1 %all-to-all-start.2 = ((f32[32,1,1280]{2,1,0:T(1,128)}), f32[32,1,1280]{2,1,0:T(1,128)S(1)}, u32[]{:S(2)}, u32[]{:S(2)}) async-start(f32[32,1,1280]{2,1,0:T(1,128)} %bitcast.10), calls=%async_computation.2 | async-start | bytes 327680 | tf_op jit(solution)/shard_map/all_to_all | solution.py:469
  105.5 5.7 %near.7.refs_3_ = f32[1536,256]{1,0:T(8,128)S(1)} custom-call(f32[3088,128]{1,0:T(8,128)} %get-tuple-element.36.v_hbm, f32[3088,128]{1,0:T(8,128)} %get-tuple-element.30.v_hbm.e_hbm, bf16[1536,256]{1,0:T(8,128)(2,1)} %get-tuple-element.31.nh_hbm, bf16[1536,256]{1,0:T(8,128)(2,1)} %get-tuple-element.32.nl_hbm, s32[48]{0:T(128)S(1)} %copy-done.1), custom_call_target="tpu_custom_call" | custom-call | flops 1000000000 | bytes 8000000 | tf_op jit(solution)/shard_map/near/pallas_call | solution.py:456
  111.2 2.9 %all-to-all-done.2 = f32[32,1,1280]{2,1,0:T(1,128)S(1)} async-done(((f32[32,1,1280]{2,1,0:T(1,128)}), f32[32,1,1280]{2,1,0:T(1,128)S(1)}, u32[]{:S(2)}, u32[]{:S(2)}) %all-to-all-start.2) | async-done | bytes 163872 | tf_op jit(solution)/shard_map/all_to_all | solution.py:469
  114.1 4.7 %far_sums.1 = (f32[3088,128]{1,0:T(8,128)}, f32[320,128]{1,0:T(8,128)}) custom-call(f32[320,128]{1,0:T(8,128)S(1)} %bitcast.24, bf16[1536,256]{1,0:T(8,128)(2,1)S(1)} %get-tuple-element.28.refs_1_, bf16[1536,256]{1,0:T(8,128)(2,1)S(1)} %get-tuple-element.29.refs_2_, f32[1536,256]{1,0:T(8,128)S(1)} %near.7.refs_3_, ...), custom_call_target="tpu_custom_call" | custom-call | tf_op jit(solution)/shard_map/far_sums/pallas_call | solution.py:456
  118.8 2.9 %all-to-all-start.3 = ((f32[32,1,1280]{2,1,0:T(1,128)}), f32[32,1,1280]{2,1,0:T(1,128)S(1)}, u32[]{:S(2)}, u32[]{:S(2)}) async-start(f32[32,1,1280]{2,1,0:T(1,128)} %bitcast.12), calls=%async_computation.3 | async-start | bytes 327680 | tf_op jit(solution)/shard_map/all_to_all | solution.py:469
  121.7 5.7 %near.8.refs_3_ = f32[1536,256]{1,0:T(8,128)S(1)} custom-call(f32[3088,128]{1,0:T(8,128)} %get-tuple-element.39.v_hbm, f32[3088,128]{1,0:T(8,128)} %get-tuple-element.30.v_hbm.e_hbm, bf16[1536,256]{1,0:T(8,128)(2,1)} %get-tuple-element.31.nh_hbm, bf16[1536,256]{1,0:T(8,128)(2,1)} %get-tuple-element.32.nl_hbm, s32[48]{0:T(128)S(1)} %copy-done.1), custom_call_target="tpu_custom_call" | custom-call | flops 1000000000 | bytes 8000000 | tf_op jit(solution)/shard_map/near/pallas_call | solution.py:456
  127.4 2.9 %all-to-all-done.3 = f32[32,1,1280]{2,1,0:T(1,128)S(1)} async-done(((f32[32,1,1280]{2,1,0:T(1,128)}), f32[32,1,1280]{2,1,0:T(1,128)S(1)}, u32[]{:S(2)}, u32[]{:S(2)}) %all-to-all-start.3) | async-done | bytes 163872 | tf_op jit(solution)/shard_map/all_to_all | solution.py:469
  130.3 7.3 %far_turn.1 = (f32[3088,128]{1,0:T(8,128)}, f32[320,128]{1,0:T(8,128)}) custom-call(f32[320,128]{1,0:T(8,128)S(1)} %bitcast.21, bf16[1536,256]{1,0:T(8,128)(2,1)S(1)} %get-tuple-element.28.refs_1_, bf16[1536,256]{1,0:T(8,128)(2,1)S(1)} %get-tuple-element.29.refs_2_, f32[1536,256]{1,0:T(8,128)S(1)} %near.8.refs_3_, ...), custom_call_target="tpu_custom_call" | custom-call | tf_op jit(solution)/shard_map/far_turn/pallas_call | solution.py:456
  137.6 2.9 %all-to-all-start.4 = ((f32[32,1,1280]{2,1,0:T(1,128)}), f32[32,1,1280]{2,1,0:T(1,128)S(1)}, u32[]{:S(2)}, u32[]{:S(2)}) async-start(f32[32,1,1280]{2,1,0:T(1,128)} %bitcast.14), calls=%async_computation.4 | async-start | bytes 327680 | tf_op jit(solution)/shard_map/all_to_all | solution.py:469
  140.5 5.7 %near.9.refs_3_ = f32[1536,256]{1,0:T(8,128)S(1)} custom-call(f32[3088,128]{1,0:T(8,128)} %get-tuple-element.42.v_hbm.e_hbm, f32[3088,128]{1,0:T(8,128)} %get-tuple-element.42.v_hbm.e_hbm, bf16[1536,256]{1,0:T(8,128)(2,1)} %get-tuple-element.31.nh_hbm, bf16[1536,256]{1,0:T(8,128)(2,1)} %get-tuple-element.32.nl_hbm, s32[48]{0:T(128)S(1)} %copy-done.1), custom_call_target="tpu_custom_call" | custom-call | flops 1000000000 | bytes 8000000 | tf_op jit(solution)/shard_map/near/pallas_call | solution.py:456
  146.2 2.9 %all-to-all-done.4 = f32[32,1,1280]{2,1,0:T(1,128)S(1)} async-done(((f32[32,1,1280]{2,1,0:T(1,128)}), f32[32,1,1280]{2,1,0:T(1,128)S(1)}, u32[]{:S(2)}, u32[]{:S(2)}) %all-to-all-start.4) | async-done | bytes 163872 | tf_op jit(solution)/shard_map/all_to_all | solution.py:469
  149.1 4.6 %far_step.4 = (f32[3088,128]{1,0:T(8,128)}, f32[320,128]{1,0:T(8,128)}) custom-call(f32[320,128]{1,0:T(8,128)S(1)} %bitcast.26, bf16[1536,256]{1,0:T(8,128)(2,1)S(1)} %get-tuple-element.28.refs_1_, bf16[1536,256]{1,0:T(8,128)(2,1)S(1)} %get-tuple-element.29.refs_2_, f32[1536,256]{1,0:T(8,128)S(1)} %near.9.refs_3_, ...), custom_call_target="tpu_custom_call" | custom-call | tf_op jit(solution)/shard_map/far_step/pallas_call | solution.py:456
  153.8 2.9 %all-to-all-start.5 = ((f32[32,1,1280]{2,1,0:T(1,128)}), f32[32,1,1280]{2,1,0:T(1,128)S(1)}, u32[]{:S(2)}, u32[]{:S(2)}) async-start(f32[32,1,1280]{2,1,0:T(1,128)} %bitcast.16), calls=%async_computation.5 | async-start | bytes 327680 | tf_op jit(solution)/shard_map/all_to_all | solution.py:469
  156.7 5.7 %near.10.refs_3_ = f32[1536,256]{1,0:T(8,128)S(1)} custom-call(f32[3088,128]{1,0:T(8,128)} %get-tuple-element.44.v_hbm, f32[3088,128]{1,0:T(8,128)} %get-tuple-element.42.v_hbm.e_hbm, bf16[1536,256]{1,0:T(8,128)(2,1)} %get-tuple-element.31.nh_hbm, bf16[1536,256]{1,0:T(8,128)(2,1)} %get-tuple-element.32.nl_hbm, s32[48]{0:T(128)S(1)} %copy-done.1), custom_call_target="tpu_custom_call" | custom-call | flops 1000000000 | bytes 8000000 | tf_op jit(solution)/shard_map/near/pallas_call | solution.py:456
  162.4 2.9 %all-to-all-done.5 = f32[32,1,1280]{2,1,0:T(1,128)S(1)} async-done(((f32[32,1,1280]{2,1,0:T(1,128)}), f32[32,1,1280]{2,1,0:T(1,128)S(1)}, u32[]{:S(2)}, u32[]{:S(2)}) %all-to-all-start.5) | async-done | bytes 163872 | tf_op jit(solution)/shard_map/all_to_all | solution.py:469
  165.3 4.6 %far_step.5 = (f32[3088,128]{1,0:T(8,128)}, f32[320,128]{1,0:T(8,128)}) custom-call(f32[320,128]{1,0:T(8,128)S(1)} %bitcast.25, bf16[1536,256]{1,0:T(8,128)(2,1)S(1)} %get-tuple-element.28.refs_1_, bf16[1536,256]{1,0:T(8,128)(2,1)S(1)} %get-tuple-element.29.refs_2_, f32[1536,256]{1,0:T(8,128)S(1)} %near.10.refs_3_, ...), custom_call_target="tpu_custom_call" | custom-call | tf_op jit(solution)/shard_map/far_step/pallas_call | solution.py:456
  170.0 2.9 %all-to-all-start.6 = ((f32[32,1,1280]{2,1,0:T(1,128)}), f32[32,1,1280]{2,1,0:T(1,128)S(1)}, u32[]{:S(2)}, u32[]{:S(2)}) async-start(f32[32,1,1280]{2,1,0:T(1,128)} %bitcast.18), calls=%async_computation.6 | async-start | bytes 327680 | tf_op jit(solution)/shard_map/all_to_all | solution.py:469
  172.9 5.7 %near.11.refs_3_ = f32[1536,256]{1,0:T(8,128)S(1)} custom-call(f32[3088,128]{1,0:T(8,128)} %get-tuple-element.46.v_hbm, f32[3088,128]{1,0:T(8,128)} %get-tuple-element.42.v_hbm.e_hbm, bf16[1536,256]{1,0:T(8,128)(2,1)} %get-tuple-element.31.nh_hbm, bf16[1536,256]{1,0:T(8,128)(2,1)} %get-tuple-element.32.nl_hbm, s32[48]{0:T(128)S(1)} %copy-done.1), custom_call_target="tpu_custom_call" | custom-call | flops 1000000000 | bytes 8000000 | tf_op jit(solution)/shard_map/near/pallas_call | solution.py:456
  178.6 2.9 %all-to-all-done.6 = f32[32,1,1280]{2,1,0:T(1,128)S(1)} async-done(((f32[32,1,1280]{2,1,0:T(1,128)}), f32[32,1,1280]{2,1,0:T(1,128)S(1)}, u32[]{:S(2)}, u32[]{:S(2)}) %all-to-all-start.6) | async-done | bytes 163872 | tf_op jit(solution)/shard_map/all_to_all | solution.py:469
  181.5 3.1 %far_last.1 = f32[153,1536]{1,0:T(8,128)} custom-call(f32[320,128]{1,0:T(8,128)S(1)} %bitcast.22, bf16[1536,256]{1,0:T(8,128)(2,1)S(1)} %get-tuple-element.28.refs_1_, bf16[1536,256]{1,0:T(8,128)(2,1)S(1)} %get-tuple-element.29.refs_2_, f32[1536,256]{1,0:T(8,128)S(1)} %near.11.refs_3_), custom_call_target="tpu_custom_call" | custom-call | tf_op jit(solution)/shard_map/far_last/pallas_call | solution.py:456
  (1 shorter events, 0.0 us)
Async XLA Ops:
  34.7 7.4 %copy-start.5 = (s32[1,32,8]{1,2,0:T(8,128)S(1)}, s32[1,32,8]{1,2,0:T(8,128)}, u32[]{:S(2)}) copy-start(s32[1,32,8]{1,2,0:T(8,128)} %param.27) | copy-start | bytes 3076
  34.8 7.5 %copy-start.1 = (s32[48]{0:T(128)S(1)}, s32[48]{0:T(128)}, u32[]{:S(2)}) copy-start(s32[48]{0:T(128)} %cols.13) | copy-start | bytes 580
  34.8 7.5 %copy-start.3 = (s32[1536]{0:T(1024)S(1)}, s32[1536]{0:T(1024)}, u32[]{:S(2)}) copy-start(s32[1536]{0:T(1024)} %param.25) | copy-start | bytes 18436
  34.8 7.5 %copy-start.4 = (s32[1536]{0:T(1024)S(1)}, s32[1536]{0:T(1024)}, u32[]{:S(2)}) copy-start(s32[1536]{0:T(1024)} %param.26) | copy-start | bytes 18436
  34.8 42.2 %all-to-all-start = ((f32[32,88,128]{2,1,0:T(8,128)}), f32[32,88,128]{2,1,0:T(8,128)S(1)}, u32[]{:S(2)}, u32[]{:S(2)}) async-start(f32[32,88,128]{2,1,0:T(8,128)} %scores.1), calls=%async_computation | async-start | bytes 2883584 | tf_op jit(solution)/shard_map/all_to_all | solution.py:469
  42.3 1.9 %copy-start = (f32[48,128,128]{2,1,0:T(8,128)S(1)}, f32[48,128,128]{2,1,0:T(8,128)}, u32[]{:S(2)}) copy-start(f32[48,128,128]{2,1,0:T(8,128)} %tiles.3) | copy-start | bytes 9437188
  44.1 32.9 %copy-start.2 = (s32[1,32,72]{2,1,0:T(8,128)S(1)}, s32[1,32,72]{2,1,0:T(8,128)}, u32[]{:S(2)}) copy-start(s32[1,32,72]{2,1,0:T(8,128)} %recv.1) | copy-start | bytes 27652
  85.5 12.3 %all-to-all-start.1 = ((f32[32,1,1280]{2,1,0:T(1,128)}), f32[32,1,1280]{2,1,0:T(1,128)S(1)}, u32[]{:S(2)}, u32[]{:S(2)}) async-start(f32[32,1,1280]{2,1,0:T(1,128)} %bitcast.8), calls=%async_computation.1 | async-start | bytes 327680 | tf_op jit(solution)/shard_map/all_to_all | solution.py:469
  102.4 11.7 %all-to-all-start.2 = ((f32[32,1,1280]{2,1,0:T(1,128)}), f32[32,1,1280]{2,1,0:T(1,128)S(1)}, u32[]{:S(2)}, u32[]{:S(2)}) async-start(f32[32,1,1280]{2,1,0:T(1,128)} %bitcast.10), calls=%async_computation.2 | async-start | bytes 327680 | tf_op jit(solution)/shard_map/all_to_all | solution.py:469
  118.8 11.5 %all-to-all-start.3 = ((f32[32,1,1280]{2,1,0:T(1,128)}), f32[32,1,1280]{2,1,0:T(1,128)S(1)}, u32[]{:S(2)}, u32[]{:S(2)}) async-start(f32[32,1,1280]{2,1,0:T(1,128)} %bitcast.12), calls=%async_computation.3 | async-start | bytes 327680 | tf_op jit(solution)/shard_map/all_to_all | solution.py:469
  137.6 11.5 %all-to-all-start.4 = ((f32[32,1,1280]{2,1,0:T(1,128)}), f32[32,1,1280]{2,1,0:T(1,128)S(1)}, u32[]{:S(2)}, u32[]{:S(2)}) async-start(f32[32,1,1280]{2,1,0:T(1,128)} %bitcast.14), calls=%async_computation.4 | async-start | bytes 327680 | tf_op jit(solution)/shard_map/all_to_all | solution.py:469
  153.8 11.5 %all-to-all-start.5 = ((f32[32,1,1280]{2,1,0:T(1,128)}), f32[32,1,1280]{2,1,0:T(1,128)S(1)}, u32[]{:S(2)}, u32[]{:S(2)}) async-start(f32[32,1,1280]{2,1,0:T(1,128)} %bitcast.16), calls=%async_computation.5 | async-start | bytes 327680 | tf_op jit(solution)/shard_map/all_to_all | solution.py:469
  170.0 11.6 %all-to-all-start.6 = ((f32[32,1,1280]{2,1,0:T(1,128)}), f32[32,1,1280]{2,1,0:T(1,128)S(1)}, u32[]{:S(2)}, u32[]{:S(2)}) async-start(f32[32,1,1280]{2,1,0:T(1,128)} %bitcast.18), calls=%async_computation.6 | async-start | bytes 327680 | tf_op jit(solution)/shard_map/all_to_all | solution.py:469

commit v4 on v3

--- a/solution.py
+++ b/solution.py
@@ -46,10 +46,16 @@
 
 
 def gather_rows(idx_ref, src, stg, peers, slots):
-    for p in range(peers):
-        for k in range(slots):
-            at = pl.ds(pl.multiple_of(idx_ref[0, p, k], 2), 2)
-            stg[pl.ds(2 * (p * slots + k), 2), :] = src[at, :]
+    group = 4
+
+    def body(g, _):
+        for p in range(group):
+            for k in range(slots):
+                at = pl.ds(pl.multiple_of(idx_ref[0, g * group + p, k], 2), 2)
+                pair(stg, g * (group * slots) + (p * slots + k))[...] = src[at, :]
+        return 0
+
+    lax.fori_loop(0, peers // group, body, 0)
 
 
 def fetch(src, rows, refs, sems):
@@ -60,8 +66,8 @@
 
 
 def scores_kernel(
-    hid, bt, st, bias, coef, es, ed, er, send, out,
-    pt, p0, p1, m2, s0, s1, s2, s3, sc2, stg, kj, kd, kp, sj, sd, sp, *ks, classes, slots, per,
+    hid, bt, st, bias, coef, es, ed, er, send, out, blank,
+    pt, p0, m2, s0, s1, s2, s3, sc2, stg, kj, kd, kp, zero, sj, sd, sp, sz, *ks, classes, slots, per,
 ):
     n, hdim = hid.shape
     rest = classes - L
@@ -74,6 +80,9 @@
     kd[...] = (er[...] * n + ed[...]) * 2
     kp[:, 0:slots] = send[0] * 2
     copies = fetch(kj, range(erows), ksj, sj) + fetch(kd, range(erows), ksd, sd) + fetch(kp, range(peers), ksp, sp)
+    zero[...] = jnp.zeros_like(zero)
+    wipe = pltpu.make_async_copy(zero, blank, sz.at[0])
+    wipe.start()
 
     base_r = nb * L
     base_s = base_r + 2 * L
@@ -94,10 +103,15 @@
         return 0
 
     lax.fori_loop(0, hdim // step, arrange, 0)
-
-    chunk = 256
+    wipe.wait()
+    zrows = blank.shape[0]
+    for c, s in enumerate(acc):
+        for i in range(nrel):
+            copies.append(pltpu.make_async_copy(blank, s.at[pl.ds(i * zrows, zrows), :], sz.at[1 + c * nrel + i]))
+            copies[-1].start()
+
+    chunk = p0.shape[0]
     sub = 32
-    zrows = 2 * nrel * chunk
     lane = lanes(sub)
     one = jnp.where(lane == rest, 1.0, 0.0)
     lane8 = lanes(8)
@@ -111,24 +125,19 @@
     bias0 = bias[0:1, 0:L]
     bias1 = jnp.concatenate([bias[0:1, L:classes], jnp.zeros((1, L - rest), F32)], 1)
 
-    def project(i, dst):
-        h = hid[pl.ds(pl.multiple_of(i * chunk, chunk), chunk), :]
+    def project(i, _):
+        row0 = pl.multiple_of(i * chunk, chunk)
+        h = hid[pl.ds(row0, chunk), :]
         for j in range(0, base_s + 2 * L, 2 * L):
-            dst[:, j : j + 2 * L] = lax.dot_general(
+            p0[:, j : j + 2 * L] = lax.dot_general(
                 h, pt[j : j + 2 * L, :], (((1,), (1,)), ((), ())), preferred_element_type=F32
             )
-            yield
-
-    def mix(i, src):
-        row0 = i * chunk
-        for u in range(0, chunk, sub):
-            for z in acc:
-                piece = zrows * sub // chunk
-                at = pl.multiple_of(i * zrows + u * piece // sub, piece)
-                z[pl.ds(at, piece), :] = jnp.zeros((piece, L), F32)
-            rows = slice(u, u + sub)
-            mains = [src[rows, b * L : (b + 1) * L] for b in range(nb)]
-            q = [src[rows, base_r + h * L : base_r + (h + 1) * L] for h in range(2)]
+
+        def mix(u, _):
+            rows = pl.ds(pl.multiple_of(u * sub, sub), sub)
+            row = row0 + u * sub
+            mains = [p0[rows, b * L : (b + 1) * L] for b in range(nb)]
+            q = [p0[rows, base_r + h * L : base_r + (h + 1) * L] for h in range(2)]
             for r in range(nrel):
                 x = coef[r, 0] * mains[0]
                 for b in range(1, nb):
@@ -138,33 +147,19 @@
                 while turn >= gap:
                     t = t + pltpu.roll(t, turn, axis=1)
                     turn //= 2
-                at = 2 * (r * n + row0 + u)
+                at = 2 * (r * n + row)
                 m2[pl.ds(at, sub, stride=2), :] = x
                 m2[pl.ds(at + 1, sub, stride=2), :] = jnp.where(lane < rest, t, one)
-            at = 2 * (row0 + u)
-            sc2[pl.ds(at, sub, stride=2), :] = src[rows, base_s : base_s + L] + bias0
-            sc2[pl.ds(at + 1, sub, stride=2), :] = src[rows, base_s + L : base_s + 2 * L] + bias1
-            yield
-
-    def weave(*works):
-        works = list(works)
-        while works:
-            for w in list(works):
-                if next(w, 0) == 0:
-                    works.remove(w)
+            at = 2 * row
+            sc2[pl.ds(at, sub, stride=2), :] = p0[rows, base_s : base_s + L] + bias0
+            sc2[pl.ds(at + 1, sub, stride=2), :] = p0[rows, base_s + L : base_s + 2 * L] + bias1
+            return 0
+
+        lax.fori_loop(0, chunk // sub, mix, 0)
+        return 0
 
     sc2[pl.ds(2 * n, 16), :] = jnp.zeros((16, L), F32)
-    count = n // chunk
-    weave(project(0, p0))
-
-    def pipe(t, _):
-        weave(project(2 * t + 1, p1), mix(2 * t, p0))
-        weave(project(2 * t + 2, p0), mix(2 * t + 1, p1))
-        return 0
-
-    lax.fori_loop(0, count // 2 - 1, pipe, 0)
-    weave(project(count - 1, p1), mix(count - 2, p0))
-    weave(mix(count - 1, p1))
+    lax.fori_loop(0, n // chunk, project, 0)
     for c in copies:
         c.wait()
 
@@ -181,7 +176,7 @@
 
     lax.fori_loop(0, L // 2, edges, 0)
 
-    fin = 64
+    fin = 128
     flane = lanes(fin)
 
     def finish(i, _):
@@ -240,7 +235,8 @@
 
 
 def errors_kernel(
-    arr, recv, bnd, labk_hbm, base_hbm, e_hbm, out, stg, base2, v2, stgb, labk, sems, *, classes, per, n
+    arr, recv, bnd, labk_hbm, base_hbm, e_hbm, out, stg, base2, v2, stgb, labk, kr, sems, sr, esem, *ksr,
+    classes, per, n,
 ):
     rest = classes - L
     peers, blk, _ = arr.shape
@@ -249,6 +245,8 @@
     tlane = lanes(ntail)
     load = pltpu.make_async_copy(labk_hbm, labk, sems.at[0])
     load.start()
+    kr[:, 0:slots] = recv[0] * 2
+    copies = fetch(kr, range(peers), ksr, sr)
 
     def unpack(p, _):
         at = p * 2 * slots
@@ -262,14 +260,20 @@
 
     lax.fori_loop(0, peers, unpack, 0)
 
-    def spread(p, _):
-        for k in range(slots):
-            row = recv[0, p, k]
-            pair(base2, row)[...] = pair(stg, p * slots + k)[...]
-        return 0
-
-    lax.fori_loop(0, peers, spread, 0)
-    keep = pltpu.make_async_copy(base2, base_hbm, sems.at[1])
+    for c in copies:
+        c.wait()
+    unroll = 2
+
+    def spread(t, _):
+        for v in range(unroll):
+            k = t * unroll + v
+            for p in range(peers):
+                at = pl.ds(pl.multiple_of(ksr[p][0, k], 2), 2)
+                base2[at, :] = pair(stg, p * slots + k)[...]
+        return 0
+
+    lax.fori_loop(0, slots // unroll, spread, 0)
+    keep = pltpu.make_async_copy(base2.at[pl.ds(0, 2 * n), :], base_hbm, sems.at[1])
     keep.start()
     load.wait()
 
@@ -284,15 +288,19 @@
             rows = pl.ds(2 * row + h, chunk, stride=2)
             onehot = jnp.where(lab == (lane + h * L).astype(F32), 1.0, 0.0)
             v2[rows, :] = jnp.where(known, onehot - base2[rows, :], 0.0)
-        return 0
-
+        piece(i).start()
+        return 0
+
+    def piece(i):
+        rows = pl.ds(pl.multiple_of(2 * i * chunk, 2 * chunk), 2 * chunk)
+        return pltpu.make_async_copy(v2.at[rows, :], e_hbm.at[rows, :], esem.at[i])
+
+    v2[pl.ds(2 * n, 16), :] = jnp.zeros((16, L), F32)
     lax.fori_loop(0, n // chunk, error, 0)
-    v2[pl.ds(2 * n, 16), :] = jnp.zeros((16, L), F32)
-    save = pltpu.make_async_copy(v2, e_hbm, sems.at[2])
-    save.start()
     pack(bnd, v2, stgb, out, None, peers=peers, slots=bnd.shape[2], per=per, rest=rest)
     keep.wait()
-    save.wait()
+    for i in range(n // chunk):
+        piece(i).wait()
 
 
 def tiles_kernel(tiles, cols, labels, mask, nh_hbm, nl_hbm, fh, fl, lab_hbm, cnt, nh, nl, labk, sems):
@@ -412,8 +420,16 @@
         for c in loads:
             c.wait()
 
-    chunk = 256
+    chunk = n // 2
     lane = lanes(chunk)
+    count = n // chunk
+
+    def piece(i):
+        rows = pl.ds(pl.multiple_of(2 * i * chunk, 2 * chunk), 2 * chunk)
+        return pltpu.make_async_copy(v2.at[rows, :], v_hbm.at[rows, :], vsem.at[i])
+
+    if mode != "last":
+        v2[pl.ds(2 * n, 16), :] = jnp.zeros((16, L), F32)
 
     def body(i, _):
         row = pl.multiple_of(i * chunk, chunk)
@@ -437,16 +453,15 @@
                 onehot = jnp.where(lab == (lane + h * L).astype(F32), 1.0, 0.0)
                 x = jnp.where(lab >= 0.0, onehot, base2[rows2, :] + scale * x)
             v2[rows2, :] = x
-        return 0
-
-    lax.fori_loop(0, n // chunk, body, 0)
+        piece(i).start()
+        return 0
+
+    lax.fori_loop(0, count, body, 0)
     if mode != "last":
-        v2[pl.ds(2 * n, 16), :] = jnp.zeros((16, L), F32)
-        save = pltpu.make_async_copy(v2, v_hbm, vsem)
-        save.start()
         extra = tot[0:1, :] if mode == "sums" else None
         pack(bnd, v2, stgb, out, extra, peers=peers, slots=slots, per=per, rest=rest)
-        save.wait()
+        for i in range(count):
+            piece(i).wait()
 
 
 def call(kernel, outs, ins, args, scratch=(), vmem=0, flops=0, size=0, name=None, specs=None):
@@ -496,24 +511,27 @@
     wide = (nb + 4) * L
     erows = ne // L
     bnd_rows = 2 * bnd_rows
-    sent = call(
+    sent, _ = call(
         functools.partial(scores_kernel, classes=classes, slots=slots, per=per),
-        sds((peers, blk, L), F32),
+        (sds((peers, blk, L), F32), sds((2 * n, L), F32)),
         [VM, VM, VM, VM, SM, VM, VM, VM, VM],
         (hidden, bases.T, self_weight.T, bias.reshape(1, -1), coef)
         + (square(edge_src), square(edge_dst), square(edge_rel), send_rows),
         [pltpu.VMEM((wide, hdim), BF16)]
-        + [pltpu.VMEM((256, wide), F32)] * 2
+        + [pltpu.VMEM((n // 2, wide), F32)]
         + [sums] * 5
         + [rows2, stage]
         + [pltpu.VMEM((erows, L), jnp.int32)] * 2
-        + [pltpu.VMEM((peers, L), jnp.int32), dma(erows), dma(erows), dma(peers)]
+        + [pltpu.VMEM((peers, L), jnp.int32), pltpu.VMEM((2 * n, L), F32), dma(erows), dma(erows), dma(peers)]
+        + [dma(1 + 4 * nrel)]
         + [pltpu.SMEM((1, L), jnp.int32)] * (2 * erows + peers),
         vmem=60 * MIB,
         name="scores",
+        specs=(VM, HB),
     )
     arrived = swap(sent)
-    spread = sds((2 * n + 16, L), F32)
+    spread = sds((2 * n, L), F32)
+    flat2 = pltpu.VMEM((2 * n, L), F32)
     labv = pltpu.VMEM((n, L), F32)
     halfv = pltpu.VMEM((n, 2 * L), BF16)
     nh, nl, fh, fl, labk, cnt = call(
@@ -534,9 +552,10 @@
     base, v, out = call(
         functools.partial(errors_kernel, classes=classes, per=per, n=n),
         (spread, spread, packed),
-        [VM, SM, SM, HB],
+        [VM, VM, SM, HB],
         (arrived, recv_rows, bnd_rows, labk),
-        [stage, rows2, rows2, stageb, labv, dma(3)],
+        [stage, rows2, rows2, stageb, labv, pltpu.VMEM((peers, L), jnp.int32), dma(2), dma(peers), dma(n // L)]
+        + [pltpu.SMEM((1, L), jnp.int32)] * peers,
         vmem=28 * MIB,
         name="errors",
         specs=(HB, HB, VM),
@@ -553,7 +572,7 @@
             (state, sds((8, L), F32)) if sums else (state,),
             [HB, HB, HB, HB, SM] + [VM] * sums,
             (v, e, nh, nl, tile_cols) + ((cnt,) if sums else ()),
-            [rows2, rows2, halfv, halfv, halfv, halfv, dma(4)],
+            [flat2, flat2, halfv, halfv, halfv, halfv, dma(4)],
             vmem=24 * MIB,
             flops=10**9,
             size=8 * 10**6,
@@ -569,12 +588,12 @@
         if mode == "last":
             return call(far, sds((classes, n), F32), ins, args, hscr, vmem=24 * MIB, name="far_last").T
         args, ins = args + (bnd_rows,), ins + [SM]
-        scratch = hscr + [rows2, stageb, pltpu.SemaphoreType.DMA]
+        scratch = hscr + [rows2, stageb, dma(n // L)]
         if mode == "sums":
             args, ins = args + (tot,), ins + [VM]
         if mode == "turn":
             args, ins = args + (base, labk), ins + [HB, HB]
-            scratch = scratch + [dma(2), labv, rows2]
+            scratch = scratch + [dma(2), labv, flat2]
         v, out = call(
             far, (spread, packed), ins, args, scratch, vmem=24 * MIB, name="far_" + mode, specs=(HB, VM)
         )

time: 185 us -> 180 us (0.973)
  Pallas kernels: 110 us -> 105 us
    pallas_call x15, Pallas kernels: 110 us -> 105 us  [call(): pl.pallas_call(kernel, out_shape=outs, in_specs=ins, out_specs=specs or j...]
  transfers between devices with their start and end apart: 7 -> 7, of which waited for: 7 -> 7; matrix products, arithmetic and copies ran while one was open for 0% -> 0% of each run, Pallas kernels for 20% -> 21%
where the time goes in v4:
time: 180 us; the launch traced here: 179 us
  Pallas kernels  105 us (58%)
  waiting for transfers between devices  46.8 us (26%)
  starting transfers between devices  25.6 us (14%)
  local copies, waits for them, and re-layouts  1.99 us (1%)
    pallas_call x15, Pallas kernels, call(): pl.pallas_call(kernel, out_shape=outs, in_specs=ins, out_specs=specs or j...  105 us
    all_to_all x7, waiting for transfers between devices, swap(): return lax.all_to_all(x, 'dom', split_axis=0, concat_axis=0, tiled=True)  46.8 us
    all_to_all x7, starting transfers between devices, swap(): return lax.all_to_all(x, 'dom', split_axis=0, concat_axis=0, tiled=True)  25.6 us
  transfers between devices with their start and end apart: 7, of which 7 were waited for; matrix products, arithmetic and copies ran while one was open for 0% of the time, Pallas kernels for 21%

profile of v4, /device:TPU:0, one launch (start us, length us, event | category | flops | bytes accessed | tf_op | source)
XLA Modules:
  0.0 179.3 jit_solution(16347379564420955931)
XLA Ops:
  0.0 36.1 %scores.1 = (f32[32,88,128]{2,1,0:T(8,128)}, f32[3072,128]{1,0:T(8,128)}) custom-call(bf16[1536,1024]{1,0:T(8,128)(2,1)} %hid.1, bf16[1224,1024]{1,0:T(8,128)(2,1)} %bitcast.29, bf16[153,1024]{1,0:T(8,128)(2,1)} %bitcast.30, f32[1,153]{1,0:T(1,128)} %bitcast.34, f32[5,8]{1,0:T(8,128)} %coef.1, s32[48,128]{1,0:T(8,128)} %bitcast.31, s32[48,128]{1,0:T(8,128)} %bitcast.32, ...), custom_call_target="tpu_custom_call" | custom-call | tf_op jit(solution)/shard_map/scores/pallas_call | solution.py:471
  36.1 0.0 copy-start.5
  36.1 0.0 copy-start.1
  36.1 0.0 copy-start.3
  36.1 0.0 copy-start.4
  36.1 7.3 %all-to-all-start = ((f32[32,88,128]{2,1,0:T(8,128)}), f32[32,88,128]{2,1,0:T(8,128)S(1)}, u32[]{:S(2)}, u32[]{:S(2)}) async-start(f32[32,88,128]{2,1,0:T(8,128)} %get-tuple-element.27), calls=%async_computation | async-start | bytes 2883584 | tf_op jit(solution)/shard_map/all_to_all | solution.py:484
  43.5 0.0 copy-done.5
  43.5 0.1 copy.17
  43.5 0.0 copy-done.1
  43.5 0.0 copy-done.3
  43.6 0.0 copy-done.4
  43.6 0.0 copy-start
  43.6 1.9 %copy-done = f32[48,128,128]{2,1,0:T(8,128)S(1)} copy-done((f32[48,128,128]{2,1,0:T(8,128)S(1)}, f32[48,128,128]{2,1,0:T(8,128)}, u32[]{:S(2)}) %copy-start) | copy-done | bytes 3145752
  45.5 0.0 copy-start.2
  45.5 3.6 %tiles.2 = (bf16[1536,256]{1,0:T(8,128)(2,1)}, bf16[1536,256]{1,0:T(8,128)(2,1)}, bf16[1536,256]{1,0:T(8,128)(2,1)S(1)}, bf16[1536,256]{1,0:T(8,128)(2,1)S(1)}, ...) custom-call(f32[48,128,128]{2,1,0:T(8,128)S(1)} %copy-done, s32[48]{0:T(128)S(1)} %copy-done.1, s32[12,128]{1,0:T(8,128)S(1)} %bitcast.27, ...), custom_call_target="tpu_custom_call" | custom-call | flops 10000000 | bytes 8000000 | tf_op jit(solution)/shard_map/tiles/pallas_call | solution.py:471
  49.1 29.2 %all-to-all-done.arr = f32[32,88,128]{2,1,0:T(8,128)S(1)} async-done(((f32[32,88,128]{2,1,0:T(8,128)}), f32[32,88,128]{2,1,0:T(8,128)S(1)}, u32[]{:S(2)}, u32[]{:S(2)}) %all-to-all-start) | async-done | bytes 1441824 | tf_op jit(solution)/shard_map/all_to_all | solution.py:484
  78.3 0.0 copy-done.2
  78.3 7.6 %errors.1 = (f32[3072,128]{1,0:T(8,128)}, f32[3072,128]{1,0:T(8,128)}, f32[320,128]{1,0:T(8,128)}) custom-call(f32[32,88,128]{2,1,0:T(8,128)S(1)} %all-to-all-done.arr, s32[1,32,72]{2,1,0:T(8,128)S(1)} %copy-done.2, s32[1,32,8]{2,1,0:T(8,128)S(1)} %broadcast_multiply_fusion.bnd.refs_4_, f32[1536,128]{1,0:T(8,128)} %get-tuple-element.28.labk_hbm.refs_6_), custom_call_target="tpu_custom_call" | custom-call | tf_op jit(solution)/shard_map/errors/pallas_call | solution.py:471
  86.0 3.6 %all-to-all-start.1 = ((f32[32,1,1280]{2,1,0:T(1,128)}), f32[32,1,1280]{2,1,0:T(1,128)S(1)}, u32[]{:S(2)}, u32[]{:S(2)}) async-start(f32[32,1,1280]{2,1,0:T(1,128)} %bitcast.8), calls=%async_computation.1 | async-start | bytes 327680 | tf_op jit(solution)/shard_map/all_to_all | solution.py:484
  89.6 5.8 %near.6 = (f32[1536,256]{1,0:T(8,128)S(1)}, f32[8,128]{1,0:T(8,128)S(1)}) custom-call(f32[3072,128]{1,0:T(8,128)} %get-tuple-element.32.v_hbm.e_hbm, f32[3072,128]{1,0:T(8,128)} %get-tuple-element.32.v_hbm.e_hbm, bf16[1536,256]{1,0:T(8,128)(2,1)} %get-tuple-element.33.nh_hbm, bf16[1536,256]{1,0:T(8,128)(2,1)} %get-tuple-element.34.nl_hbm, s32[48]{0:T(128)S(1)} %copy-done.1, ...), custom_call_target="tpu_custom_call" | custom-call | flops 1000000000 | bytes 8000000 | tf_op jit(solution)/shard_map/near/pallas_call | solution.py:471
  95.4 2.8 %all-to-all-done.1 = f32[32,1,1280]{2,1,0:T(1,128)S(1)} async-done(((f32[32,1,1280]{2,1,0:T(1,128)}), f32[32,1,1280]{2,1,0:T(1,128)S(1)}, u32[]{:S(2)}, u32[]{:S(2)}) %all-to-all-start.1) | async-done | bytes 163872 | tf_op jit(solution)/shard_map/all_to_all | solution.py:484
  98.2 3.6 %far_step.3 = (f32[3072,128]{1,0:T(8,128)}, f32[320,128]{1,0:T(8,128)}) custom-call(f32[320,128]{1,0:T(8,128)S(1)} %bitcast.23, bf16[1536,256]{1,0:T(8,128)(2,1)S(1)} %get-tuple-element.30.refs_1_, bf16[1536,256]{1,0:T(8,128)(2,1)S(1)} %get-tuple-element.31.refs_2_, f32[1536,256]{1,0:T(8,128)S(1)} %get-tuple-element.36.refs_3_, ...), custom_call_target="tpu_custom_call" | custom-call | tf_op jit(solution)/shard_map/far_step/pallas_call | solution.py:471
  101.8 3.0 %all-to-all-start.2 = ((f32[32,1,1280]{2,1,0:T(1,128)}), f32[32,1,1280]{2,1,0:T(1,128)S(1)}, u32[]{:S(2)}, u32[]{:S(2)}) async-start(f32[32,1,1280]{2,1,0:T(1,128)} %bitcast.10), calls=%async_computation.2 | async-start | bytes 327680 | tf_op jit(solution)/shard_map/all_to_all | solution.py:484
  104.8 5.7 %near.7.refs_3_ = f32[1536,256]{1,0:T(8,128)S(1)} custom-call(f32[3072,128]{1,0:T(8,128)} %get-tuple-element.38.v_hbm, f32[3072,128]{1,0:T(8,128)} %get-tuple-element.32.v_hbm.e_hbm, bf16[1536,256]{1,0:T(8,128)(2,1)} %get-tuple-element.33.nh_hbm, bf16[1536,256]{1,0:T(8,128)(2,1)} %get-tuple-element.34.nl_hbm, s32[48]{0:T(128)S(1)} %copy-done.1), custom_call_target="tpu_custom_call" | custom-call | flops 1000000000 | bytes 8000000 | tf_op jit(solution)/shard_map/near/pallas_call | solution.py:471
  110.5 3.0 %all-to-all-done.2 = f32[32,1,1280]{2,1,0:T(1,128)S(1)} async-done(((f32[32,1,1280]{2,1,0:T(1,128)}), f32[32,1,1280]{2,1,0:T(1,128)S(1)}, u32[]{:S(2)}, u32[]{:S(2)}) %all-to-all-start.2) | async-done | bytes 163872 | tf_op jit(solution)/shard_map/all_to_all | solution.py:484
  113.5 3.5 %far_sums.1 = (f32[3072,128]{1,0:T(8,128)}, f32[320,128]{1,0:T(8,128)}) custom-call(f32[320,128]{1,0:T(8,128)S(1)} %bitcast.24, bf16[1536,256]{1,0:T(8,128)(2,1)S(1)} %get-tuple-element.30.refs_1_, bf16[1536,256]{1,0:T(8,128)(2,1)S(1)} %get-tuple-element.31.refs_2_, f32[1536,256]{1,0:T(8,128)S(1)} %near.7.refs_3_, ...), custom_call_target="tpu_custom_call" | custom-call | tf_op jit(solution)/shard_map/far_sums/pallas_call | solution.py:471
  117.0 2.9 %all-to-all-start.3 = ((f32[32,1,1280]{2,1,0:T(1,128)}), f32[32,1,1280]{2,1,0:T(1,128)S(1)}, u32[]{:S(2)}, u32[]{:S(2)}) async-start(f32[32,1,1280]{2,1,0:T(1,128)} %bitcast.12), calls=%async_computation.3 | async-start | bytes 327680 | tf_op jit(solution)/shard_map/all_to_all | solution.py:484
  119.9 5.7 %near.8.refs_3_ = f32[1536,256]{1,0:T(8,128)S(1)} custom-call(f32[3072,128]{1,0:T(8,128)} %get-tuple-element.41.v_hbm, f32[3072,128]{1,0:T(8,128)} %get-tuple-element.32.v_hbm.e_hbm, bf16[1536,256]{1,0:T(8,128)(2,1)} %get-tuple-element.33.nh_hbm, bf16[1536,256]{1,0:T(8,128)(2,1)} %get-tuple-element.34.nl_hbm, s32[48]{0:T(128)S(1)} %copy-done.1), custom_call_target="tpu_custom_call" | custom-call | flops 1000000000 | bytes 8000000 | tf_op jit(solution)/shard_map/near/pallas_call | solution.py:471
  125.6 2.9 %all-to-all-done.3 = f32[32,1,1280]{2,1,0:T(1,128)S(1)} async-done(((f32[32,1,1280]{2,1,0:T(1,128)}), f32[32,1,1280]{2,1,0:T(1,128)S(1)}, u32[]{:S(2)}, u32[]{:S(2)}) %all-to-all-start.3) | async-done | bytes 163872 | tf_op jit(solution)/shard_map/all_to_all | solution.py:484
  128.5 6.9 %far_turn.1 = (f32[3072,128]{1,0:T(8,128)}, f32[320,128]{1,0:T(8,128)}) custom-call(f32[320,128]{1,0:T(8,128)S(1)} %bitcast.21, bf16[1536,256]{1,0:T(8,128)(2,1)S(1)} %get-tuple-element.30.refs_1_, bf16[1536,256]{1,0:T(8,128)(2,1)S(1)} %get-tuple-element.31.refs_2_, f32[1536,256]{1,0:T(8,128)S(1)} %near.8.refs_3_, ...), custom_call_target="tpu_custom_call" | custom-call | tf_op jit(solution)/shard_map/far_turn/pallas_call | solution.py:471
  135.4 2.9 %all-to-all-start.4 = ((f32[32,1,1280]{2,1,0:T(1,128)}), f32[32,1,1280]{2,1,0:T(1,128)S(1)}, u32[]{:S(2)}, u32[]{:S(2)}) async-start(f32[32,1,1280]{2,1,0:T(1,128)} %bitcast.14), calls=%async_computation.4 | async-start | bytes 327680 | tf_op jit(solution)/shard_map/all_to_all | solution.py:484
  138.3 5.7 %near.9.refs_3_ = f32[1536,256]{1,0:T(8,128)S(1)} custom-call(f32[3072,128]{1,0:T(8,128)} %get-tuple-element.44.v_hbm.e_hbm, f32[3072,128]{1,0:T(8,128)} %get-tuple-element.44.v_hbm.e_hbm, bf16[1536,256]{1,0:T(8,128)(2,1)} %get-tuple-element.33.nh_hbm, bf16[1536,256]{1,0:T(8,128)(2,1)} %get-tuple-element.34.nl_hbm, s32[48]{0:T(128)S(1)} %copy-done.1), custom_call_target="tpu_custom_call" | custom-call | flops 1000000000 | bytes 8000000 | tf_op jit(solution)/shard_map/near/pallas_call | solution.py:471
  144.0 3.0 %all-to-all-done.4 = f32[32,1,1280]{2,1,0:T(1,128)S(1)} async-done(((f32[32,1,1280]{2,1,0:T(1,128)}), f32[32,1,1280]{2,1,0:T(1,128)S(1)}, u32[]{:S(2)}, u32[]{:S(2)}) %all-to-all-start.4) | async-done | bytes 163872 | tf_op jit(solution)/shard_map/all_to_all | solution.py:484
  146.9 3.6 %far_step.4 = (f32[3072,128]{1,0:T(8,128)}, f32[320,128]{1,0:T(8,128)}) custom-call(f32[320,128]{1,0:T(8,128)S(1)} %bitcast.26, bf16[1536,256]{1,0:T(8,128)(2,1)S(1)} %get-tuple-element.30.refs_1_, bf16[1536,256]{1,0:T(8,128)(2,1)S(1)} %get-tuple-element.31.refs_2_, f32[1536,256]{1,0:T(8,128)S(1)} %near.9.refs_3_, ...), custom_call_target="tpu_custom_call" | custom-call | tf_op jit(solution)/shard_map/far_step/pallas_call | solution.py:471
  150.5 2.9 %all-to-all-start.5 = ((f32[32,1,1280]{2,1,0:T(1,128)}), f32[32,1,1280]{2,1,0:T(1,128)S(1)}, u32[]{:S(2)}, u32[]{:S(2)}) async-start(f32[32,1,1280]{2,1,0:T(1,128)} %bitcast.16), calls=%async_computation.5 | async-start | bytes 327680 | tf_op jit(solution)/shard_map/all_to_all | solution.py:484
  153.4 5.7 %near.10.refs_3_ = f32[1536,256]{1,0:T(8,128)S(1)} custom-call(f32[3072,128]{1,0:T(8,128)} %get-tuple-element.46.v_hbm, f32[3072,128]{1,0:T(8,128)} %get-tuple-element.44.v_hbm.e_hbm, bf16[1536,256]{1,0:T(8,128)(2,1)} %get-tuple-element.33.nh_hbm, bf16[1536,256]{1,0:T(8,128)(2,1)} %get-tuple-element.34.nl_hbm, s32[48]{0:T(128)S(1)} %copy-done.1), custom_call_target="tpu_custom_call" | custom-call | flops 1000000000 | bytes 8000000 | tf_op jit(solution)/shard_map/near/pallas_call | solution.py:471
  159.1 3.0 %all-to-all-done.5 = f32[32,1,1280]{2,1,0:T(1,128)S(1)} async-done(((f32[32,1,1280]{2,1,0:T(1,128)}), f32[32,1,1280]{2,1,0:T(1,128)S(1)}, u32[]{:S(2)}, u32[]{:S(2)}) %all-to-all-start.5) | async-done | bytes 163872 | tf_op jit(solution)/shard_map/all_to_all | solution.py:484
  162.0 3.5 %far_step.5 = (f32[3072,128]{1,0:T(8,128)}, f32[320,128]{1,0:T(8,128)}) custom-call(f32[320,128]{1,0:T(8,128)S(1)} %bitcast.25, bf16[1536,256]{1,0:T(8,128)(2,1)S(1)} %get-tuple-element.30.refs_1_, bf16[1536,256]{1,0:T(8,128)(2,1)S(1)} %get-tuple-element.31.refs_2_, f32[1536,256]{1,0:T(8,128)S(1)} %near.10.refs_3_, ...), custom_call_target="tpu_custom_call" | custom-call | tf_op jit(solution)/shard_map/far_step/pallas_call | solution.py:471
  165.6 2.9 %all-to-all-start.6 = ((f32[32,1,1280]{2,1,0:T(1,128)}), f32[32,1,1280]{2,1,0:T(1,128)S(1)}, u32[]{:S(2)}, u32[]{:S(2)}) async-start(f32[32,1,1280]{2,1,0:T(1,128)} %bitcast.18), calls=%async_computation.6 | async-start | bytes 327680 | tf_op jit(solution)/shard_map/all_to_all | solution.py:484
  168.5 5.7 %near.11.refs_3_ = f32[1536,256]{1,0:T(8,128)S(1)} custom-call(f32[3072,128]{1,0:T(8,128)} %get-tuple-element.48.v_hbm, f32[3072,128]{1,0:T(8,128)} %get-tuple-element.44.v_hbm.e_hbm, bf16[1536,256]{1,0:T(8,128)(2,1)} %get-tuple-element.33.nh_hbm, bf16[1536,256]{1,0:T(8,128)(2,1)} %get-tuple-element.34.nl_hbm, s32[48]{0:T(128)S(1)} %copy-done.1), custom_call_target="tpu_custom_call" | custom-call | flops 1000000000 | bytes 8000000 | tf_op jit(solution)/shard_map/near/pallas_call | solution.py:471
  174.2 3.0 %all-to-all-done.6 = f32[32,1,1280]{2,1,0:T(1,128)S(1)} async-done(((f32[32,1,1280]{2,1,0:T(1,128)}), f32[32,1,1280]{2,1,0:T(1,128)S(1)}, u32[]{:S(2)}, u32[]{:S(2)}) %all-to-all-start.6) | async-done | bytes 163872 | tf_op jit(solution)/shard_map/all_to_all | solution.py:484
  177.1 2.2 %far_last.1 = f32[153,1536]{1,0:T(8,128)} custom-call(f32[320,128]{1,0:T(8,128)S(1)} %bitcast.22, bf16[1536,256]{1,0:T(8,128)(2,1)S(1)} %get-tuple-element.30.refs_1_, bf16[1536,256]{1,0:T(8,128)(2,1)S(1)} %get-tuple-element.31.refs_2_, f32[1536,256]{1,0:T(8,128)S(1)} %near.11.refs_3_), custom_call_target="tpu_custom_call" | custom-call | tf_op jit(solution)/shard_map/far_last/pallas_call | solution.py:471
  (1 shorter events, 0.0 us)
Async XLA Ops:
  36.1 7.4 %copy-start.5 = (s32[1,32,8]{1,2,0:T(8,128)S(1)}, s32[1,32,8]{1,2,0:T(8,128)}, u32[]{:S(2)}) copy-start(s32[1,32,8]{1,2,0:T(8,128)} %param.27) | copy-start | bytes 3076
  36.1 7.5 %copy-start.1 = (s32[48]{0:T(128)S(1)}, s32[48]{0:T(128)}, u32[]{:S(2)}) copy-start(s32[48]{0:T(128)} %cols.13) | copy-start | bytes 580
  36.1 7.5 %copy-start.3 = (s32[1536]{0:T(1024)S(1)}, s32[1536]{0:T(1024)}, u32[]{:S(2)}) copy-start(s32[1536]{0:T(1024)} %param.25) | copy-start | bytes 18436
  36.1 7.4 %copy-start.4 = (s32[1536]{0:T(1024)S(1)}, s32[1536]{0:T(1024)}, u32[]{:S(2)}) copy-start(s32[1536]{0:T(1024)} %param.26) | copy-start | bytes 18436
  36.1 42.2 %all-to-all-start = ((f32[32,88,128]{2,1,0:T(8,128)}), f32[32,88,128]{2,1,0:T(8,128)S(1)}, u32[]{:S(2)}, u32[]{:S(2)}) async-start(f32[32,88,128]{2,1,0:T(8,128)} %get-tuple-element.27), calls=%async_computation | async-start | bytes 2883584 | tf_op jit(solution)/shard_map/all_to_all | solution.py:484
  43.6 1.9 %copy-start = (f32[48,128,128]{2,1,0:T(8,128)S(1)}, f32[48,128,128]{2,1,0:T(8,128)}, u32[]{:S(2)}) copy-start(f32[48,128,128]{2,1,0:T(8,128)} %tiles.3) | copy-start | bytes 9437188
  45.5 32.9 %copy-start.2 = (s32[1,32,72]{2,1,0:T(8,128)S(1)}, s32[1,32,72]{2,1,0:T(8,128)}, u32[]{:S(2)}) copy-start(s32[1,32,72]{2,1,0:T(8,128)} %recv.1) | copy-start | bytes 27652
  86.0 12.3 %all-to-all-start.1 = ((f32[32,1,1280]{2,1,0:T(1,128)}), f32[32,1,1280]{2,1,0:T(1,128)S(1)}, u32[]{:S(2)}, u32[]{:S(2)}) async-start(f32[32,1,1280]{2,1,0:T(1,128)} %bitcast.8), calls=%async_computation.1 | async-start | bytes 327680 | tf_op jit(solution)/shard_map/all_to_all | solution.py:484
  101.8 11.7 %all-to-all-start.2 = ((f32[32,1,1280]{2,1,0:T(1,128)}), f32[32,1,1280]{2,1,0:T(1,128)S(1)}, u32[]{:S(2)}, u32[]{:S(2)}) async-start(f32[32,1,1280]{2,1,0:T(1,128)} %bitcast.10), calls=%async_computation.2 | async-start | bytes 327680 | tf_op jit(solution)/shard_map/all_to_all | solution.py:484
  117.0 11.5 %all-to-all-start.3 = ((f32[32,1,1280]{2,1,0:T(1,128)}), f32[32,1,1280]{2,1,0:T(1,128)S(1)}, u32[]{:S(2)}, u32[]{:S(2)}) async-start(f32[32,1,1280]{2,1,0:T(1,128)} %bitcast.12), calls=%async_computation.3 | async-start | bytes 327680 | tf_op jit(solution)/shard_map/all_to_all | solution.py:484
  135.4 11.5 %all-to-all-start.4 = ((f32[32,1,1280]{2,1,0:T(1,128)}), f32[32,1,1280]{2,1,0:T(1,128)S(1)}, u32[]{:S(2)}, u32[]{:S(2)}) async-start(f32[32,1,1280]{2,1,0:T(1,128)} %bitcast.14), calls=%async_computation.4 | async-start | bytes 327680 | tf_op jit(solution)/shard_map/all_to_all | solution.py:484
  150.5 11.5 %all-to-all-start.5 = ((f32[32,1,1280]{2,1,0:T(1,128)}), f32[32,1,1280]{2,1,0:T(1,128)S(1)}, u32[]{:S(2)}, u32[]{:S(2)}) async-start(f32[32,1,1280]{2,1,0:T(1,128)} %bitcast.16), calls=%async_computation.5 | async-start | bytes 327680 | tf_op jit(solution)/shard_map/all_to_all | solution.py:484
  165.6 11.5 %all-to-all-start.6 = ((f32[32,1,1280]{2,1,0:T(1,128)}), f32[32,1,1280]{2,1,0:T(1,128)S(1)}, u32[]{:S(2)}, u32[]{:S(2)}) async-start(f32[32,1,1280]{2,1,0:T(1,128)} %bitcast.18), calls=%async_computation.6 | async-start | bytes 327680 | tf_op jit(solution)/shard_map/all_to_all | solution.py:484

commit v5 on v4

--- a/solution.py
+++ b/solution.py
@@ -21,6 +21,7 @@
 VM = pl.BlockSpec(memory_space=pltpu.VMEM)
 SM = pl.BlockSpec(memory_space=pltpu.SMEM)
 HB = pl.BlockSpec(memory_space=pltpu.HBM)
+VO = pl.BlockSpec(memory_space=pltpu.VMEM)
 MIB = 1 << 20
 
 
@@ -45,13 +46,15 @@
     return ref.at[pl.ds(pl.multiple_of(2 * row, 2), 2), :]
 
 
-def gather_rows(idx_ref, src, stg, peers, slots):
+def gather_rows(idx, src, stg, peers, slots):
+    copy, idx_ref = idx
+    copy.wait()
     group = 4
 
     def body(g, _):
         for p in range(group):
             for k in range(slots):
-                at = pl.ds(pl.multiple_of(idx_ref[0, g * group + p, k], 2), 2)
+                at = pl.ds(pl.multiple_of(idx_ref[g * group + p, k], 2), 2)
                 pair(stg, g * (group * slots) + (p * slots + k))[...] = src[at, :]
         return 0
 
@@ -66,10 +69,12 @@
 
 
 def scores_kernel(
-    hid, bt, st, bias, coef, es, ed, er, send, out, blank,
-    pt, p0, m2, s0, s1, s2, s3, sc2, stg, kj, kd, kp, zero, sj, sd, sp, sz, *ks, classes, slots, per,
+    hid_hbm, bt, st, bias, coef, es, ed, er, send, out, blank,
+    hid, pt, p0, m2, s0, s1, s2, s3, sc2, stg, kj, kd, kp, zero, sj, sd, sp, sz, *ks, classes, slots, per,
 ):
     n, hdim = hid.shape
+    hload = pltpu.make_async_copy(hid_hbm, hid, sz.at[1 + 4 * coef.shape[0]])
+    hload.start()
     rest = classes - L
     nrel, nb = coef.shape
     peers = out.shape[0]
@@ -105,7 +110,7 @@
     lax.fori_loop(0, hdim // step, arrange, 0)
     wipe.wait()
     zrows = blank.shape[0]
-    for c, s in enumerate(acc):
+    for c, s in enumerate(acc[:3]):
         for i in range(nrel):
             copies.append(pltpu.make_async_copy(blank, s.at[pl.ds(i * zrows, zrows), :], sz.at[1 + c * nrel + i]))
             copies[-1].start()
@@ -159,7 +164,14 @@
         return 0
 
     sc2[pl.ds(2 * n, 16), :] = jnp.zeros((16, L), F32)
+    hload.wait()
     lax.fori_loop(0, n // chunk, project, 0)
+
+    def clear(i, _):
+        s3[pl.ds(pl.multiple_of(i * 512, 512), 512), :] = jnp.zeros((512, L), F32)
+        return 0
+
+    lax.fori_loop(0, s3.shape[0] // 512, clear, 0)
     for c in copies:
         c.wait()
 
@@ -235,7 +247,7 @@
 
 
 def errors_kernel(
-    arr, recv, bnd, labk_hbm, base_hbm, e_hbm, out, stg, base2, v2, stgb, labk, kr, sems, sr, esem, *ksr,
+    arr, recv, bnd_hbm, labk_hbm, t_hbm, e_hbm, out, stg, base2, v2, stgb, labk, kr, bnd, sems, sr, esem, *ksr,
     classes, per, n,
 ):
     rest = classes - L
@@ -245,6 +257,8 @@
     tlane = lanes(ntail)
     load = pltpu.make_async_copy(labk_hbm, labk, sems.at[0])
     load.start()
+    bcopy = pltpu.make_async_copy(bnd_hbm.at[0], bnd, sems.at[1])
+    bcopy.start()
     kr[:, 0:slots] = recv[0] * 2
     copies = fetch(kr, range(peers), ksr, sr)
 
@@ -273,8 +287,6 @@
         return 0
 
     lax.fori_loop(0, slots // unroll, spread, 0)
-    keep = pltpu.make_async_copy(base2.at[pl.ds(0, 2 * n), :], base_hbm, sems.at[1])
-    keep.start()
     load.wait()
 
     chunk = 128
@@ -287,20 +299,25 @@
         for h in range(2):
             rows = pl.ds(2 * row + h, chunk, stride=2)
             onehot = jnp.where(lab == (lane + h * L).astype(F32), 1.0, 0.0)
-            v2[rows, :] = jnp.where(known, onehot - base2[rows, :], 0.0)
-        piece(i).start()
-        return 0
-
-    def piece(i):
+            b = base2[rows, :]
+            v2[rows, :] = jnp.where(known, onehot - b, 0.0)
+            t = jnp.where(known, onehot, b)
+            base2[rows, :] = jnp.where(lane == L - 1, jnp.where(known, 0.0, 1.0), t) if h else t
+        piece(i, 0).start()
+        piece(i, 1).start()
+        return 0
+
+    def piece(i, w):
         rows = pl.ds(pl.multiple_of(2 * i * chunk, 2 * chunk), 2 * chunk)
-        return pltpu.make_async_copy(v2.at[rows, :], e_hbm.at[rows, :], esem.at[i])
+        a, b = ((v2, e_hbm), (base2, t_hbm))[w]
+        return pltpu.make_async_copy(a.at[rows, :], b.at[rows, :], esem.at[w, i])
 
     v2[pl.ds(2 * n, 16), :] = jnp.zeros((16, L), F32)
     lax.fori_loop(0, n // chunk, error, 0)
-    pack(bnd, v2, stgb, out, None, peers=peers, slots=bnd.shape[2], per=per, rest=rest)
-    keep.wait()
+    pack((bcopy, bnd), v2, stgb, out, None, peers=peers, slots=bnd.shape[1], per=per, rest=rest)
     for i in range(n // chunk):
-        piece(i).wait()
+        piece(i, 0).wait()
+        piece(i, 1).wait()
 
 
 def tiles_kernel(tiles, cols, labels, mask, nh_hbm, nl_hbm, fh, fl, lab_hbm, cnt, nh, nl, labk, sems):
@@ -386,14 +403,17 @@
     arr, fh, fl, part = refs[:4]
     refs = refs[4:]
     if mode != "last":
-        bnd = refs.pop(0)
+        bnd_hbm, bnd, bsem = refs.pop(0), refs.pop(), refs.pop()
+        bcopy = pltpu.make_async_copy(bnd_hbm.at[0], bnd, bsem)
+        bcopy.start()
     if mode == "sums":
         tot = refs.pop(0)
     if mode == "turn":
-        base_hbm, lab_hbm, base2, labk, sems = refs.pop(0), refs.pop(0), refs.pop(), refs.pop(), refs.pop()
+        t_hbm, t2, sems = refs.pop(0), refs.pop(), refs.pop()
+        half = t2.shape[0] // 2
         loads = [
-            pltpu.make_async_copy(base_hbm, base2, sems.at[0]),
-            pltpu.make_async_copy(lab_hbm, labk, sems.at[1]),
+            pltpu.make_async_copy(t_hbm.at[pl.ds(i * half, half), :], t2.at[pl.ds(i * half, half), :], sems.at[i])
+            for i in range(2)
         ]
         for c in loads:
             c.start()
@@ -416,9 +436,6 @@
             x = jnp.where(tlane < rest, x, 0.0)
             hr[pl.ds(j * per + q, peers, stride=slots), :] = x
     hh, hl = split(jnp.concatenate([hm[...], hr[...]], 1))
-    if mode == "turn":
-        for c in loads:
-            c.wait()
 
     chunk = n // 2
     lane = lanes(chunk)
@@ -444,14 +461,16 @@
         if mode == "turn":
             mag = jnp.abs(v)
             mag = jnp.sum(mag[:, :L] + mag[:, L:], -1, keepdims=True) * (1.0 / classes) + tiny
-            scale = sigma / mag
-            lab = labk[rows, :]
+            hit = pl.ds(pl.multiple_of(i * half, half), half)
+            pltpu.make_async_copy(t_hbm.at[hit, :], t2.at[hit, :], sems.at[i]).wait()
+            free = t2[pl.ds(2 * row + 1, chunk, stride=2), :]
+            scale = free[:, L - 1 : L] * sigma / mag
         for h in range(2):
             x = v[:, h * L : (h + 1) * L]
             rows2 = pl.ds(2 * row + h, chunk, stride=2)
             if mode == "turn":
-                onehot = jnp.where(lab == (lane + h * L).astype(F32), 1.0, 0.0)
-                x = jnp.where(lab >= 0.0, onehot, base2[rows2, :] + scale * x)
+                x = t2[rows2, :] + scale * x
+                x = jnp.where(lane < rest, x, 0.0) if h else x
             v2[rows2, :] = x
         piece(i).start()
         return 0
@@ -459,14 +478,15 @@
     lax.fori_loop(0, count, body, 0)
     if mode != "last":
         extra = tot[0:1, :] if mode == "sums" else None
-        pack(bnd, v2, stgb, out, extra, peers=peers, slots=slots, per=per, rest=rest)
+        pack((bcopy, bnd), v2, stgb, out, extra, peers=peers, slots=slots, per=per, rest=rest)
         for i in range(count):
             piece(i).wait()
 
 
 def call(kernel, outs, ins, args, scratch=(), vmem=0, flops=0, size=0, name=None, specs=None):
     if specs:
-        outs = tuple(pltpu.HBM(o.shape, o.dtype) if p is HB else o for o, p in zip(outs, specs))
+        place = {id(HB): pltpu.HBM, id(VO): pltpu.VMEM}
+        outs = tuple(place.get(id(p), jax.ShapeDtypeStruct)(o.shape, o.dtype) for o, p in zip(outs, specs))
     args = [pltpu.with_memory_space_constraint(a, pltpu.HBM) if p is HB else a for a, p in zip(args, ins)]
     return pl.pallas_call(
         kernel,
@@ -514,16 +534,16 @@
     sent, _ = call(
         functools.partial(scores_kernel, classes=classes, slots=slots, per=per),
         (sds((peers, blk, L), F32), sds((2 * n, L), F32)),
-        [VM, VM, VM, VM, SM, VM, VM, VM, VM],
+        [HB, VM, VM, VM, SM, VM, VM, VM, VM],
         (hidden, bases.T, self_weight.T, bias.reshape(1, -1), coef)
         + (square(edge_src), square(edge_dst), square(edge_rel), send_rows),
-        [pltpu.VMEM((wide, hdim), BF16)]
+        [pltpu.VMEM((n, hdim), BF16), pltpu.VMEM((wide, hdim), BF16)]
         + [pltpu.VMEM((n // 2, wide), F32)]
         + [sums] * 5
         + [rows2, stage]
         + [pltpu.VMEM((erows, L), jnp.int32)] * 2
         + [pltpu.VMEM((peers, L), jnp.int32), pltpu.VMEM((2 * n, L), F32), dma(erows), dma(erows), dma(peers)]
-        + [dma(1 + 4 * nrel)]
+        + [dma(2 + 4 * nrel)]
         + [pltpu.SMEM((1, L), jnp.int32)] * (2 * erows + peers),
         vmem=60 * MIB,
         name="scores",
@@ -549,16 +569,18 @@
     lines = peers * (bnd + up(bnd, per))
     packed = sds((lines, L), F32)
     stageb = pltpu.VMEM((2 * halo, L), F32)
+    bnds = pltpu.SMEM((peers, bnd), jnp.int32)
     base, v, out = call(
         functools.partial(errors_kernel, classes=classes, per=per, n=n),
         (spread, spread, packed),
-        [VM, VM, SM, HB],
+        [VM, VM, HB, HB],
         (arrived, recv_rows, bnd_rows, labk),
-        [stage, rows2, rows2, stageb, labv, pltpu.VMEM((peers, L), jnp.int32), dma(2), dma(peers), dma(n // L)]
+        [stage, rows2, rows2, stageb, labv, pltpu.VMEM((peers, L), jnp.int32), bnds, dma(2), dma(peers)]
+        + [pltpu.SemaphoreType.DMA((2, n // L))]
         + [pltpu.SMEM((1, L), jnp.int32)] * peers,
         vmem=28 * MIB,
         name="errors",
-        specs=(HB, HB, VM),
+        specs=(HB, HB, VO),
     )
     e = v
     hscr = [pltpu.VMEM((halo, L), F32)] * 2
@@ -587,15 +609,16 @@
         args, ins = (halos, fh, fl, part), [VM] * 4
         if mode == "last":
             return call(far, sds((classes, n), F32), ins, args, hscr, vmem=24 * MIB, name="far_last").T
-        args, ins = args + (bnd_rows,), ins + [SM]
+        args, ins = args + (bnd_rows,), ins + [HB]
         scratch = hscr + [rows2, stageb, dma(n // L)]
         if mode == "sums":
             args, ins = args + (tot,), ins + [VM]
         if mode == "turn":
-            args, ins = args + (base, labk), ins + [HB, HB]
-            scratch = scratch + [dma(2), labv, flat2]
+            args, ins = args + (base,), ins + [HB]
+            scratch = scratch + [dma(2), flat2]
+        scratch = scratch + [pltpu.SemaphoreType.DMA, bnds]
         v, out = call(
-            far, (spread, packed), ins, args, scratch, vmem=24 * MIB, name="far_" + mode, specs=(HB, VM)
+            far, (spread, packed), ins, args, scratch, vmem=24 * MIB, name="far_" + mode, specs=(HB, VO)
         )
         if mode == "turn":
             e = v

time: 180 us -> 174 us (0.967)
  Pallas kernels: 105 us -> 98.4 us
    pallas_call x15, Pallas kernels: 105 us -> 98.4 us  [call(): pl.pallas_call(kernel, out_shape=outs, in_specs=ins, out_specs=specs or j...]
  transfers between devices with their start and end apart: 7 -> 7, of which waited for: 7 -> 7; matrix products, arithmetic and copies ran while one was open for 0% -> 0% of each run, Pallas kernels for 21% -> 22%
where the time goes in v5:
time: 174 us; the launch traced here: 173 us
  Pallas kernels  98.4 us (57%)
  waiting for transfers between devices  46.2 us (27%)
  starting transfers between devices  25.6 us (15%)
  local copies, waits for them, and re-layouts  1.99 us (1%)
    pallas_call x15, Pallas kernels, call(): pl.pallas_call(kernel, out_shape=outs, in_specs=ins, out_specs=specs or j...  98.4 us
    all_to_all x7, waiting for transfers between devices, swap(): return lax.all_to_all(x, 'dom', split_axis=0, concat_axis=0, tiled=True)  46.2 us
    all_to_all x7, starting transfers between devices, swap(): return lax.all_to_all(x, 'dom', split_axis=0, concat_axis=0, tiled=True)  25.6 us
  transfers between devices with their start and end apart: 7, of which 7 were waited for; matrix products, arithmetic and copies ran while one was open for 0% of the time, Pallas kernels for 22%

profile of v5, /device:TPU:0, one launch (start us, length us, event | category | flops | bytes accessed | tf_op | source)
XLA Modules:
  0.0 173.0 jit_solution(1632262838542304523)
XLA Ops:
  0.0 36.4 %scores.1 = (f32[32,88,128]{2,1,0:T(8,128)}, f32[3072,128]{1,0:T(8,128)}) custom-call(bf16[1536,1024]{1,0:T(8,128)(2,1)} %hid_hbm.1, bf16[1224,1024]{1,0:T(8,128)(2,1)} %bitcast.29, bf16[153,1024]{1,0:T(8,128)(2,1)} %bitcast.30, f32[1,153]{1,0:T(1,128)} %bitcast.34, f32[5,8]{1,0:T(8,128)} %coef.1, s32[48,128]{1,0:T(8,128)} %bitcast.31, s32[48,128]{1,0:T(8,128)} %bitcast.32, ...), custom_call_target="tpu_custom_call" | custom-call | tf_op jit(solution)/shard_map/scores/pallas_call | solution.py:491
  36.4 0.0 copy-start.5
  36.4 0.0 copy-start.1
  36.4 0.0 copy-start.3
  36.5 0.0 copy-start.4
  36.5 7.3 %all-to-all-start = ((f32[32,88,128]{2,1,0:T(8,128)}), f32[32,88,128]{2,1,0:T(8,128)S(1)}, u32[]{:S(2)}, u32[]{:S(2)}) async-start(f32[32,88,128]{2,1,0:T(8,128)} %get-tuple-element.27), calls=%async_computation | async-start | bytes 2883584 | tf_op jit(solution)/shard_map/all_to_all | solution.py:504
  43.8 0.0 copy-done.5
  43.8 0.1 copy.17
  43.9 0.0 copy-done.1
  43.9 0.0 copy-done.3
  43.9 0.0 copy-done.4
  43.9 0.0 copy-start
  43.9 1.9 %copy-done = f32[48,128,128]{2,1,0:T(8,128)S(1)} copy-done((f32[48,128,128]{2,1,0:T(8,128)S(1)}, f32[48,128,128]{2,1,0:T(8,128)}, u32[]{:S(2)}) %copy-start) | copy-done | bytes 3145752
  45.8 0.0 copy-start.2
  45.8 3.6 %tiles.2 = (bf16[1536,256]{1,0:T(8,128)(2,1)}, bf16[1536,256]{1,0:T(8,128)(2,1)}, bf16[1536,256]{1,0:T(8,128)(2,1)S(1)}, bf16[1536,256]{1,0:T(8,128)(2,1)S(1)}, ...) custom-call(f32[48,128,128]{2,1,0:T(8,128)S(1)} %copy-done, s32[48]{0:T(128)S(1)} %copy-done.1, s32[12,128]{1,0:T(8,128)S(1)} %bitcast.27, ...), custom_call_target="tpu_custom_call" | custom-call | flops 10000000 | bytes 8000000 | tf_op jit(solution)/shard_map/tiles/pallas_call | solution.py:491
  49.4 0.6 broadcast_multiply_fusion.bnd_hbm.refs_4_
  50.0 28.6 %all-to-all-done.arr = f32[32,88,128]{2,1,0:T(8,128)S(1)} async-done(((f32[32,88,128]{2,1,0:T(8,128)}), f32[32,88,128]{2,1,0:T(8,128)S(1)}, u32[]{:S(2)}, u32[]{:S(2)}) %all-to-all-start) | async-done | bytes 1441824 | tf_op jit(solution)/shard_map/all_to_all | solution.py:504
  78.6 0.0 copy-done.2
  78.6 7.0 %errors.1 = (f32[3072,128]{1,0:T(8,128)}, f32[3072,128]{1,0:T(8,128)}, f32[320,128]{1,0:T(8,128)}) custom-call(f32[32,88,128]{2,1,0:T(8,128)S(1)} %all-to-all-done.arr, s32[1,32,72]{2,1,0:T(8,128)S(1)} %copy-done.2, s32[1,32,8]{2,1,0:T(8,128)} %broadcast_multiply_fusion.bnd_hbm.refs_4_, f32[1536,128]{1,0:T(8,128)} %get-tuple-element.28.labk_hbm), custom_call_target="tpu_custom_call" | custom-call | tf_op jit(solution)/shard_map/errors/pallas_call | solution.py:491
  85.7 3.6 %all-to-all-start.1 = ((f32[32,1,1280]{2,1,0:T(1,128)}), f32[32,1,1280]{2,1,0:T(1,128)S(1)}, u32[]{:S(2)}, u32[]{:S(2)}) async-start(f32[32,1,1280]{2,1,0:T(1,128)} %bitcast.8), calls=%async_computation.1 | async-start | bytes 327680 | tf_op jit(solution)/shard_map/all_to_all | solution.py:504
  89.3 5.8 %near.6 = (f32[1536,256]{1,0:T(8,128)S(1)}, f32[8,128]{1,0:T(8,128)S(1)}) custom-call(f32[3072,128]{1,0:T(8,128)} %get-tuple-element.32.v_hbm.e_hbm, f32[3072,128]{1,0:T(8,128)} %get-tuple-element.32.v_hbm.e_hbm, bf16[1536,256]{1,0:T(8,128)(2,1)} %get-tuple-element.33.nh_hbm, bf16[1536,256]{1,0:T(8,128)(2,1)} %get-tuple-element.34.nl_hbm, s32[48]{0:T(128)S(1)} %copy-done.1, ...), custom_call_target="tpu_custom_call" | custom-call | flops 1000000000 | bytes 8000000 | tf_op jit(solution)/shard_map/near/pallas_call | solution.py:491
  95.1 2.8 %all-to-all-done.1 = f32[32,1,1280]{2,1,0:T(1,128)S(1)} async-done(((f32[32,1,1280]{2,1,0:T(1,128)}), f32[32,1,1280]{2,1,0:T(1,128)S(1)}, u32[]{:S(2)}, u32[]{:S(2)}) %all-to-all-start.1) | async-done | bytes 163872 | tf_op jit(solution)/shard_map/all_to_all | solution.py:504
  98.0 2.8 %far_step.3 = (f32[3072,128]{1,0:T(8,128)}, f32[320,128]{1,0:T(8,128)}) custom-call(f32[320,128]{1,0:T(8,128)S(1)} %bitcast.23, bf16[1536,256]{1,0:T(8,128)(2,1)S(1)} %get-tuple-element.30.refs_1_, bf16[1536,256]{1,0:T(8,128)(2,1)S(1)} %get-tuple-element.31.refs_2_, f32[1536,256]{1,0:T(8,128)S(1)} %get-tuple-element.36.refs_3_, ...), custom_call_target="tpu_custom_call" | custom-call | tf_op jit(solution)/shard_map/far_step/pallas_call | solution.py:491
  100.7 3.0 %all-to-all-start.2 = ((f32[32,1,1280]{2,1,0:T(1,128)}), f32[32,1,1280]{2,1,0:T(1,128)S(1)}, u32[]{:S(2)}, u32[]{:S(2)}) async-start(f32[32,1,1280]{2,1,0:T(1,128)} %bitcast.10), calls=%async_computation.2 | async-start | bytes 327680 | tf_op jit(solution)/shard_map/all_to_all | solution.py:504
  103.8 5.7 %near.7.refs_3_ = f32[1536,256]{1,0:T(8,128)S(1)} custom-call(f32[3072,128]{1,0:T(8,128)} %get-tuple-element.38.v_hbm, f32[3072,128]{1,0:T(8,128)} %get-tuple-element.32.v_hbm.e_hbm, bf16[1536,256]{1,0:T(8,128)(2,1)} %get-tuple-element.33.nh_hbm, bf16[1536,256]{1,0:T(8,128)(2,1)} %get-tuple-element.34.nl_hbm, s32[48]{0:T(128)S(1)} %copy-done.1), custom_call_target="tpu_custom_call" | custom-call | flops 1000000000 | bytes 8000000 | tf_op jit(solution)/shard_map/near/pallas_call | solution.py:491
  109.4 3.0 %all-to-all-done.2 = f32[32,1,1280]{2,1,0:T(1,128)S(1)} async-done(((f32[32,1,1280]{2,1,0:T(1,128)}), f32[32,1,1280]{2,1,0:T(1,128)S(1)}, u32[]{:S(2)}, u32[]{:S(2)}) %all-to-all-start.2) | async-done | bytes 163872 | tf_op jit(solution)/shard_map/all_to_all | solution.py:504
  112.4 2.8 %far_sums.1 = (f32[3072,128]{1,0:T(8,128)}, f32[320,128]{1,0:T(8,128)}) custom-call(f32[320,128]{1,0:T(8,128)S(1)} %bitcast.24, bf16[1536,256]{1,0:T(8,128)(2,1)S(1)} %get-tuple-element.30.refs_1_, bf16[1536,256]{1,0:T(8,128)(2,1)S(1)} %get-tuple-element.31.refs_2_, f32[1536,256]{1,0:T(8,128)S(1)} %near.7.refs_3_, ...), custom_call_target="tpu_custom_call" | custom-call | tf_op jit(solution)/shard_map/far_sums/pallas_call | solution.py:491
  115.2 2.9 %all-to-all-start.3 = ((f32[32,1,1280]{2,1,0:T(1,128)}), f32[32,1,1280]{2,1,0:T(1,128)S(1)}, u32[]{:S(2)}, u32[]{:S(2)}) async-start(f32[32,1,1280]{2,1,0:T(1,128)} %bitcast.12), calls=%async_computation.3 | async-start | bytes 327680 | tf_op jit(solution)/shard_map/all_to_all | solution.py:504
  118.1 5.7 %near.8.refs_3_ = f32[1536,256]{1,0:T(8,128)S(1)} custom-call(f32[3072,128]{1,0:T(8,128)} %get-tuple-element.41.v_hbm, f32[3072,128]{1,0:T(8,128)} %get-tuple-element.32.v_hbm.e_hbm, bf16[1536,256]{1,0:T(8,128)(2,1)} %get-tuple-element.33.nh_hbm, bf16[1536,256]{1,0:T(8,128)(2,1)} %get-tuple-element.34.nl_hbm, s32[48]{0:T(128)S(1)} %copy-done.1), custom_call_target="tpu_custom_call" | custom-call | flops 1000000000 | bytes 8000000 | tf_op jit(solution)/shard_map/near/pallas_call | solution.py:491
  123.7 2.9 %all-to-all-done.3 = f32[32,1,1280]{2,1,0:T(1,128)S(1)} async-done(((f32[32,1,1280]{2,1,0:T(1,128)}), f32[32,1,1280]{2,1,0:T(1,128)S(1)}, u32[]{:S(2)}, u32[]{:S(2)}) %all-to-all-start.3) | async-done | bytes 163872 | tf_op jit(solution)/shard_map/all_to_all | solution.py:504
  126.7 4.0 %far_turn.1 = (f32[3072,128]{1,0:T(8,128)}, f32[320,128]{1,0:T(8,128)}) custom-call(f32[320,128]{1,0:T(8,128)S(1)} %bitcast.21, bf16[1536,256]{1,0:T(8,128)(2,1)S(1)} %get-tuple-element.30.refs_1_, bf16[1536,256]{1,0:T(8,128)(2,1)S(1)} %get-tuple-element.31.refs_2_, f32[1536,256]{1,0:T(8,128)S(1)} %near.8.refs_3_, ...), custom_call_target="tpu_custom_call" | custom-call | tf_op jit(solution)/shard_map/far_turn/pallas_call | solution.py:491
  130.7 2.9 %all-to-all-start.4 = ((f32[32,1,1280]{2,1,0:T(1,128)}), f32[32,1,1280]{2,1,0:T(1,128)S(1)}, u32[]{:S(2)}, u32[]{:S(2)}) async-start(f32[32,1,1280]{2,1,0:T(1,128)} %bitcast.14), calls=%async_computation.4 | async-start | bytes 327680 | tf_op jit(solution)/shard_map/all_to_all | solution.py:504
  133.6 5.7 %near.9.refs_3_ = f32[1536,256]{1,0:T(8,128)S(1)} custom-call(f32[3072,128]{1,0:T(8,128)} %get-tuple-element.44.v_hbm.e_hbm, f32[3072,128]{1,0:T(8,128)} %get-tuple-element.44.v_hbm.e_hbm, bf16[1536,256]{1,0:T(8,128)(2,1)} %get-tuple-element.33.nh_hbm, bf16[1536,256]{1,0:T(8,128)(2,1)} %get-tuple-element.34.nl_hbm, s32[48]{0:T(128)S(1)} %copy-done.1), custom_call_target="tpu_custom_call" | custom-call | flops 1000000000 | bytes 8000000 | tf_op jit(solution)/shard_map/near/pallas_call | solution.py:491
  139.3 2.9 %all-to-all-done.4 = f32[32,1,1280]{2,1,0:T(1,128)S(1)} async-done(((f32[32,1,1280]{2,1,0:T(1,128)}), f32[32,1,1280]{2,1,0:T(1,128)S(1)}, u32[]{:S(2)}, u32[]{:S(2)}) %all-to-all-start.4) | async-done | bytes 163872 | tf_op jit(solution)/shard_map/all_to_all | solution.py:504
  142.2 2.8 %far_step.4 = (f32[3072,128]{1,0:T(8,128)}, f32[320,128]{1,0:T(8,128)}) custom-call(f32[320,128]{1,0:T(8,128)S(1)} %bitcast.26, bf16[1536,256]{1,0:T(8,128)(2,1)S(1)} %get-tuple-element.30.refs_1_, bf16[1536,256]{1,0:T(8,128)(2,1)S(1)} %get-tuple-element.31.refs_2_, f32[1536,256]{1,0:T(8,128)S(1)} %near.9.refs_3_, ...), custom_call_target="tpu_custom_call" | custom-call | tf_op jit(solution)/shard_map/far_step/pallas_call | solution.py:491
  145.0 2.9 %all-to-all-start.5 = ((f32[32,1,1280]{2,1,0:T(1,128)}), f32[32,1,1280]{2,1,0:T(1,128)S(1)}, u32[]{:S(2)}, u32[]{:S(2)}) async-start(f32[32,1,1280]{2,1,0:T(1,128)} %bitcast.16), calls=%async_computation.5 | async-start | bytes 327680 | tf_op jit(solution)/shard_map/all_to_all | solution.py:504
  147.9 5.7 %near.10.refs_3_ = f32[1536,256]{1,0:T(8,128)S(1)} custom-call(f32[3072,128]{1,0:T(8,128)} %get-tuple-element.46.v_hbm, f32[3072,128]{1,0:T(8,128)} %get-tuple-element.44.v_hbm.e_hbm, bf16[1536,256]{1,0:T(8,128)(2,1)} %get-tuple-element.33.nh_hbm, bf16[1536,256]{1,0:T(8,128)(2,1)} %get-tuple-element.34.nl_hbm, s32[48]{0:T(128)S(1)} %copy-done.1), custom_call_target="tpu_custom_call" | custom-call | flops 1000000000 | bytes 8000000 | tf_op jit(solution)/shard_map/near/pallas_call | solution.py:491
  153.6 3.0 %all-to-all-done.5 = f32[32,1,1280]{2,1,0:T(1,128)S(1)} async-done(((f32[32,1,1280]{2,1,0:T(1,128)}), f32[32,1,1280]{2,1,0:T(1,128)S(1)}, u32[]{:S(2)}, u32[]{:S(2)}) %all-to-all-start.5) | async-done | bytes 163872 | tf_op jit(solution)/shard_map/all_to_all | solution.py:504
  156.5 2.8 %far_step.5 = (f32[3072,128]{1,0:T(8,128)}, f32[320,128]{1,0:T(8,128)}) custom-call(f32[320,128]{1,0:T(8,128)S(1)} %bitcast.25, bf16[1536,256]{1,0:T(8,128)(2,1)S(1)} %get-tuple-element.30.refs_1_, bf16[1536,256]{1,0:T(8,128)(2,1)S(1)} %get-tuple-element.31.refs_2_, f32[1536,256]{1,0:T(8,128)S(1)} %near.10.refs_3_, ...), custom_call_target="tpu_custom_call" | custom-call | tf_op jit(solution)/shard_map/far_step/pallas_call | solution.py:491
  159.3 2.9 %all-to-all-start.6 = ((f32[32,1,1280]{2,1,0:T(1,128)}), f32[32,1,1280]{2,1,0:T(1,128)S(1)}, u32[]{:S(2)}, u32[]{:S(2)}) async-start(f32[32,1,1280]{2,1,0:T(1,128)} %bitcast.18), calls=%async_computation.6 | async-start | bytes 327680 | tf_op jit(solution)/shard_map/all_to_all | solution.py:504
  162.2 5.7 %near.11.refs_3_ = f32[1536,256]{1,0:T(8,128)S(1)} custom-call(f32[3072,128]{1,0:T(8,128)} %get-tuple-element.48.v_hbm, f32[3072,128]{1,0:T(8,128)} %get-tuple-element.44.v_hbm.e_hbm, bf16[1536,256]{1,0:T(8,128)(2,1)} %get-tuple-element.33.nh_hbm, bf16[1536,256]{1,0:T(8,128)(2,1)} %get-tuple-element.34.nl_hbm, s32[48]{0:T(128)S(1)} %copy-done.1), custom_call_target="tpu_custom_call" | custom-call | flops 1000000000 | bytes 8000000 | tf_op jit(solution)/shard_map/near/pallas_call | solution.py:491
  167.8 3.0 %all-to-all-done.6 = f32[32,1,1280]{2,1,0:T(1,128)S(1)} async-done(((f32[32,1,1280]{2,1,0:T(1,128)}), f32[32,1,1280]{2,1,0:T(1,128)S(1)}, u32[]{:S(2)}, u32[]{:S(2)}) %all-to-all-start.6) | async-done | bytes 163872 | tf_op jit(solution)/shard_map/all_to_all | solution.py:504
  170.8 2.2 %far_last.1 = f32[153,1536]{1,0:T(8,128)} custom-call(f32[320,128]{1,0:T(8,128)S(1)} %bitcast.22, bf16[1536,256]{1,0:T(8,128)(2,1)S(1)} %get-tuple-element.30.refs_1_, bf16[1536,256]{1,0:T(8,128)(2,1)S(1)} %get-tuple-element.31.refs_2_, f32[1536,256]{1,0:T(8,128)S(1)} %near.11.refs_3_), custom_call_target="tpu_custom_call" | custom-call | tf_op jit(solution)/shard_map/far_last/pallas_call | solution.py:491
Async XLA Ops:
  36.4 7.4 %copy-start.5 = (s32[1,32,8]{1,2,0:T(8,128)S(1)}, s32[1,32,8]{1,2,0:T(8,128)}, u32[]{:S(2)}) copy-start(s32[1,32,8]{1,2,0:T(8,128)} %param.27) | copy-start | bytes 3076
  36.4 7.5 %copy-start.1 = (s32[48]{0:T(128)S(1)}, s32[48]{0:T(128)}, u32[]{:S(2)}) copy-start(s32[48]{0:T(128)} %cols.13) | copy-start | bytes 580
  36.4 7.5 %copy-start.3 = (s32[1536]{0:T(1024)S(1)}, s32[1536]{0:T(1024)}, u32[]{:S(2)}) copy-start(s32[1536]{0:T(1024)} %param.25) | copy-start | bytes 18436
  36.5 7.4 %copy-start.4 = (s32[1536]{0:T(1024)S(1)}, s32[1536]{0:T(1024)}, u32[]{:S(2)}) copy-start(s32[1536]{0:T(1024)} %param.26) | copy-start | bytes 18436
  36.5 42.2 %all-to-all-start = ((f32[32,88,128]{2,1,0:T(8,128)}), f32[32,88,128]{2,1,0:T(8,128)S(1)}, u32[]{:S(2)}, u32[]{:S(2)}) async-start(f32[32,88,128]{2,1,0:T(8,128)} %get-tuple-element.27), calls=%async_computation | async-start | bytes 2883584 | tf_op jit(solution)/shard_map/all_to_all | solution.py:504
  43.9 1.9 %copy-start = (f32[48,128,128]{2,1,0:T(8,128)S(1)}, f32[48,128,128]{2,1,0:T(8,128)}, u32[]{:S(2)}) copy-start(f32[48,128,128]{2,1,0:T(8,128)} %tiles.3) | copy-start | bytes 9437188
  45.8 32.9 %copy-start.2 = (s32[1,32,72]{2,1,0:T(8,128)S(1)}, s32[1,32,72]{2,1,0:T(8,128)}, u32[]{:S(2)}) copy-start(s32[1,32,72]{2,1,0:T(8,128)} %recv.1) | copy-start | bytes 27652
  85.7 12.3 %all-to-all-start.1 = ((f32[32,1,1280]{2,1,0:T(1,128)}), f32[32,1,1280]{2,1,0:T(1,128)S(1)}, u32[]{:S(2)}, u32[]{:S(2)}) async-start(f32[32,1,1280]{2,1,0:T(1,128)} %bitcast.8), calls=%async_computation.1 | async-start | bytes 327680 | tf_op jit(solution)/shard_map/all_to_all | solution.py:504
  100.7 11.7 %all-to-all-start.2 = ((f32[32,1,1280]{2,1,0:T(1,128)}), f32[32,1,1280]{2,1,0:T(1,128)S(1)}, u32[]{:S(2)}, u32[]{:S(2)}) async-start(f32[32,1,1280]{2,1,0:T(1,128)} %bitcast.10), calls=%async_computation.2 | async-start | bytes 327680 | tf_op jit(solution)/shard_map/all_to_all | solution.py:504
  115.2 11.5 %all-to-all-start.3 = ((f32[32,1,1280]{2,1,0:T(1,128)}), f32[32,1,1280]{2,1,0:T(1,128)S(1)}, u32[]{:S(2)}, u32[]{:S(2)}) async-start(f32[32,1,1280]{2,1,0:T(1,128)} %bitcast.12), calls=%async_computation.3 | async-start | bytes 327680 | tf_op jit(solution)/shard_map/all_to_all | solution.py:504
  130.7 11.5 %all-to-all-start.4 = ((f32[32,1,1280]{2,1,0:T(1,128)}), f32[32,1,1280]{2,1,0:T(1,128)S(1)}, u32[]{:S(2)}, u32[]{:S(2)}) async-start(f32[32,1,1280]{2,1,0:T(1,128)} %bitcast.14), calls=%async_computation.4 | async-start | bytes 327680 | tf_op jit(solution)/shard_map/all_to_all | solution.py:504
  145.0 11.5 %all-to-all-start.5 = ((f32[32,1,1280]{2,1,0:T(1,128)}), f32[32,1,1280]{2,1,0:T(1,128)S(1)}, u32[]{:S(2)}, u32[]{:S(2)}) async-start(f32[32,1,1280]{2,1,0:T(1,128)} %bitcast.16), calls=%async_computation.5 | async-start | bytes 327680 | tf_op jit(solution)/shard_map/all_to_all | solution.py:504
  159.3 11.5 %all-to-all-start.6 = ((f32[32,1,1280]{2,1,0:T(1,128)}), f32[32,1,1280]{2,1,0:T(1,128)S(1)}, u32[]{:S(2)}, u32[]{:S(2)}) async-start(f32[32,1,1280]{2,1,0:T(1,128)} %bitcast.18), calls=%async_computation.6 | async-start | bytes 327680 | tf_op jit(solution)/shard_map/all_to_all | solution.py:504

commit v6 on v5

--- a/solution.py
+++ b/solution.py
@@ -116,7 +116,7 @@
             copies[-1].start()
 
     chunk = p0.shape[0]
-    sub = 32
+    sub = 128
     lane = lanes(sub)
     one = jnp.where(lane == rest, 1.0, 0.0)
     lane8 = lanes(8)
@@ -216,17 +216,21 @@
     lax.fori_loop(0, slots, collect, 0)
     ntail = up(slots, per)
 
-    def put(p, _):
-        at = p * 2 * slots
-        out[p, 0:slots, :] = stg[pl.ds(at, slots, stride=2), :]
-        tail = stg[pl.ds(at + 1, ntail, stride=2 * per), :]
-        for q in range(1, per):
-            x = stg[pl.ds(at + 2 * q + 1, ntail, stride=2 * per), :]
-            tail = tail + pltpu.roll(x, q * rest, axis=1)
-        out[p, slots : slots + ntail, :] = tail
-        return 0
-
-    lax.fori_loop(0, peers, put, 0)
+    many = 8
+
+    def put(g, _):
+        tails = []
+        for v in range(many):
+            p = g * many + v
+            at = p * 2 * slots
+            out[p, 0:slots, :] = stg[pl.ds(at, slots, stride=2), :]
+            tails.append([stg[pl.ds(at + 2 * q + 1, ntail, stride=2 * per), :] for q in range(per)])
+        tails = [[pltpu.roll(x, q * rest, axis=1) if q else x for q, x in enumerate(t)] for t in tails]
+        for v, t in enumerate(tails):
+            out[g * many + v, slots : slots + ntail, :] = sum(t[1:], t[0])
+        return 0
+
+    lax.fori_loop(0, peers // many, put, 0)
 
 
 def pack(bnd, v2, stg, out, extra, *, peers, slots, per, rest):
@@ -262,17 +266,22 @@
     kr[:, 0:slots] = recv[0] * 2
     copies = fetch(kr, range(peers), ksr, sr)
 
-    def unpack(p, _):
-        at = p * 2 * slots
-        tail = arr[p, slots : slots + ntail, :]
-        for q in range(per):
-            x = pltpu.roll(tail, (L - q * rest) % L, axis=1) if q else tail
-            x = jnp.where(tlane < rest, x, 0.0)
-            stg[pl.ds(at + 2 * q + 1, ntail, stride=2 * per), :] = x
-        stg[pl.ds(at, slots, stride=2), :] = arr[p, 0:slots, :]
-        return 0
-
-    lax.fori_loop(0, peers, unpack, 0)
+    many = 4
+
+    def unpack(g, _):
+        tails = []
+        for v in range(many):
+            tail = arr[g * many + v, slots : slots + ntail, :]
+            tails.append([pltpu.roll(tail, (L - q * rest) % L, axis=1) if q else tail for q in range(per)])
+        for v in range(many):
+            p = g * many + v
+            at = p * 2 * slots
+            for q, x in enumerate(tails[v]):
+                stg[pl.ds(at + 2 * q + 1, ntail, stride=2 * per), :] = jnp.where(tlane < rest, x, 0.0)
+            stg[pl.ds(at, slots, stride=2), :] = arr[p, 0:slots, :]
+        return 0
+
+    lax.fori_loop(0, peers // many, unpack, 0)
 
     for c in copies:
         c.wait()

time: 174 us -> 168 us (0.966)
  Pallas kernels: 98.4 us -> 92.6 us
    pallas_call x15, Pallas kernels: 98.4 us -> 92.6 us  [call(): pl.pallas_call(kernel, out_shape=outs, in_specs=ins, out_specs=specs or j...]
  transfers between devices with their start and end apart: 7 -> 7, of which waited for: 7 -> 7; matrix products, arithmetic and copies ran while one was open for 0% -> 0% of each run, Pallas kernels for 22% -> 23%
where the time goes in v6:
time: 168 us; the launch traced here: 167 us
  Pallas kernels  92.6 us (55%)
  waiting for transfers between devices  46.2 us (28%)
  starting transfers between devices  25.6 us (15%)
  local copies, waits for them, and re-layouts  1.99 us (1%)
    pallas_call x15, Pallas kernels, call(): pl.pallas_call(kernel, out_shape=outs, in_specs=ins, out_specs=specs or j...  92.6 us
    all_to_all x7, waiting for transfers between devices, swap(): return lax.all_to_all(x, 'dom', split_axis=0, concat_axis=0, tiled=True)  46.2 us
    all_to_all x7, starting transfers between devices, swap(): return lax.all_to_all(x, 'dom', split_axis=0, concat_axis=0, tiled=True)  25.6 us
  transfers between devices with their start and end apart: 7, of which 7 were waited for; matrix products, arithmetic and copies ran while one was open for 0% of the time, Pallas kernels for 23%

profile of v6, /device:TPU:0, one launch (start us, length us, event | category | flops | bytes accessed | tf_op | source)
XLA Modules:
  0.0 167.2 jit_solution(4020398113582485893)
XLA Ops:
  0.0 32.2 %scores.1 = (f32[32,88,128]{2,1,0:T(8,128)}, f32[3072,128]{1,0:T(8,128)}) custom-call(bf16[1536,1024]{1,0:T(8,128)(2,1)} %hid_hbm.1, bf16[1224,1024]{1,0:T(8,128)(2,1)} %bitcast.29, bf16[153,1024]{1,0:T(8,128)(2,1)} %bitcast.30, f32[1,153]{1,0:T(1,128)} %bitcast.34, f32[5,8]{1,0:T(8,128)} %coef.1, s32[48,128]{1,0:T(8,128)} %bitcast.31, s32[48,128]{1,0:T(8,128)} %bitcast.32, ...), custom_call_target="tpu_custom_call" | custom-call | tf_op jit(solution)/shard_map/scores/pallas_call | solution.py:500
  32.2 0.0 copy-start.5
  32.3 0.0 copy-start.1
  32.3 0.0 copy-start.3
  32.3 0.0 copy-start.4
  32.3 7.3 %all-to-all-start = ((f32[32,88,128]{2,1,0:T(8,128)}), f32[32,88,128]{2,1,0:T(8,128)S(1)}, u32[]{:S(2)}, u32[]{:S(2)}) async-start(f32[32,88,128]{2,1,0:T(8,128)} %get-tuple-element.27), calls=%async_computation | async-start | bytes 2883584 | tf_op jit(solution)/shard_map/all_to_all | solution.py:513
  39.6 0.0 copy-done.5
  39.6 0.1 copy.17
  39.7 0.0 copy-done.1
  39.7 0.0 copy-done.3
  39.7 0.0 copy-done.4
  39.7 0.0 copy-start
  39.7 1.9 %copy-done = f32[48,128,128]{2,1,0:T(8,128)S(1)} copy-done((f32[48,128,128]{2,1,0:T(8,128)S(1)}, f32[48,128,128]{2,1,0:T(8,128)}, u32[]{:S(2)}) %copy-start) | copy-done | bytes 3145752
  41.6 0.0 copy-start.2
  41.6 3.6 %tiles.2 = (bf16[1536,256]{1,0:T(8,128)(2,1)}, bf16[1536,256]{1,0:T(8,128)(2,1)}, bf16[1536,256]{1,0:T(8,128)(2,1)S(1)}, bf16[1536,256]{1,0:T(8,128)(2,1)S(1)}, ...) custom-call(f32[48,128,128]{2,1,0:T(8,128)S(1)} %copy-done, s32[48]{0:T(128)S(1)} %copy-done.1, s32[12,128]{1,0:T(8,128)S(1)} %bitcast.27, ...), custom_call_target="tpu_custom_call" | custom-call | flops 10000000 | bytes 8000000 | tf_op jit(solution)/shard_map/tiles/pallas_call | solution.py:500
  45.2 0.6 broadcast_multiply_fusion.bnd_hbm.refs_4_
  45.8 28.6 %all-to-all-done.arr = f32[32,88,128]{2,1,0:T(8,128)S(1)} async-done(((f32[32,88,128]{2,1,0:T(8,128)}), f32[32,88,128]{2,1,0:T(8,128)S(1)}, u32[]{:S(2)}, u32[]{:S(2)}) %all-to-all-start) | async-done | bytes 1441824 | tf_op jit(solution)/shard_map/all_to_all | solution.py:513
  74.5 0.0 copy-done.2
  74.5 5.4 %errors.1 = (f32[3072,128]{1,0:T(8,128)}, f32[3072,128]{1,0:T(8,128)}, f32[320,128]{1,0:T(8,128)}) custom-call(f32[32,88,128]{2,1,0:T(8,128)S(1)} %all-to-all-done.arr, s32[1,32,72]{2,1,0:T(8,128)S(1)} %copy-done.2, s32[1,32,8]{2,1,0:T(8,128)} %broadcast_multiply_fusion.bnd_hbm.refs_4_, f32[1536,128]{1,0:T(8,128)} %get-tuple-element.28.labk_hbm), custom_call_target="tpu_custom_call" | custom-call | tf_op jit(solution)/shard_map/errors/pallas_call | solution.py:500
  79.9 3.6 %all-to-all-start.1 = ((f32[32,1,1280]{2,1,0:T(1,128)}), f32[32,1,1280]{2,1,0:T(1,128)S(1)}, u32[]{:S(2)}, u32[]{:S(2)}) async-start(f32[32,1,1280]{2,1,0:T(1,128)} %bitcast.8), calls=%async_computation.1 | async-start | bytes 327680 | tf_op jit(solution)/shard_map/all_to_all | solution.py:513
  83.6 5.8 %near.6 = (f32[1536,256]{1,0:T(8,128)S(1)}, f32[8,128]{1,0:T(8,128)S(1)}) custom-call(f32[3072,128]{1,0:T(8,128)} %get-tuple-element.32.v_hbm.e_hbm, f32[3072,128]{1,0:T(8,128)} %get-tuple-element.32.v_hbm.e_hbm, bf16[1536,256]{1,0:T(8,128)(2,1)} %get-tuple-element.33.nh_hbm, bf16[1536,256]{1,0:T(8,128)(2,1)} %get-tuple-element.34.nl_hbm, s32[48]{0:T(128)S(1)} %copy-done.1, ...), custom_call_target="tpu_custom_call" | custom-call | flops 1000000000 | bytes 8000000 | tf_op jit(solution)/shard_map/near/pallas_call | solution.py:500
  89.4 2.8 %all-to-all-done.1 = f32[32,1,1280]{2,1,0:T(1,128)S(1)} async-done(((f32[32,1,1280]{2,1,0:T(1,128)}), f32[32,1,1280]{2,1,0:T(1,128)S(1)}, u32[]{:S(2)}, u32[]{:S(2)}) %all-to-all-start.1) | async-done | bytes 163872 | tf_op jit(solution)/shard_map/all_to_all | solution.py:513
  92.2 2.8 %far_step.3 = (f32[3072,128]{1,0:T(8,128)}, f32[320,128]{1,0:T(8,128)}) custom-call(f32[320,128]{1,0:T(8,128)S(1)} %bitcast.23, bf16[1536,256]{1,0:T(8,128)(2,1)S(1)} %get-tuple-element.30.refs_1_, bf16[1536,256]{1,0:T(8,128)(2,1)S(1)} %get-tuple-element.31.refs_2_, f32[1536,256]{1,0:T(8,128)S(1)} %get-tuple-element.36.refs_3_, ...), custom_call_target="tpu_custom_call" | custom-call | tf_op jit(solution)/shard_map/far_step/pallas_call | solution.py:500
  95.0 3.0 %all-to-all-start.2 = ((f32[32,1,1280]{2,1,0:T(1,128)}), f32[32,1,1280]{2,1,0:T(1,128)S(1)}, u32[]{:S(2)}, u32[]{:S(2)}) async-start(f32[32,1,1280]{2,1,0:T(1,128)} %bitcast.10), calls=%async_computation.2 | async-start | bytes 327680 | tf_op jit(solution)/shard_map/all_to_all | solution.py:513
  98.0 5.7 %near.7.refs_3_ = f32[1536,256]{1,0:T(8,128)S(1)} custom-call(f32[3072,128]{1,0:T(8,128)} %get-tuple-element.38.v_hbm, f32[3072,128]{1,0:T(8,128)} %get-tuple-element.32.v_hbm.e_hbm, bf16[1536,256]{1,0:T(8,128)(2,1)} %get-tuple-element.33.nh_hbm, bf16[1536,256]{1,0:T(8,128)(2,1)} %get-tuple-element.34.nl_hbm, s32[48]{0:T(128)S(1)} %copy-done.1), custom_call_target="tpu_custom_call" | custom-call | flops 1000000000 | bytes 8000000 | tf_op jit(solution)/shard_map/near/pallas_call | solution.py:500
  103.7 3.0 %all-to-all-done.2 = f32[32,1,1280]{2,1,0:T(1,128)S(1)} async-done(((f32[32,1,1280]{2,1,0:T(1,128)}), f32[32,1,1280]{2,1,0:T(1,128)S(1)}, u32[]{:S(2)}, u32[]{:S(2)}) %all-to-all-start.2) | async-done | bytes 163872 | tf_op jit(solution)/shard_map/all_to_all | solution.py:513
  106.6 2.8 %far_sums.1 = (f32[3072,128]{1,0:T(8,128)}, f32[320,128]{1,0:T(8,128)}) custom-call(f32[320,128]{1,0:T(8,128)S(1)} %bitcast.24, bf16[1536,256]{1,0:T(8,128)(2,1)S(1)} %get-tuple-element.30.refs_1_, bf16[1536,256]{1,0:T(8,128)(2,1)S(1)} %get-tuple-element.31.refs_2_, f32[1536,256]{1,0:T(8,128)S(1)} %near.7.refs_3_, ...), custom_call_target="tpu_custom_call" | custom-call | tf_op jit(solution)/shard_map/far_sums/pallas_call | solution.py:500
  109.4 2.9 %all-to-all-start.3 = ((f32[32,1,1280]{2,1,0:T(1,128)}), f32[32,1,1280]{2,1,0:T(1,128)S(1)}, u32[]{:S(2)}, u32[]{:S(2)}) async-start(f32[32,1,1280]{2,1,0:T(1,128)} %bitcast.12), calls=%async_computation.3 | async-start | bytes 327680 | tf_op jit(solution)/shard_map/all_to_all | solution.py:513
  112.3 5.7 %near.8.refs_3_ = f32[1536,256]{1,0:T(8,128)S(1)} custom-call(f32[3072,128]{1,0:T(8,128)} %get-tuple-element.41.v_hbm, f32[3072,128]{1,0:T(8,128)} %get-tuple-element.32.v_hbm.e_hbm, bf16[1536,256]{1,0:T(8,128)(2,1)} %get-tuple-element.33.nh_hbm, bf16[1536,256]{1,0:T(8,128)(2,1)} %get-tuple-element.34.nl_hbm, s32[48]{0:T(128)S(1)} %copy-done.1), custom_call_target="tpu_custom_call" | custom-call | flops 1000000000 | bytes 8000000 | tf_op jit(solution)/shard_map/near/pallas_call | solution.py:500
  118.0 2.9 %all-to-all-done.3 = f32[32,1,1280]{2,1,0:T(1,128)S(1)} async-done(((f32[32,1,1280]{2,1,0:T(1,128)}), f32[32,1,1280]{2,1,0:T(1,128)S(1)}, u32[]{:S(2)}, u32[]{:S(2)}) %all-to-all-start.3) | async-done | bytes 163872 | tf_op jit(solution)/shard_map/all_to_all | solution.py:513
  120.9 4.0 %far_turn.1 = (f32[3072,128]{1,0:T(8,128)}, f32[320,128]{1,0:T(8,128)}) custom-call(f32[320,128]{1,0:T(8,128)S(1)} %bitcast.21, bf16[1536,256]{1,0:T(8,128)(2,1)S(1)} %get-tuple-element.30.refs_1_, bf16[1536,256]{1,0:T(8,128)(2,1)S(1)} %get-tuple-element.31.refs_2_, f32[1536,256]{1,0:T(8,128)S(1)} %near.8.refs_3_, ...), custom_call_target="tpu_custom_call" | custom-call | tf_op jit(solution)/shard_map/far_turn/pallas_call | solution.py:500
  124.9 2.9 %all-to-all-start.4 = ((f32[32,1,1280]{2,1,0:T(1,128)}), f32[32,1,1280]{2,1,0:T(1,128)S(1)}, u32[]{:S(2)}, u32[]{:S(2)}) async-start(f32[32,1,1280]{2,1,0:T(1,128)} %bitcast.14), calls=%async_computation.4 | async-start | bytes 327680 | tf_op jit(solution)/shard_map/all_to_all | solution.py:513
  127.8 5.7 %near.9.refs_3_ = f32[1536,256]{1,0:T(8,128)S(1)} custom-call(f32[3072,128]{1,0:T(8,128)} %get-tuple-element.44.v_hbm.e_hbm, f32[3072,128]{1,0:T(8,128)} %get-tuple-element.44.v_hbm.e_hbm, bf16[1536,256]{1,0:T(8,128)(2,1)} %get-tuple-element.33.nh_hbm, bf16[1536,256]{1,0:T(8,128)(2,1)} %get-tuple-element.34.nl_hbm, s32[48]{0:T(128)S(1)} %copy-done.1), custom_call_target="tpu_custom_call" | custom-call | flops 1000000000 | bytes 8000000 | tf_op jit(solution)/shard_map/near/pallas_call | solution.py:500
  133.5 2.9 %all-to-all-done.4 = f32[32,1,1280]{2,1,0:T(1,128)S(1)} async-done(((f32[32,1,1280]{2,1,0:T(1,128)}), f32[32,1,1280]{2,1,0:T(1,128)S(1)}, u32[]{:S(2)}, u32[]{:S(2)}) %all-to-all-start.4) | async-done | bytes 163872 | tf_op jit(solution)/shard_map/all_to_all | solution.py:513
  136.4 2.8 %far_step.4 = (f32[3072,128]{1,0:T(8,128)}, f32[320,128]{1,0:T(8,128)}) custom-call(f32[320,128]{1,0:T(8,128)S(1)} %bitcast.26, bf16[1536,256]{1,0:T(8,128)(2,1)S(1)} %get-tuple-element.30.refs_1_, bf16[1536,256]{1,0:T(8,128)(2,1)S(1)} %get-tuple-element.31.refs_2_, f32[1536,256]{1,0:T(8,128)S(1)} %near.9.refs_3_, ...), custom_call_target="tpu_custom_call" | custom-call | tf_op jit(solution)/shard_map/far_step/pallas_call | solution.py:500
  139.2 2.9 %all-to-all-start.5 = ((f32[32,1,1280]{2,1,0:T(1,128)}), f32[32,1,1280]{2,1,0:T(1,128)S(1)}, u32[]{:S(2)}, u32[]{:S(2)}) async-start(f32[32,1,1280]{2,1,0:T(1,128)} %bitcast.16), calls=%async_computation.5 | async-start | bytes 327680 | tf_op jit(solution)/shard_map/all_to_all | solution.py:513
  142.1 5.7 %near.10.refs_3_ = f32[1536,256]{1,0:T(8,128)S(1)} custom-call(f32[3072,128]{1,0:T(8,128)} %get-tuple-element.46.v_hbm, f32[3072,128]{1,0:T(8,128)} %get-tuple-element.44.v_hbm.e_hbm, bf16[1536,256]{1,0:T(8,128)(2,1)} %get-tuple-element.33.nh_hbm, bf16[1536,256]{1,0:T(8,128)(2,1)} %get-tuple-element.34.nl_hbm, s32[48]{0:T(128)S(1)} %copy-done.1), custom_call_target="tpu_custom_call" | custom-call | flops 1000000000 | bytes 8000000 | tf_op jit(solution)/shard_map/near/pallas_call | solution.py:500
  147.8 3.0 %all-to-all-done.5 = f32[32,1,1280]{2,1,0:T(1,128)S(1)} async-done(((f32[32,1,1280]{2,1,0:T(1,128)}), f32[32,1,1280]{2,1,0:T(1,128)S(1)}, u32[]{:S(2)}, u32[]{:S(2)}) %all-to-all-start.5) | async-done | bytes 163872 | tf_op jit(solution)/shard_map/all_to_all | solution.py:513
  150.7 2.8 %far_step.5 = (f32[3072,128]{1,0:T(8,128)}, f32[320,128]{1,0:T(8,128)}) custom-call(f32[320,128]{1,0:T(8,128)S(1)} %bitcast.25, bf16[1536,256]{1,0:T(8,128)(2,1)S(1)} %get-tuple-element.30.refs_1_, bf16[1536,256]{1,0:T(8,128)(2,1)S(1)} %get-tuple-element.31.refs_2_, f32[1536,256]{1,0:T(8,128)S(1)} %near.10.refs_3_, ...), custom_call_target="tpu_custom_call" | custom-call | tf_op jit(solution)/shard_map/far_step/pallas_call | solution.py:500
  153.5 2.9 %all-to-all-start.6 = ((f32[32,1,1280]{2,1,0:T(1,128)}), f32[32,1,1280]{2,1,0:T(1,128)S(1)}, u32[]{:S(2)}, u32[]{:S(2)}) async-start(f32[32,1,1280]{2,1,0:T(1,128)} %bitcast.18), calls=%async_computation.6 | async-start | bytes 327680 | tf_op jit(solution)/shard_map/all_to_all | solution.py:513
  156.4 5.7 %near.11.refs_3_ = f32[1536,256]{1,0:T(8,128)S(1)} custom-call(f32[3072,128]{1,0:T(8,128)} %get-tuple-element.48.v_hbm, f32[3072,128]{1,0:T(8,128)} %get-tuple-element.44.v_hbm.e_hbm, bf16[1536,256]{1,0:T(8,128)(2,1)} %get-tuple-element.33.nh_hbm, bf16[1536,256]{1,0:T(8,128)(2,1)} %get-tuple-element.34.nl_hbm, s32[48]{0:T(128)S(1)} %copy-done.1), custom_call_target="tpu_custom_call" | custom-call | flops 1000000000 | bytes 8000000 | tf_op jit(solution)/shard_map/near/pallas_call | solution.py:500
  162.1 3.0 %all-to-all-done.6 = f32[32,1,1280]{2,1,0:T(1,128)S(1)} async-done(((f32[32,1,1280]{2,1,0:T(1,128)}), f32[32,1,1280]{2,1,0:T(1,128)S(1)}, u32[]{:S(2)}, u32[]{:S(2)}) %all-to-all-start.6) | async-done | bytes 163872 | tf_op jit(solution)/shard_map/all_to_all | solution.py:513
  165.0 2.2 %far_last.1 = f32[153,1536]{1,0:T(8,128)} custom-call(f32[320,128]{1,0:T(8,128)S(1)} %bitcast.22, bf16[1536,256]{1,0:T(8,128)(2,1)S(1)} %get-tuple-element.30.refs_1_, bf16[1536,256]{1,0:T(8,128)(2,1)S(1)} %get-tuple-element.31.refs_2_, f32[1536,256]{1,0:T(8,128)S(1)} %near.11.refs_3_), custom_call_target="tpu_custom_call" | custom-call | tf_op jit(solution)/shard_map/far_last/pallas_call | solution.py:500
Async XLA Ops:
  32.2 7.4 %copy-start.5 = (s32[1,32,8]{1,2,0:T(8,128)S(1)}, s32[1,32,8]{1,2,0:T(8,128)}, u32[]{:S(2)}) copy-start(s32[1,32,8]{1,2,0:T(8,128)} %param.27) | copy-start | bytes 3076
  32.3 7.5 %copy-start.1 = (s32[48]{0:T(128)S(1)}, s32[48]{0:T(128)}, u32[]{:S(2)}) copy-start(s32[48]{0:T(128)} %cols.13) | copy-start | bytes 580
  32.3 7.5 %copy-start.3 = (s32[1536]{0:T(1024)S(1)}, s32[1536]{0:T(1024)}, u32[]{:S(2)}) copy-start(s32[1536]{0:T(1024)} %param.25) | copy-start | bytes 18436
  32.3 7.4 %copy-start.4 = (s32[1536]{0:T(1024)S(1)}, s32[1536]{0:T(1024)}, u32[]{:S(2)}) copy-start(s32[1536]{0:T(1024)} %param.26) | copy-start | bytes 18436
  32.3 42.2 %all-to-all-start = ((f32[32,88,128]{2,1,0:T(8,128)}), f32[32,88,128]{2,1,0:T(8,128)S(1)}, u32[]{:S(2)}, u32[]{:S(2)}) async-start(f32[32,88,128]{2,1,0:T(8,128)} %get-tuple-element.27), calls=%async_computation | async-start | bytes 2883584 | tf_op jit(solution)/shard_map/all_to_all | solution.py:513
  39.7 1.9 %copy-start = (f32[48,128,128]{2,1,0:T(8,128)S(1)}, f32[48,128,128]{2,1,0:T(8,128)}, u32[]{:S(2)}) copy-start(f32[48,128,128]{2,1,0:T(8,128)} %tiles.3) | copy-start | bytes 9437188
  41.6 32.9 %copy-start.2 = (s32[1,32,72]{2,1,0:T(8,128)S(1)}, s32[1,32,72]{2,1,0:T(8,128)}, u32[]{:S(2)}) copy-start(s32[1,32,72]{2,1,0:T(8,128)} %recv.1) | copy-start | bytes 27652
  79.9 12.3 %all-to-all-start.1 = ((f32[32,1,1280]{2,1,0:T(1,128)}), f32[32,1,1280]{2,1,0:T(1,128)S(1)}, u32[]{:S(2)}, u32[]{:S(2)}) async-start(f32[32,1,1280]{2,1,0:T(1,128)} %bitcast.8), calls=%async_computation.1 | async-start | bytes 327680 | tf_op jit(solution)/shard_map/all_to_all | solution.py:513
  95.0 11.7 %all-to-all-start.2 = ((f32[32,1,1280]{2,1,0:T(1,128)}), f32[32,1,1280]{2,1,0:T(1,128)S(1)}, u32[]{:S(2)}, u32[]{:S(2)}) async-start(f32[32,1,1280]{2,1,0:T(1,128)} %bitcast.10), calls=%async_computation.2 | async-start | bytes 327680 | tf_op jit(solution)/shard_map/all_to_all | solution.py:513
  109.4 11.5 %all-to-all-start.3 = ((f32[32,1,1280]{2,1,0:T(1,128)}), f32[32,1,1280]{2,1,0:T(1,128)S(1)}, u32[]{:S(2)}, u32[]{:S(2)}) async-start(f32[32,1,1280]{2,1,0:T(1,128)} %bitcast.12), calls=%async_computation.3 | async-start | bytes 327680 | tf_op jit(solution)/shard_map/all_to_all | solution.py:513
  124.9 11.5 %all-to-all-start.4 = ((f32[32,1,1280]{2,1,0:T(1,128)}), f32[32,1,1280]{2,1,0:T(1,128)S(1)}, u32[]{:S(2)}, u32[]{:S(2)}) async-start(f32[32,1,1280]{2,1,0:T(1,128)} %bitcast.14), calls=%async_computation.4 | async-start | bytes 327680 | tf_op jit(solution)/shard_map/all_to_all | solution.py:513
  139.2 11.5 %all-to-all-start.5 = ((f32[32,1,1280]{2,1,0:T(1,128)}), f32[32,1,1280]{2,1,0:T(1,128)S(1)}, u32[]{:S(2)}, u32[]{:S(2)}) async-start(f32[32,1,1280]{2,1,0:T(1,128)} %bitcast.16), calls=%async_computation.5 | async-start | bytes 327680 | tf_op jit(solution)/shard_map/all_to_all | solution.py:513
  153.5 11.5 %all-to-all-start.6 = ((f32[32,1,1280]{2,1,0:T(1,128)}), f32[32,1,1280]{2,1,0:T(1,128)S(1)}, u32[]{:S(2)}, u32[]{:S(2)}) async-start(f32[32,1,1280]{2,1,0:T(1,128)} %bitcast.18), calls=%async_computation.6 | async-start | bytes 327680 | tf_op jit(solution)/shard_map/all_to_all | solution.py:513

commit v7 on v6

--- a/solution.py
+++ b/solution.py
@@ -70,7 +70,7 @@
 
 def scores_kernel(
     hid_hbm, bt, st, bias, coef, es, ed, er, send, out, blank,
-    hid, pt, p0, m2, s0, s1, s2, s3, sc2, stg, kj, kd, kp, zero, sj, sd, sp, sz, *ks, classes, slots, per,
+    hid, pt, p0, p1, m2, s0, s1, s2, s3, sc2, stg, kj, kd, kp, zero, sj, sd, sp, sz, *ks, classes, slots, per,
 ):
     n, hdim = hid.shape
     hload = pltpu.make_async_copy(hid_hbm, hid, sz.at[1 + 4 * coef.shape[0]])
@@ -130,19 +130,20 @@
     bias0 = bias[0:1, 0:L]
     bias1 = jnp.concatenate([bias[0:1, L:classes], jnp.zeros((1, L - rest), F32)], 1)
 
-    def project(i, _):
-        row0 = pl.multiple_of(i * chunk, chunk)
-        h = hid[pl.ds(row0, chunk), :]
+    def project(i, dst):
+        h = hid[pl.ds(pl.multiple_of(i * chunk, chunk), chunk), :]
         for j in range(0, base_s + 2 * L, 2 * L):
-            p0[:, j : j + 2 * L] = lax.dot_general(
+            dst[:, j : j + 2 * L] = lax.dot_general(
                 h, pt[j : j + 2 * L, :], (((1,), (1,)), ((), ())), preferred_element_type=F32
             )
-
-        def mix(u, _):
-            rows = pl.ds(pl.multiple_of(u * sub, sub), sub)
-            row = row0 + u * sub
-            mains = [p0[rows, b * L : (b + 1) * L] for b in range(nb)]
-            q = [p0[rows, base_r + h * L : base_r + (h + 1) * L] for h in range(2)]
+            yield
+
+    def mix(i, src):
+        for u in range(0, chunk, sub):
+            rows = slice(u, u + sub)
+            row = i * chunk + u
+            mains = [src[rows, b * L : (b + 1) * L] for b in range(nb)]
+            q = [src[rows, base_r + h * L : base_r + (h + 1) * L] for h in range(2)]
             for r in range(nrel):
                 x = coef[r, 0] * mains[0]
                 for b in range(1, nb):
@@ -155,17 +156,31 @@
                 at = 2 * (r * n + row)
                 m2[pl.ds(at, sub, stride=2), :] = x
                 m2[pl.ds(at + 1, sub, stride=2), :] = jnp.where(lane < rest, t, one)
+                yield
             at = 2 * row
-            sc2[pl.ds(at, sub, stride=2), :] = p0[rows, base_s : base_s + L] + bias0
-            sc2[pl.ds(at + 1, sub, stride=2), :] = p0[rows, base_s + L : base_s + 2 * L] + bias1
-            return 0
-
-        lax.fori_loop(0, chunk // sub, mix, 0)
-        return 0
+            sc2[pl.ds(at, sub, stride=2), :] = src[rows, base_s : base_s + L] + bias0
+            sc2[pl.ds(at + 1, sub, stride=2), :] = src[rows, base_s + L : base_s + 2 * L] + bias1
+
+    def weave(*works):
+        works = list(works)
+        while works:
+            for w in list(works):
+                if next(w, 0) == 0:
+                    works.remove(w)
 
     sc2[pl.ds(2 * n, 16), :] = jnp.zeros((16, L), F32)
+    count = n // chunk
     hload.wait()
-    lax.fori_loop(0, n // chunk, project, 0)
+    weave(project(0, p0))
+
+    def pipe(t, _):
+        weave(mix(2 * t, p0), project(2 * t + 1, p1))
+        weave(mix(2 * t + 1, p1), project(2 * t + 2, p0))
+        return 0
+
+    lax.fori_loop(0, count // 2 - 1, pipe, 0)
+    weave(mix(count - 2, p0), project(count - 1, p1))
+    weave(mix(count - 1, p1))
 
     def clear(i, _):
         s3[pl.ds(pl.multiple_of(i * 512, 512), 512), :] = jnp.zeros((512, L), F32)
@@ -547,7 +562,7 @@
         (hidden, bases.T, self_weight.T, bias.reshape(1, -1), coef)
         + (square(edge_src), square(edge_dst), square(edge_rel), send_rows),
         [pltpu.VMEM((n, hdim), BF16), pltpu.VMEM((wide, hdim), BF16)]
-        + [pltpu.VMEM((n // 2, wide), F32)]
+        + [pltpu.VMEM((n // 4, wide), F32)] * 2
         + [sums] * 5
         + [rows2, stage]
         + [pltpu.VMEM((erows, L), jnp.int32)] * 2

time: 168 us -> 165 us (0.982)
  Pallas kernels: 92.6 us -> 90.1 us
    pallas_call x15, Pallas kernels: 92.6 us -> 90.1 us  [call(): pl.pallas_call(kernel, out_shape=outs, in_specs=ins, out_specs=specs or j...]
where the time goes in v7:
time: 165 us
  Pallas kernels  90.1 us (55%)
  waiting for transfers between devices  46.1 us (28%)
  starting transfers between devices  25.8 us (16%)
  local copies, waits for them, and re-layouts  1.99 us (1%)
    pallas_call x15, Pallas kernels, call(): pl.pallas_call(kernel, out_shape=outs, in_specs=ins, out_specs=specs or j...  90.1 us
    all_to_all x7, waiting for transfers between devices, swap(): return lax.all_to_all(x, 'dom', split_axis=0, concat_axis=0, tiled=True)  46.1 us
    all_to_all x7, starting transfers between devices, swap(): return lax.all_to_all(x, 'dom', split_axis=0, concat_axis=0, tiled=True)  25.8 us
  transfers between devices with their start and end apart: 7, of which 7 were waited for; matrix products, arithmetic and copies ran while one was open for 0% of the time, Pallas kernels for 23%

profile of v7, /device:TPU:0, one launch (start us, length us, event | category | flops | bytes accessed | tf_op | source)
XLA Modules:
  0.0 164.7 jit_solution(4652730161762990629)
XLA Ops:
  0.0 29.8 %scores.1 = (f32[32,88,128]{2,1,0:T(8,128)}, f32[3072,128]{1,0:T(8,128)}) custom-call(bf16[1536,1024]{1,0:T(8,128)(2,1)} %hid_hbm.1, bf16[1224,1024]{1,0:T(8,128)(2,1)} %bitcast.29, bf16[153,1024]{1,0:T(8,128)(2,1)} %bitcast.30, f32[1,153]{1,0:T(1,128)} %bitcast.34, f32[5,8]{1,0:T(8,128)} %coef.1, s32[48,128]{1,0:T(8,128)} %bitcast.31, s32[48,128]{1,0:T(8,128)} %bitcast.32, ...), custom_call_target="tpu_custom_call" | custom-call | tf_op jit(solution)/shard_map/scores/pallas_call | solution.py:515
  29.8 0.0 copy-start.5
  29.8 0.0 copy-start.1
  29.8 0.0 copy-start.3
  29.8 0.0 copy-start.4
  29.8 7.3 %all-to-all-start = ((f32[32,88,128]{2,1,0:T(8,128)}), f32[32,88,128]{2,1,0:T(8,128)S(1)}, u32[]{:S(2)}, u32[]{:S(2)}) async-start(f32[32,88,128]{2,1,0:T(8,128)} %get-tuple-element.27), calls=%async_computation | async-start | bytes 2883584 | tf_op jit(solution)/shard_map/all_to_all | solution.py:528
  37.2 0.0 copy-done.5
  37.2 0.1 copy.17
  37.2 0.0 copy-done.1
  37.3 0.0 copy-done.3
  37.3 0.0 copy-done.4
  37.3 0.0 copy-start
  37.3 1.9 %copy-done = f32[48,128,128]{2,1,0:T(8,128)S(1)} copy-done((f32[48,128,128]{2,1,0:T(8,128)S(1)}, f32[48,128,128]{2,1,0:T(8,128)}, u32[]{:S(2)}) %copy-start) | copy-done | bytes 3145752
  39.2 0.0 copy-start.2
  39.2 3.6 %tiles.2 = (bf16[1536,256]{1,0:T(8,128)(2,1)}, bf16[1536,256]{1,0:T(8,128)(2,1)}, bf16[1536,256]{1,0:T(8,128)(2,1)S(1)}, bf16[1536,256]{1,0:T(8,128)(2,1)S(1)}, ...) custom-call(f32[48,128,128]{2,1,0:T(8,128)S(1)} %copy-done, s32[48]{0:T(128)S(1)} %copy-done.1, s32[12,128]{1,0:T(8,128)S(1)} %bitcast.27, ...), custom_call_target="tpu_custom_call" | custom-call | flops 10000000 | bytes 8000000 | tf_op jit(solution)/shard_map/tiles/pallas_call | solution.py:515
  42.8 0.6 broadcast_multiply_fusion.bnd_hbm.refs_4_
  43.4 28.6 %all-to-all-done.arr = f32[32,88,128]{2,1,0:T(8,128)S(1)} async-done(((f32[32,88,128]{2,1,0:T(8,128)}), f32[32,88,128]{2,1,0:T(8,128)S(1)}, u32[]{:S(2)}, u32[]{:S(2)}) %all-to-all-start) | async-done | bytes 1441824 | tf_op jit(solution)/shard_map/all_to_all | solution.py:528
  72.0 0.0 copy-done.2
  72.0 5.4 %errors.1 = (f32[3072,128]{1,0:T(8,128)}, f32[3072,128]{1,0:T(8,128)}, f32[320,128]{1,0:T(8,128)}) custom-call(f32[32,88,128]{2,1,0:T(8,128)S(1)} %all-to-all-done.arr, s32[1,32,72]{2,1,0:T(8,128)S(1)} %copy-done.2, s32[1,32,8]{2,1,0:T(8,128)} %broadcast_multiply_fusion.bnd_hbm.refs_4_, f32[1536,128]{1,0:T(8,128)} %get-tuple-element.28.labk_hbm), custom_call_target="tpu_custom_call" | custom-call | tf_op jit(solution)/shard_map/errors/pallas_call | solution.py:515
  77.5 3.6 %all-to-all-start.1 = ((f32[32,1,1280]{2,1,0:T(1,128)}), f32[32,1,1280]{2,1,0:T(1,128)S(1)}, u32[]{:S(2)}, u32[]{:S(2)}) async-start(f32[32,1,1280]{2,1,0:T(1,128)} %bitcast.8), calls=%async_computation.1 | async-start | bytes 327680 | tf_op jit(solution)/shard_map/all_to_all | solution.py:528
  81.1 5.8 %near.6 = (f32[1536,256]{1,0:T(8,128)S(1)}, f32[8,128]{1,0:T(8,128)S(1)}) custom-call(f32[3072,128]{1,0:T(8,128)} %get-tuple-element.32.v_hbm.e_hbm, f32[3072,128]{1,0:T(8,128)} %get-tuple-element.32.v_hbm.e_hbm, bf16[1536,256]{1,0:T(8,128)(2,1)} %get-tuple-element.33.nh_hbm, bf16[1536,256]{1,0:T(8,128)(2,1)} %get-tuple-element.34.nl_hbm, s32[48]{0:T(128)S(1)} %copy-done.1, ...), custom_call_target="tpu_custom_call" | custom-call | flops 1000000000 | bytes 8000000 | tf_op jit(solution)/shard_map/near/pallas_call | solution.py:515
  86.9 2.8 %all-to-all-done.1 = f32[32,1,1280]{2,1,0:T(1,128)S(1)} async-done(((f32[32,1,1280]{2,1,0:T(1,128)}), f32[32,1,1280]{2,1,0:T(1,128)S(1)}, u32[]{:S(2)}, u32[]{:S(2)}) %all-to-all-start.1) | async-done | bytes 163872 | tf_op jit(solution)/shard_map/all_to_all | solution.py:528
  89.7 2.8 %far_step.3 = (f32[3072,128]{1,0:T(8,128)}, f32[320,128]{1,0:T(8,128)}) custom-call(f32[320,128]{1,0:T(8,128)S(1)} %bitcast.23, bf16[1536,256]{1,0:T(8,128)(2,1)S(1)} %get-tuple-element.30.refs_1_, bf16[1536,256]{1,0:T(8,128)(2,1)S(1)} %get-tuple-element.31.refs_2_, f32[1536,256]{1,0:T(8,128)S(1)} %get-tuple-element.36.refs_3_, ...), custom_call_target="tpu_custom_call" | custom-call | tf_op jit(solution)/shard_map/far_step/pallas_call | solution.py:515
  92.5 3.0 %all-to-all-start.2 = ((f32[32,1,1280]{2,1,0:T(1,128)}), f32[32,1,1280]{2,1,0:T(1,128)S(1)}, u32[]{:S(2)}, u32[]{:S(2)}) async-start(f32[32,1,1280]{2,1,0:T(1,128)} %bitcast.10), calls=%async_computation.2 | async-start | bytes 327680 | tf_op jit(solution)/shard_map/all_to_all | solution.py:528
  95.5 5.7 %near.7.refs_3_ = f32[1536,256]{1,0:T(8,128)S(1)} custom-call(f32[3072,128]{1,0:T(8,128)} %get-tuple-element.38.v_hbm, f32[3072,128]{1,0:T(8,128)} %get-tuple-element.32.v_hbm.e_hbm, bf16[1536,256]{1,0:T(8,128)(2,1)} %get-tuple-element.33.nh_hbm, bf16[1536,256]{1,0:T(8,128)(2,1)} %get-tuple-element.34.nl_hbm, s32[48]{0:T(128)S(1)} %copy-done.1), custom_call_target="tpu_custom_call" | custom-call | flops 1000000000 | bytes 8000000 | tf_op jit(solution)/shard_map/near/pallas_call | solution.py:515
  101.2 3.0 %all-to-all-done.2 = f32[32,1,1280]{2,1,0:T(1,128)S(1)} async-done(((f32[32,1,1280]{2,1,0:T(1,128)}), f32[32,1,1280]{2,1,0:T(1,128)S(1)}, u32[]{:S(2)}, u32[]{:S(2)}) %all-to-all-start.2) | async-done | bytes 163872 | tf_op jit(solution)/shard_map/all_to_all | solution.py:528
  104.1 2.8 %far_sums.1 = (f32[3072,128]{1,0:T(8,128)}, f32[320,128]{1,0:T(8,128)}) custom-call(f32[320,128]{1,0:T(8,128)S(1)} %bitcast.24, bf16[1536,256]{1,0:T(8,128)(2,1)S(1)} %get-tuple-element.30.refs_1_, bf16[1536,256]{1,0:T(8,128)(2,1)S(1)} %get-tuple-element.31.refs_2_, f32[1536,256]{1,0:T(8,128)S(1)} %near.7.refs_3_, ...), custom_call_target="tpu_custom_call" | custom-call | tf_op jit(solution)/shard_map/far_sums/pallas_call | solution.py:515
  106.9 3.1 %all-to-all-start.3 = ((f32[32,1,1280]{2,1,0:T(1,128)}), f32[32,1,1280]{2,1,0:T(1,128)S(1)}, u32[]{:S(2)}, u32[]{:S(2)}) async-start(f32[32,1,1280]{2,1,0:T(1,128)} %bitcast.12), calls=%async_computation.3 | async-start | bytes 327680 | tf_op jit(solution)/shard_map/all_to_all | solution.py:528
  110.0 5.7 %near.8.refs_3_ = f32[1536,256]{1,0:T(8,128)S(1)} custom-call(f32[3072,128]{1,0:T(8,128)} %get-tuple-element.41.v_hbm, f32[3072,128]{1,0:T(8,128)} %get-tuple-element.32.v_hbm.e_hbm, bf16[1536,256]{1,0:T(8,128)(2,1)} %get-tuple-element.33.nh_hbm, bf16[1536,256]{1,0:T(8,128)(2,1)} %get-tuple-element.34.nl_hbm, s32[48]{0:T(128)S(1)} %copy-done.1), custom_call_target="tpu_custom_call" | custom-call | flops 1000000000 | bytes 8000000 | tf_op jit(solution)/shard_map/near/pallas_call | solution.py:515
  115.7 2.8 %all-to-all-done.3 = f32[32,1,1280]{2,1,0:T(1,128)S(1)} async-done(((f32[32,1,1280]{2,1,0:T(1,128)}), f32[32,1,1280]{2,1,0:T(1,128)S(1)}, u32[]{:S(2)}, u32[]{:S(2)}) %all-to-all-start.3) | async-done | bytes 163872 | tf_op jit(solution)/shard_map/all_to_all | solution.py:528
  118.5 4.0 %far_turn.1 = (f32[3072,128]{1,0:T(8,128)}, f32[320,128]{1,0:T(8,128)}) custom-call(f32[320,128]{1,0:T(8,128)S(1)} %bitcast.21, bf16[1536,256]{1,0:T(8,128)(2,1)S(1)} %get-tuple-element.30.refs_1_, bf16[1536,256]{1,0:T(8,128)(2,1)S(1)} %get-tuple-element.31.refs_2_, f32[1536,256]{1,0:T(8,128)S(1)} %near.8.refs_3_, ...), custom_call_target="tpu_custom_call" | custom-call | tf_op jit(solution)/shard_map/far_turn/pallas_call | solution.py:515
  122.4 2.9 %all-to-all-start.4 = ((f32[32,1,1280]{2,1,0:T(1,128)}), f32[32,1,1280]{2,1,0:T(1,128)S(1)}, u32[]{:S(2)}, u32[]{:S(2)}) async-start(f32[32,1,1280]{2,1,0:T(1,128)} %bitcast.14), calls=%async_computation.4 | async-start | bytes 327680 | tf_op jit(solution)/shard_map/all_to_all | solution.py:528
  125.3 5.7 %near.9.refs_3_ = f32[1536,256]{1,0:T(8,128)S(1)} custom-call(f32[3072,128]{1,0:T(8,128)} %get-tuple-element.44.v_hbm.e_hbm, f32[3072,128]{1,0:T(8,128)} %get-tuple-element.44.v_hbm.e_hbm, bf16[1536,256]{1,0:T(8,128)(2,1)} %get-tuple-element.33.nh_hbm, bf16[1536,256]{1,0:T(8,128)(2,1)} %get-tuple-element.34.nl_hbm, s32[48]{0:T(128)S(1)} %copy-done.1), custom_call_target="tpu_custom_call" | custom-call | flops 1000000000 | bytes 8000000 | tf_op jit(solution)/shard_map/near/pallas_call | solution.py:515
  131.0 2.9 %all-to-all-done.4 = f32[32,1,1280]{2,1,0:T(1,128)S(1)} async-done(((f32[32,1,1280]{2,1,0:T(1,128)}), f32[32,1,1280]{2,1,0:T(1,128)S(1)}, u32[]{:S(2)}, u32[]{:S(2)}) %all-to-all-start.4) | async-done | bytes 163872 | tf_op jit(solution)/shard_map/all_to_all | solution.py:528
  134.0 2.8 %far_step.4 = (f32[3072,128]{1,0:T(8,128)}, f32[320,128]{1,0:T(8,128)}) custom-call(f32[320,128]{1,0:T(8,128)S(1)} %bitcast.26, bf16[1536,256]{1,0:T(8,128)(2,1)S(1)} %get-tuple-element.30.refs_1_, bf16[1536,256]{1,0:T(8,128)(2,1)S(1)} %get-tuple-element.31.refs_2_, f32[1536,256]{1,0:T(8,128)S(1)} %near.9.refs_3_, ...), custom_call_target="tpu_custom_call" | custom-call | tf_op jit(solution)/shard_map/far_step/pallas_call | solution.py:515
  136.7 2.9 %all-to-all-start.5 = ((f32[32,1,1280]{2,1,0:T(1,128)}), f32[32,1,1280]{2,1,0:T(1,128)S(1)}, u32[]{:S(2)}, u32[]{:S(2)}) async-start(f32[32,1,1280]{2,1,0:T(1,128)} %bitcast.16), calls=%async_computation.5 | async-start | bytes 327680 | tf_op jit(solution)/shard_map/all_to_all | solution.py:528
  139.6 5.7 %near.10.refs_3_ = f32[1536,256]{1,0:T(8,128)S(1)} custom-call(f32[3072,128]{1,0:T(8,128)} %get-tuple-element.46.v_hbm, f32[3072,128]{1,0:T(8,128)} %get-tuple-element.44.v_hbm.e_hbm, bf16[1536,256]{1,0:T(8,128)(2,1)} %get-tuple-element.33.nh_hbm, bf16[1536,256]{1,0:T(8,128)(2,1)} %get-tuple-element.34.nl_hbm, s32[48]{0:T(128)S(1)} %copy-done.1), custom_call_target="tpu_custom_call" | custom-call | flops 1000000000 | bytes 8000000 | tf_op jit(solution)/shard_map/near/pallas_call | solution.py:515
  145.3 3.0 %all-to-all-done.5 = f32[32,1,1280]{2,1,0:T(1,128)S(1)} async-done(((f32[32,1,1280]{2,1,0:T(1,128)}), f32[32,1,1280]{2,1,0:T(1,128)S(1)}, u32[]{:S(2)}, u32[]{:S(2)}) %all-to-all-start.5) | async-done | bytes 163872 | tf_op jit(solution)/shard_map/all_to_all | solution.py:528
  148.3 2.8 %far_step.5 = (f32[3072,128]{1,0:T(8,128)}, f32[320,128]{1,0:T(8,128)}) custom-call(f32[320,128]{1,0:T(8,128)S(1)} %bitcast.25, bf16[1536,256]{1,0:T(8,128)(2,1)S(1)} %get-tuple-element.30.refs_1_, bf16[1536,256]{1,0:T(8,128)(2,1)S(1)} %get-tuple-element.31.refs_2_, f32[1536,256]{1,0:T(8,128)S(1)} %near.10.refs_3_, ...), custom_call_target="tpu_custom_call" | custom-call | tf_op jit(solution)/shard_map/far_step/pallas_call | solution.py:515
  151.0 2.9 %all-to-all-start.6 = ((f32[32,1,1280]{2,1,0:T(1,128)}), f32[32,1,1280]{2,1,0:T(1,128)S(1)}, u32[]{:S(2)}, u32[]{:S(2)}) async-start(f32[32,1,1280]{2,1,0:T(1,128)} %bitcast.18), calls=%async_computation.6 | async-start | bytes 327680 | tf_op jit(solution)/shard_map/all_to_all | solution.py:528
  153.9 5.7 %near.11.refs_3_ = f32[1536,256]{1,0:T(8,128)S(1)} custom-call(f32[3072,128]{1,0:T(8,128)} %get-tuple-element.48.v_hbm, f32[3072,128]{1,0:T(8,128)} %get-tuple-element.44.v_hbm.e_hbm, bf16[1536,256]{1,0:T(8,128)(2,1)} %get-tuple-element.33.nh_hbm, bf16[1536,256]{1,0:T(8,128)(2,1)} %get-tuple-element.34.nl_hbm, s32[48]{0:T(128)S(1)} %copy-done.1), custom_call_target="tpu_custom_call" | custom-call | flops 1000000000 | bytes 8000000 | tf_op jit(solution)/shard_map/near/pallas_call | solution.py:515
  159.6 3.0 %all-to-all-done.6 = f32[32,1,1280]{2,1,0:T(1,128)S(1)} async-done(((f32[32,1,1280]{2,1,0:T(1,128)}), f32[32,1,1280]{2,1,0:T(1,128)S(1)}, u32[]{:S(2)}, u32[]{:S(2)}) %all-to-all-start.6) | async-done | bytes 163872 | tf_op jit(solution)/shard_map/all_to_all | solution.py:528
  162.6 2.2 %far_last.1 = f32[153,1536]{1,0:T(8,128)} custom-call(f32[320,128]{1,0:T(8,128)S(1)} %bitcast.22, bf16[1536,256]{1,0:T(8,128)(2,1)S(1)} %get-tuple-element.30.refs_1_, bf16[1536,256]{1,0:T(8,128)(2,1)S(1)} %get-tuple-element.31.refs_2_, f32[1536,256]{1,0:T(8,128)S(1)} %near.11.refs_3_), custom_call_target="tpu_custom_call" | custom-call | tf_op jit(solution)/shard_map/far_last/pallas_call | solution.py:515
Async XLA Ops:
  29.8 7.4 %copy-start.5 = (s32[1,32,8]{1,2,0:T(8,128)S(1)}, s32[1,32,8]{1,2,0:T(8,128)}, u32[]{:S(2)}) copy-start(s32[1,32,8]{1,2,0:T(8,128)} %param.27) | copy-start | bytes 3076
  29.8 7.5 %copy-start.1 = (s32[48]{0:T(128)S(1)}, s32[48]{0:T(128)}, u32[]{:S(2)}) copy-start(s32[48]{0:T(128)} %cols.13) | copy-start | bytes 580
  29.8 7.5 %copy-start.3 = (s32[1536]{0:T(1024)S(1)}, s32[1536]{0:T(1024)}, u32[]{:S(2)}) copy-start(s32[1536]{0:T(1024)} %param.25) | copy-start | bytes 18436
  29.8 7.4 %copy-start.4 = (s32[1536]{0:T(1024)S(1)}, s32[1536]{0:T(1024)}, u32[]{:S(2)}) copy-start(s32[1536]{0:T(1024)} %param.26) | copy-start | bytes 18436
  29.8 42.2 %all-to-all-start = ((f32[32,88,128]{2,1,0:T(8,128)}), f32[32,88,128]{2,1,0:T(8,128)S(1)}, u32[]{:S(2)}, u32[]{:S(2)}) async-start(f32[32,88,128]{2,1,0:T(8,128)} %get-tuple-element.27), calls=%async_computation | async-start | bytes 2883584 | tf_op jit(solution)/shard_map/all_to_all | solution.py:528
  37.3 1.9 %copy-start = (f32[48,128,128]{2,1,0:T(8,128)S(1)}, f32[48,128,128]{2,1,0:T(8,128)}, u32[]{:S(2)}) copy-start(f32[48,128,128]{2,1,0:T(8,128)} %tiles.3) | copy-start | bytes 9437188
  39.2 32.9 %copy-start.2 = (s32[1,32,72]{2,1,0:T(8,128)S(1)}, s32[1,32,72]{2,1,0:T(8,128)}, u32[]{:S(2)}) copy-start(s32[1,32,72]{2,1,0:T(8,128)} %recv.1) | copy-start | bytes 27652
  77.5 12.3 %all-to-all-start.1 = ((f32[32,1,1280]{2,1,0:T(1,128)}), f32[32,1,1280]{2,1,0:T(1,128)S(1)}, u32[]{:S(2)}, u32[]{:S(2)}) async-start(f32[32,1,1280]{2,1,0:T(1,128)} %bitcast.8), calls=%async_computation.1 | async-start | bytes 327680 | tf_op jit(solution)/shard_map/all_to_all | solution.py:528
  92.5 11.6 %all-to-all-start.2 = ((f32[32,1,1280]{2,1,0:T(1,128)}), f32[32,1,1280]{2,1,0:T(1,128)S(1)}, u32[]{:S(2)}, u32[]{:S(2)}) async-start(f32[32,1,1280]{2,1,0:T(1,128)} %bitcast.10), calls=%async_computation.2 | async-start | bytes 327680 | tf_op jit(solution)/shard_map/all_to_all | solution.py:528
  106.9 11.5 %all-to-all-start.3 = ((f32[32,1,1280]{2,1,0:T(1,128)}), f32[32,1,1280]{2,1,0:T(1,128)S(1)}, u32[]{:S(2)}, u32[]{:S(2)}) async-start(f32[32,1,1280]{2,1,0:T(1,128)} %bitcast.12), calls=%async_computation.3 | async-start | bytes 327680 | tf_op jit(solution)/shard_map/all_to_all | solution.py:528
  122.4 11.5 %all-to-all-start.4 = ((f32[32,1,1280]{2,1,0:T(1,128)}), f32[32,1,1280]{2,1,0:T(1,128)S(1)}, u32[]{:S(2)}, u32[]{:S(2)}) async-start(f32[32,1,1280]{2,1,0:T(1,128)} %bitcast.14), calls=%async_computation.4 | async-start | bytes 327680 | tf_op jit(solution)/shard_map/all_to_all | solution.py:528
  136.7 11.5 %all-to-all-start.5 = ((f32[32,1,1280]{2,1,0:T(1,128)}), f32[32,1,1280]{2,1,0:T(1,128)S(1)}, u32[]{:S(2)}, u32[]{:S(2)}) async-start(f32[32,1,1280]{2,1,0:T(1,128)} %bitcast.16), calls=%async_computation.5 | async-start | bytes 327680 | tf_op jit(solution)/shard_map/all_to_all | solution.py:528
  151.0 11.5 %all-to-all-start.6 = ((f32[32,1,1280]{2,1,0:T(1,128)}), f32[32,1,1280]{2,1,0:T(1,128)S(1)}, u32[]{:S(2)}, u32[]{:S(2)}) async-start(f32[32,1,1280]{2,1,0:T(1,128)} %bitcast.18), calls=%async_computation.6 | async-start | bytes 327680 | tf_op jit(solution)/shard_map/all_to_all | solution.py:528

commit v8 on v7

--- a/solution.py
+++ b/solution.py
@@ -143,6 +143,7 @@
             rows = slice(u, u + sub)
             row = i * chunk + u
             mains = [src[rows, b * L : (b + 1) * L] for b in range(nb)]
+            size = 2 * sub
             q = [src[rows, base_r + h * L : base_r + (h + 1) * L] for h in range(2)]
             for r in range(nrel):
                 x = coef[r, 0] * mains[0]
@@ -156,6 +157,7 @@
                 at = 2 * (r * n + row)
                 m2[pl.ds(at, sub, stride=2), :] = x
                 m2[pl.ds(at + 1, sub, stride=2), :] = jnp.where(lane < rest, t, one)
+                s3[pl.ds(pl.multiple_of(2 * nrel * row + r * size, size), size), :] = jnp.zeros((size, L), F32)
                 yield
             at = 2 * row
             sc2[pl.ds(at, sub, stride=2), :] = src[rows, base_s : base_s + L] + bias0
@@ -182,11 +184,6 @@
     weave(mix(count - 2, p0), project(count - 1, p1))
     weave(mix(count - 1, p1))
 
-    def clear(i, _):
-        s3[pl.ds(pl.multiple_of(i * 512, 512), 512), :] = jnp.zeros((512, L), F32)
-        return 0
-
-    lax.fori_loop(0, s3.shape[0] // 512, clear, 0)
     for c in copies:
         c.wait()
 
@@ -222,13 +219,14 @@
 
     lax.fori_loop(0, n // fin, finish, 0)
 
-    def collect(k, _):
-        for p in range(peers):
-            at = pl.ds(pl.multiple_of(ksp[p][0, k], 2), 2)
-            pair(stg, p * slots + k)[...] = sc2[at, :]
-        return 0
-
-    lax.fori_loop(0, slots, collect, 0)
+    def collect(t, _):
+        for k in (2 * t, 2 * t + 1):
+            for p in range(peers):
+                at = pl.ds(pl.multiple_of(ksp[p][0, k], 2), 2)
+                pair(stg, p * slots + k)[...] = sc2[at, :]
+        return 0
+
+    lax.fori_loop(0, slots // 2, collect, 0)
     ntail = up(slots, per)
 
     many = 8
@@ -281,7 +279,7 @@
     kr[:, 0:slots] = recv[0] * 2
     copies = fetch(kr, range(peers), ksr, sr)
 
-    many = 4
+    many = 8
 
     def unpack(g, _):
         tails = []
@@ -465,8 +463,11 @@
     lane = lanes(chunk)
     count = n // chunk
 
+    parts = 6
+    small = chunk // parts
+
     def piece(i):
-        rows = pl.ds(pl.multiple_of(2 * i * chunk, 2 * chunk), 2 * chunk)
+        rows = pl.ds(pl.multiple_of(2 * i * small, 2 * small), 2 * small)
         return pltpu.make_async_copy(v2.at[rows, :], v_hbm.at[rows, :], vsem.at[i])
 
     if mode != "last":
@@ -489,21 +490,23 @@
             pltpu.make_async_copy(t_hbm.at[hit, :], t2.at[hit, :], sems.at[i]).wait()
             free = t2[pl.ds(2 * row + 1, chunk, stride=2), :]
             scale = free[:, L - 1 : L] * sigma / mag
-        for h in range(2):
-            x = v[:, h * L : (h + 1) * L]
-            rows2 = pl.ds(2 * row + h, chunk, stride=2)
-            if mode == "turn":
-                x = t2[rows2, :] + scale * x
-                x = jnp.where(lane < rest, x, 0.0) if h else x
-            v2[rows2, :] = x
-        piece(i).start()
+        for w in range(parts):
+            own = slice(w * small, (w + 1) * small)
+            for h in range(2):
+                x = v[own, h * L : (h + 1) * L]
+                rows2 = pl.ds(2 * (row + w * small) + h, small, stride=2)
+                if mode == "turn":
+                    x = t2[rows2, :] + scale[own] * x
+                    x = jnp.where(lane[own] < rest, x, 0.0) if h else x
+                v2[rows2, :] = x
+            piece(i * parts + w).start()
         return 0
 
     lax.fori_loop(0, count, body, 0)
     if mode != "last":
         extra = tot[0:1, :] if mode == "sums" else None
         pack((bcopy, bnd), v2, stgb, out, extra, peers=peers, slots=slots, per=per, rest=rest)
-        for i in range(count):
+        for i in range(count * parts):
             piece(i).wait()
 
 

time: 165 us -> 164 us (level)
  no operation moved by 1% of the time
where the time goes in v8:
time: 164 us
  Pallas kernels  89 us (54%)
  waiting for transfers between devices  46 us (28%)
  starting transfers between devices  25.8 us (16%)
  local copies, waits for them, and re-layouts  1.99 us (1%)
    pallas_call x15, Pallas kernels, call(): pl.pallas_call(kernel, out_shape=outs, in_specs=ins, out_specs=specs or j...  89 us
    all_to_all x7, waiting for transfers between devices, swap(): return lax.all_to_all(x, 'dom', split_axis=0, concat_axis=0, tiled=True)  46 us
    all_to_all x7, starting transfers between devices, swap(): return lax.all_to_all(x, 'dom', split_axis=0, concat_axis=0, tiled=True)  25.8 us
  transfers between devices with their start and end apart: 7, of which 7 were waited for; matrix products, arithmetic and copies ran while one was open for 0% of the time, Pallas kernels for 23%

profile of v8, /device:TPU:0, one launch (start us, length us, event | category | flops | bytes accessed | tf_op | source)
XLA Modules:
  0.0 163.6 jit_solution(3225319222750419545)
XLA Ops:
  0.0 29.5 %scores.1 = (f32[32,88,128]{2,1,0:T(8,128)}, f32[3072,128]{1,0:T(8,128)}) custom-call(bf16[1536,1024]{1,0:T(8,128)(2,1)} %hid_hbm.1, bf16[1224,1024]{1,0:T(8,128)(2,1)} %bitcast.29, bf16[153,1024]{1,0:T(8,128)(2,1)} %bitcast.30, f32[1,153]{1,0:T(1,128)} %bitcast.34, f32[5,8]{1,0:T(8,128)} %coef.1, s32[48,128]{1,0:T(8,128)} %bitcast.31, s32[48,128]{1,0:T(8,128)} %bitcast.32, ...), custom_call_target="tpu_custom_call" | custom-call | tf_op jit(solution)/shard_map/scores/pallas_call | solution.py:518
  29.5 0.0 copy-start.5
  29.6 0.0 copy-start.1
  29.6 0.0 copy-start.3
  29.6 0.0 copy-start.4
  29.6 7.3 %all-to-all-start = ((f32[32,88,128]{2,1,0:T(8,128)}), f32[32,88,128]{2,1,0:T(8,128)S(1)}, u32[]{:S(2)}, u32[]{:S(2)}) async-start(f32[32,88,128]{2,1,0:T(8,128)} %get-tuple-element.27), calls=%async_computation | async-start | bytes 2883584 | tf_op jit(solution)/shard_map/all_to_all | solution.py:531
  36.9 0.0 copy-done.5
  36.9 0.1 copy.17
  37.0 0.0 copy-done.1
  37.0 0.0 copy-done.3
  37.0 0.0 copy-done.4
  37.0 0.0 copy-start
  37.0 1.9 %copy-done = f32[48,128,128]{2,1,0:T(8,128)S(1)} copy-done((f32[48,128,128]{2,1,0:T(8,128)S(1)}, f32[48,128,128]{2,1,0:T(8,128)}, u32[]{:S(2)}) %copy-start) | copy-done | bytes 3145752
  38.9 0.0 copy-start.2
  38.9 3.6 %tiles.2 = (bf16[1536,256]{1,0:T(8,128)(2,1)}, bf16[1536,256]{1,0:T(8,128)(2,1)}, bf16[1536,256]{1,0:T(8,128)(2,1)S(1)}, bf16[1536,256]{1,0:T(8,128)(2,1)S(1)}, ...) custom-call(f32[48,128,128]{2,1,0:T(8,128)S(1)} %copy-done, s32[48]{0:T(128)S(1)} %copy-done.1, s32[12,128]{1,0:T(8,128)S(1)} %bitcast.27, ...), custom_call_target="tpu_custom_call" | custom-call | flops 10000000 | bytes 8000000 | tf_op jit(solution)/shard_map/tiles/pallas_call | solution.py:518
  42.5 0.6 broadcast_multiply_fusion.bnd_hbm.refs_4_
  43.1 28.6 %all-to-all-done.arr = f32[32,88,128]{2,1,0:T(8,128)S(1)} async-done(((f32[32,88,128]{2,1,0:T(8,128)}), f32[32,88,128]{2,1,0:T(8,128)S(1)}, u32[]{:S(2)}, u32[]{:S(2)}) %all-to-all-start) | async-done | bytes 1441824 | tf_op jit(solution)/shard_map/all_to_all | solution.py:531
  71.8 0.0 copy-done.2
  71.8 5.3 %errors.1 = (f32[3072,128]{1,0:T(8,128)}, f32[3072,128]{1,0:T(8,128)}, f32[320,128]{1,0:T(8,128)}) custom-call(f32[32,88,128]{2,1,0:T(8,128)S(1)} %all-to-all-done.arr, s32[1,32,72]{2,1,0:T(8,128)S(1)} %copy-done.2, s32[1,32,8]{2,1,0:T(8,128)} %broadcast_multiply_fusion.bnd_hbm.refs_4_, f32[1536,128]{1,0:T(8,128)} %get-tuple-element.28.labk_hbm), custom_call_target="tpu_custom_call" | custom-call | tf_op jit(solution)/shard_map/errors/pallas_call | solution.py:518
  77.1 3.6 %all-to-all-start.1 = ((f32[32,1,1280]{2,1,0:T(1,128)}), f32[32,1,1280]{2,1,0:T(1,128)S(1)}, u32[]{:S(2)}, u32[]{:S(2)}) async-start(f32[32,1,1280]{2,1,0:T(1,128)} %bitcast.8), calls=%async_computation.1 | async-start | bytes 327680 | tf_op jit(solution)/shard_map/all_to_all | solution.py:531
  80.8 5.8 %near.6 = (f32[1536,256]{1,0:T(8,128)S(1)}, f32[8,128]{1,0:T(8,128)S(1)}) custom-call(f32[3072,128]{1,0:T(8,128)} %get-tuple-element.32.v_hbm.e_hbm, f32[3072,128]{1,0:T(8,128)} %get-tuple-element.32.v_hbm.e_hbm, bf16[1536,256]{1,0:T(8,128)(2,1)} %get-tuple-element.33.nh_hbm, bf16[1536,256]{1,0:T(8,128)(2,1)} %get-tuple-element.34.nl_hbm, s32[48]{0:T(128)S(1)} %copy-done.1, ...), custom_call_target="tpu_custom_call" | custom-call | flops 1000000000 | bytes 8000000 | tf_op jit(solution)/shard_map/near/pallas_call | solution.py:518
  86.6 2.8 %all-to-all-done.1 = f32[32,1,1280]{2,1,0:T(1,128)S(1)} async-done(((f32[32,1,1280]{2,1,0:T(1,128)}), f32[32,1,1280]{2,1,0:T(1,128)S(1)}, u32[]{:S(2)}, u32[]{:S(2)}) %all-to-all-start.1) | async-done | bytes 163872 | tf_op jit(solution)/shard_map/all_to_all | solution.py:531
  89.4 2.6 %far_step.3 = (f32[3072,128]{1,0:T(8,128)}, f32[320,128]{1,0:T(8,128)}) custom-call(f32[320,128]{1,0:T(8,128)S(1)} %bitcast.23, bf16[1536,256]{1,0:T(8,128)(2,1)S(1)} %get-tuple-element.30.refs_1_, bf16[1536,256]{1,0:T(8,128)(2,1)S(1)} %get-tuple-element.31.refs_2_, f32[1536,256]{1,0:T(8,128)S(1)} %get-tuple-element.36.refs_3_, ...), custom_call_target="tpu_custom_call" | custom-call | tf_op jit(solution)/shard_map/far_step/pallas_call | solution.py:518
  92.0 3.0 %all-to-all-start.2 = ((f32[32,1,1280]{2,1,0:T(1,128)}), f32[32,1,1280]{2,1,0:T(1,128)S(1)}, u32[]{:S(2)}, u32[]{:S(2)}) async-start(f32[32,1,1280]{2,1,0:T(1,128)} %bitcast.10), calls=%async_computation.2 | async-start | bytes 327680 | tf_op jit(solution)/shard_map/all_to_all | solution.py:531
  95.0 5.7 %near.7.refs_3_ = f32[1536,256]{1,0:T(8,128)S(1)} custom-call(f32[3072,128]{1,0:T(8,128)} %get-tuple-element.38.v_hbm, f32[3072,128]{1,0:T(8,128)} %get-tuple-element.32.v_hbm.e_hbm, bf16[1536,256]{1,0:T(8,128)(2,1)} %get-tuple-element.33.nh_hbm, bf16[1536,256]{1,0:T(8,128)(2,1)} %get-tuple-element.34.nl_hbm, s32[48]{0:T(128)S(1)} %copy-done.1), custom_call_target="tpu_custom_call" | custom-call | flops 1000000000 | bytes 8000000 | tf_op jit(solution)/shard_map/near/pallas_call | solution.py:518
  100.7 2.9 %all-to-all-done.2 = f32[32,1,1280]{2,1,0:T(1,128)S(1)} async-done(((f32[32,1,1280]{2,1,0:T(1,128)}), f32[32,1,1280]{2,1,0:T(1,128)S(1)}, u32[]{:S(2)}, u32[]{:S(2)}) %all-to-all-start.2) | async-done | bytes 163872 | tf_op jit(solution)/shard_map/all_to_all | solution.py:531
  103.7 2.6 %far_sums.1 = (f32[3072,128]{1,0:T(8,128)}, f32[320,128]{1,0:T(8,128)}) custom-call(f32[320,128]{1,0:T(8,128)S(1)} %bitcast.24, bf16[1536,256]{1,0:T(8,128)(2,1)S(1)} %get-tuple-element.30.refs_1_, bf16[1536,256]{1,0:T(8,128)(2,1)S(1)} %get-tuple-element.31.refs_2_, f32[1536,256]{1,0:T(8,128)S(1)} %near.7.refs_3_, ...), custom_call_target="tpu_custom_call" | custom-call | tf_op jit(solution)/shard_map/far_sums/pallas_call | solution.py:518
  106.2 3.1 %all-to-all-start.3 = ((f32[32,1,1280]{2,1,0:T(1,128)}), f32[32,1,1280]{2,1,0:T(1,128)S(1)}, u32[]{:S(2)}, u32[]{:S(2)}) async-start(f32[32,1,1280]{2,1,0:T(1,128)} %bitcast.12), calls=%async_computation.3 | async-start | bytes 327680 | tf_op jit(solution)/shard_map/all_to_all | solution.py:531
  109.3 5.7 %near.8.refs_3_ = f32[1536,256]{1,0:T(8,128)S(1)} custom-call(f32[3072,128]{1,0:T(8,128)} %get-tuple-element.41.v_hbm, f32[3072,128]{1,0:T(8,128)} %get-tuple-element.32.v_hbm.e_hbm, bf16[1536,256]{1,0:T(8,128)(2,1)} %get-tuple-element.33.nh_hbm, bf16[1536,256]{1,0:T(8,128)(2,1)} %get-tuple-element.34.nl_hbm, s32[48]{0:T(128)S(1)} %copy-done.1), custom_call_target="tpu_custom_call" | custom-call | flops 1000000000 | bytes 8000000 | tf_op jit(solution)/shard_map/near/pallas_call | solution.py:518
  115.0 2.8 %all-to-all-done.3 = f32[32,1,1280]{2,1,0:T(1,128)S(1)} async-done(((f32[32,1,1280]{2,1,0:T(1,128)}), f32[32,1,1280]{2,1,0:T(1,128)S(1)}, u32[]{:S(2)}, u32[]{:S(2)}) %all-to-all-start.3) | async-done | bytes 163872 | tf_op jit(solution)/shard_map/all_to_all | solution.py:531
  117.8 3.9 %far_turn.1 = (f32[3072,128]{1,0:T(8,128)}, f32[320,128]{1,0:T(8,128)}) custom-call(f32[320,128]{1,0:T(8,128)S(1)} %bitcast.21, bf16[1536,256]{1,0:T(8,128)(2,1)S(1)} %get-tuple-element.30.refs_1_, bf16[1536,256]{1,0:T(8,128)(2,1)S(1)} %get-tuple-element.31.refs_2_, f32[1536,256]{1,0:T(8,128)S(1)} %near.8.refs_3_, ...), custom_call_target="tpu_custom_call" | custom-call | tf_op jit(solution)/shard_map/far_turn/pallas_call | solution.py:518
  121.6 2.9 %all-to-all-start.4 = ((f32[32,1,1280]{2,1,0:T(1,128)}), f32[32,1,1280]{2,1,0:T(1,128)S(1)}, u32[]{:S(2)}, u32[]{:S(2)}) async-start(f32[32,1,1280]{2,1,0:T(1,128)} %bitcast.14), calls=%async_computation.4 | async-start | bytes 327680 | tf_op jit(solution)/shard_map/all_to_all | solution.py:531
  124.6 5.7 %near.9.refs_3_ = f32[1536,256]{1,0:T(8,128)S(1)} custom-call(f32[3072,128]{1,0:T(8,128)} %get-tuple-element.44.v_hbm.e_hbm, f32[3072,128]{1,0:T(8,128)} %get-tuple-element.44.v_hbm.e_hbm, bf16[1536,256]{1,0:T(8,128)(2,1)} %get-tuple-element.33.nh_hbm, bf16[1536,256]{1,0:T(8,128)(2,1)} %get-tuple-element.34.nl_hbm, s32[48]{0:T(128)S(1)} %copy-done.1), custom_call_target="tpu_custom_call" | custom-call | flops 1000000000 | bytes 8000000 | tf_op jit(solution)/shard_map/near/pallas_call | solution.py:518
  130.2 3.0 %all-to-all-done.4 = f32[32,1,1280]{2,1,0:T(1,128)S(1)} async-done(((f32[32,1,1280]{2,1,0:T(1,128)}), f32[32,1,1280]{2,1,0:T(1,128)S(1)}, u32[]{:S(2)}, u32[]{:S(2)}) %all-to-all-start.4) | async-done | bytes 163872 | tf_op jit(solution)/shard_map/all_to_all | solution.py:531
  133.2 2.6 %far_step.4 = (f32[3072,128]{1,0:T(8,128)}, f32[320,128]{1,0:T(8,128)}) custom-call(f32[320,128]{1,0:T(8,128)S(1)} %bitcast.26, bf16[1536,256]{1,0:T(8,128)(2,1)S(1)} %get-tuple-element.30.refs_1_, bf16[1536,256]{1,0:T(8,128)(2,1)S(1)} %get-tuple-element.31.refs_2_, f32[1536,256]{1,0:T(8,128)S(1)} %near.9.refs_3_, ...), custom_call_target="tpu_custom_call" | custom-call | tf_op jit(solution)/shard_map/far_step/pallas_call | solution.py:518
  135.8 2.9 %all-to-all-start.5 = ((f32[32,1,1280]{2,1,0:T(1,128)}), f32[32,1,1280]{2,1,0:T(1,128)S(1)}, u32[]{:S(2)}, u32[]{:S(2)}) async-start(f32[32,1,1280]{2,1,0:T(1,128)} %bitcast.16), calls=%async_computation.5 | async-start | bytes 327680 | tf_op jit(solution)/shard_map/all_to_all | solution.py:531
  138.7 5.7 %near.10.refs_3_ = f32[1536,256]{1,0:T(8,128)S(1)} custom-call(f32[3072,128]{1,0:T(8,128)} %get-tuple-element.46.v_hbm, f32[3072,128]{1,0:T(8,128)} %get-tuple-element.44.v_hbm.e_hbm, bf16[1536,256]{1,0:T(8,128)(2,1)} %get-tuple-element.33.nh_hbm, bf16[1536,256]{1,0:T(8,128)(2,1)} %get-tuple-element.34.nl_hbm, s32[48]{0:T(128)S(1)} %copy-done.1), custom_call_target="tpu_custom_call" | custom-call | flops 1000000000 | bytes 8000000 | tf_op jit(solution)/shard_map/near/pallas_call | solution.py:518
  144.4 2.9 %all-to-all-done.5 = f32[32,1,1280]{2,1,0:T(1,128)S(1)} async-done(((f32[32,1,1280]{2,1,0:T(1,128)}), f32[32,1,1280]{2,1,0:T(1,128)S(1)}, u32[]{:S(2)}, u32[]{:S(2)}) %all-to-all-start.5) | async-done | bytes 163872 | tf_op jit(solution)/shard_map/all_to_all | solution.py:531
  147.3 2.6 %far_step.5 = (f32[3072,128]{1,0:T(8,128)}, f32[320,128]{1,0:T(8,128)}) custom-call(f32[320,128]{1,0:T(8,128)S(1)} %bitcast.25, bf16[1536,256]{1,0:T(8,128)(2,1)S(1)} %get-tuple-element.30.refs_1_, bf16[1536,256]{1,0:T(8,128)(2,1)S(1)} %get-tuple-element.31.refs_2_, f32[1536,256]{1,0:T(8,128)S(1)} %near.10.refs_3_, ...), custom_call_target="tpu_custom_call" | custom-call | tf_op jit(solution)/shard_map/far_step/pallas_call | solution.py:518
  149.9 2.9 %all-to-all-start.6 = ((f32[32,1,1280]{2,1,0:T(1,128)}), f32[32,1,1280]{2,1,0:T(1,128)S(1)}, u32[]{:S(2)}, u32[]{:S(2)}) async-start(f32[32,1,1280]{2,1,0:T(1,128)} %bitcast.18), calls=%async_computation.6 | async-start | bytes 327680 | tf_op jit(solution)/shard_map/all_to_all | solution.py:531
  152.8 5.7 %near.11.refs_3_ = f32[1536,256]{1,0:T(8,128)S(1)} custom-call(f32[3072,128]{1,0:T(8,128)} %get-tuple-element.48.v_hbm, f32[3072,128]{1,0:T(8,128)} %get-tuple-element.44.v_hbm.e_hbm, bf16[1536,256]{1,0:T(8,128)(2,1)} %get-tuple-element.33.nh_hbm, bf16[1536,256]{1,0:T(8,128)(2,1)} %get-tuple-element.34.nl_hbm, s32[48]{0:T(128)S(1)} %copy-done.1), custom_call_target="tpu_custom_call" | custom-call | flops 1000000000 | bytes 8000000 | tf_op jit(solution)/shard_map/near/pallas_call | solution.py:518
  158.5 2.9 %all-to-all-done.6 = f32[32,1,1280]{2,1,0:T(1,128)S(1)} async-done(((f32[32,1,1280]{2,1,0:T(1,128)}), f32[32,1,1280]{2,1,0:T(1,128)S(1)}, u32[]{:S(2)}, u32[]{:S(2)}) %all-to-all-start.6) | async-done | bytes 163872 | tf_op jit(solution)/shard_map/all_to_all | solution.py:531
  161.4 2.2 %far_last.1 = f32[153,1536]{1,0:T(8,128)} custom-call(f32[320,128]{1,0:T(8,128)S(1)} %bitcast.22, bf16[1536,256]{1,0:T(8,128)(2,1)S(1)} %get-tuple-element.30.refs_1_, bf16[1536,256]{1,0:T(8,128)(2,1)S(1)} %get-tuple-element.31.refs_2_, f32[1536,256]{1,0:T(8,128)S(1)} %near.11.refs_3_), custom_call_target="tpu_custom_call" | custom-call | tf_op jit(solution)/shard_map/far_last/pallas_call | solution.py:518
Async XLA Ops:
  29.5 7.4 %copy-start.5 = (s32[1,32,8]{1,2,0:T(8,128)S(1)}, s32[1,32,8]{1,2,0:T(8,128)}, u32[]{:S(2)}) copy-start(s32[1,32,8]{1,2,0:T(8,128)} %param.27) | copy-start | bytes 3076
  29.6 7.5 %copy-start.1 = (s32[48]{0:T(128)S(1)}, s32[48]{0:T(128)}, u32[]{:S(2)}) copy-start(s32[48]{0:T(128)} %cols.13) | copy-start | bytes 580
  29.6 7.5 %copy-start.3 = (s32[1536]{0:T(1024)S(1)}, s32[1536]{0:T(1024)}, u32[]{:S(2)}) copy-start(s32[1536]{0:T(1024)} %param.25) | copy-start | bytes 18436
  29.6 7.4 %copy-start.4 = (s32[1536]{0:T(1024)S(1)}, s32[1536]{0:T(1024)}, u32[]{:S(2)}) copy-start(s32[1536]{0:T(1024)} %param.26) | copy-start | bytes 18436
  29.6 42.2 %all-to-all-start = ((f32[32,88,128]{2,1,0:T(8,128)}), f32[32,88,128]{2,1,0:T(8,128)S(1)}, u32[]{:S(2)}, u32[]{:S(2)}) async-start(f32[32,88,128]{2,1,0:T(8,128)} %get-tuple-element.27), calls=%async_computation | async-start | bytes 2883584 | tf_op jit(solution)/shard_map/all_to_all | solution.py:531
  37.0 1.9 %copy-start = (f32[48,128,128]{2,1,0:T(8,128)S(1)}, f32[48,128,128]{2,1,0:T(8,128)}, u32[]{:S(2)}) copy-start(f32[48,128,128]{2,1,0:T(8,128)} %tiles.3) | copy-start | bytes 9437188
  38.9 32.9 %copy-start.2 = (s32[1,32,72]{2,1,0:T(8,128)S(1)}, s32[1,32,72]{2,1,0:T(8,128)}, u32[]{:S(2)}) copy-start(s32[1,32,72]{2,1,0:T(8,128)} %recv.1) | copy-start | bytes 27652
  77.1 12.3 %all-to-all-start.1 = ((f32[32,1,1280]{2,1,0:T(1,128)}), f32[32,1,1280]{2,1,0:T(1,128)S(1)}, u32[]{:S(2)}, u32[]{:S(2)}) async-start(f32[32,1,1280]{2,1,0:T(1,128)} %bitcast.8), calls=%async_computation.1 | async-start | bytes 327680 | tf_op jit(solution)/shard_map/all_to_all | solution.py:531
  92.0 11.7 %all-to-all-start.2 = ((f32[32,1,1280]{2,1,0:T(1,128)}), f32[32,1,1280]{2,1,0:T(1,128)S(1)}, u32[]{:S(2)}, u32[]{:S(2)}) async-start(f32[32,1,1280]{2,1,0:T(1,128)} %bitcast.10), calls=%async_computation.2 | async-start | bytes 327680 | tf_op jit(solution)/shard_map/all_to_all | solution.py:531
  106.2 11.5 %all-to-all-start.3 = ((f32[32,1,1280]{2,1,0:T(1,128)}), f32[32,1,1280]{2,1,0:T(1,128)S(1)}, u32[]{:S(2)}, u32[]{:S(2)}) async-start(f32[32,1,1280]{2,1,0:T(1,128)} %bitcast.12), calls=%async_computation.3 | async-start | bytes 327680 | tf_op jit(solution)/shard_map/all_to_all | solution.py:531
  121.6 11.5 %all-to-all-start.4 = ((f32[32,1,1280]{2,1,0:T(1,128)}), f32[32,1,1280]{2,1,0:T(1,128)S(1)}, u32[]{:S(2)}, u32[]{:S(2)}) async-start(f32[32,1,1280]{2,1,0:T(1,128)} %bitcast.14), calls=%async_computation.4 | async-start | bytes 327680 | tf_op jit(solution)/shard_map/all_to_all | solution.py:531
  135.8 11.5 %all-to-all-start.5 = ((f32[32,1,1280]{2,1,0:T(1,128)}), f32[32,1,1280]{2,1,0:T(1,128)S(1)}, u32[]{:S(2)}, u32[]{:S(2)}) async-start(f32[32,1,1280]{2,1,0:T(1,128)} %bitcast.16), calls=%async_computation.5 | async-start | bytes 327680 | tf_op jit(solution)/shard_map/all_to_all | solution.py:531
  149.9 11.5 %all-to-all-start.6 = ((f32[32,1,1280]{2,1,0:T(1,128)}), f32[32,1,1280]{2,1,0:T(1,128)S(1)}, u32[]{:S(2)}, u32[]{:S(2)}) async-start(f32[32,1,1280]{2,1,0:T(1,128)} %bitcast.18), calls=%async_computation.6 | async-start | bytes 327680 | tf_op jit(solution)/shard_map/all_to_all | solution.py:531

commit v9 on v8

--- a/solution.py
+++ b/solution.py
@@ -440,7 +440,7 @@
         for c in loads:
             c.start()
     if mode == "last":
-        out, hm, hr = refs
+        out_hbm, hm, hr, out, osem = refs
     else:
         v_hbm, out, hm, hr, v2, stgb, vsem = refs
     ntail = up(slots, per)
@@ -459,9 +459,13 @@
             hr[pl.ds(j * per + q, peers, stride=slots), :] = x
     hh, hl = split(jnp.concatenate([hm[...], hr[...]], 1))
 
-    chunk = n // 2
+    chunk = n // (4 if mode == "last" else 2)
     lane = lanes(chunk)
     count = n // chunk
+
+    def ship(i):
+        cols = pl.ds(pl.multiple_of(i * chunk, chunk), chunk)
+        return pltpu.make_async_copy(out.at[:, cols], out_hbm.at[:, cols], osem.at[i])
 
     parts = 6
     small = chunk // parts
@@ -482,6 +486,7 @@
         if mode == "last":
             out[0:L, rows] = v[:, :L].T
             out[L:classes, rows] = v[:, L:].T[:rest]
+            ship(i).start()
             return 0
         if mode == "turn":
             mag = jnp.abs(v)
@@ -503,7 +508,10 @@
         return 0
 
     lax.fori_loop(0, count, body, 0)
-    if mode != "last":
+    if mode == "last":
+        for i in range(count):
+            ship(i).wait()
+    else:
         extra = tot[0:1, :] if mode == "sums" else None
         pack((bcopy, bnd), v2, stgb, out, extra, peers=peers, slots=slots, per=per, rest=rest)
         for i in range(count * parts):
@@ -635,7 +643,11 @@
         )
         args, ins = (halos, fh, fl, part), [VM] * 4
         if mode == "last":
-            return call(far, sds((classes, n), F32), ins, args, hscr, vmem=24 * MIB, name="far_last").T
+            scratch = hscr + [pltpu.VMEM((classes, n), F32), dma(4)]
+            got = call(
+                far, (sds((classes, n), F32),), ins, args, scratch, vmem=24 * MIB, name="far_last", specs=(HB,)
+            )
+            return got[0].T
         args, ins = args + (bnd_rows,), ins + [HB]
         scratch = hscr + [rows2, stageb, dma(n // L)]
         if mode == "sums":

time: 164 us -> 165 us (level)
  no operation moved by 1% of the time
where the time goes in v9:
time: 165 us; the launch traced here: 164 us
  Pallas kernels  89.3 us (54%)
  waiting for transfers between devices  46 us (28%)
  starting transfers between devices  25.8 us (16%)
  local copies, waits for them, and re-layouts  1.99 us (1%)
    pallas_call x15, Pallas kernels, call(): pl.pallas_call(kernel, out_shape=outs, in_specs=ins, out_specs=specs or j...  89.3 us
    all_to_all x7, waiting for transfers between devices, swap(): return lax.all_to_all(x, 'dom', split_axis=0, concat_axis=0, tiled=True)  46 us
    all_to_all x7, starting transfers between devices, swap(): return lax.all_to_all(x, 'dom', split_axis=0, concat_axis=0, tiled=True)  25.8 us
  transfers between devices with their start and end apart: 7, of which 7 were waited for; matrix products, arithmetic and copies ran while one was open for 0% of the time, Pallas kernels for 23%

profile of v9, /device:TPU:0, one launch (start us, length us, event | category | flops | bytes accessed | tf_op | source)
XLA Modules:
  0.0 164.1 jit_solution(17735839166581912655)
XLA Ops:
  0.0 29.5 %scores.1 = (f32[32,88,128]{2,1,0:T(8,128)}, f32[3072,128]{1,0:T(8,128)}) custom-call(bf16[1536,1024]{1,0:T(8,128)(2,1)} %hid_hbm.1, bf16[1224,1024]{1,0:T(8,128)(2,1)} %bitcast.29, bf16[153,1024]{1,0:T(8,128)(2,1)} %bitcast.30, f32[1,153]{1,0:T(1,128)} %bitcast.34, f32[5,8]{1,0:T(8,128)} %coef.1, s32[48,128]{1,0:T(8,128)} %bitcast.31, s32[48,128]{1,0:T(8,128)} %bitcast.32, ...), custom_call_target="tpu_custom_call" | custom-call | tf_op jit(solution)/shard_map/scores/pallas_call | solution.py:526
  29.5 0.0 copy-start.5
  29.6 0.0 copy-start.1
  29.6 0.0 copy-start.3
  29.6 0.0 copy-start.4
  29.6 7.3 %all-to-all-start = ((f32[32,88,128]{2,1,0:T(8,128)}), f32[32,88,128]{2,1,0:T(8,128)S(1)}, u32[]{:S(2)}, u32[]{:S(2)}) async-start(f32[32,88,128]{2,1,0:T(8,128)} %get-tuple-element.27), calls=%async_computation | async-start | bytes 2883584 | tf_op jit(solution)/shard_map/all_to_all | solution.py:539
  36.9 0.0 copy-done.5
  36.9 0.1 copy.17
  37.0 0.0 copy-done.1
  37.0 0.0 copy-done.3
  37.0 0.0 copy-done.4
  37.0 0.0 copy-start
  37.0 1.9 %copy-done = f32[48,128,128]{2,1,0:T(8,128)S(1)} copy-done((f32[48,128,128]{2,1,0:T(8,128)S(1)}, f32[48,128,128]{2,1,0:T(8,128)}, u32[]{:S(2)}) %copy-start) | copy-done | bytes 3145752
  38.9 0.0 copy-start.2
  38.9 3.6 %tiles.2 = (bf16[1536,256]{1,0:T(8,128)(2,1)}, bf16[1536,256]{1,0:T(8,128)(2,1)}, bf16[1536,256]{1,0:T(8,128)(2,1)S(1)}, bf16[1536,256]{1,0:T(8,128)(2,1)S(1)}, ...) custom-call(f32[48,128,128]{2,1,0:T(8,128)S(1)} %copy-done, s32[48]{0:T(128)S(1)} %copy-done.1, s32[12,128]{1,0:T(8,128)S(1)} %bitcast.27, ...), custom_call_target="tpu_custom_call" | custom-call | flops 10000000 | bytes 8000000 | tf_op jit(solution)/shard_map/tiles/pallas_call | solution.py:526
  42.5 0.6 broadcast_multiply_fusion.bnd_hbm.refs_4_
  43.1 28.6 %all-to-all-done.arr = f32[32,88,128]{2,1,0:T(8,128)S(1)} async-done(((f32[32,88,128]{2,1,0:T(8,128)}), f32[32,88,128]{2,1,0:T(8,128)S(1)}, u32[]{:S(2)}, u32[]{:S(2)}) %all-to-all-start) | async-done | bytes 1441824 | tf_op jit(solution)/shard_map/all_to_all | solution.py:539
  71.8 0.0 copy-done.2
  71.8 5.3 %errors.1 = (f32[3072,128]{1,0:T(8,128)}, f32[3072,128]{1,0:T(8,128)}, f32[320,128]{1,0:T(8,128)}) custom-call(f32[32,88,128]{2,1,0:T(8,128)S(1)} %all-to-all-done.arr, s32[1,32,72]{2,1,0:T(8,128)S(1)} %copy-done.2, s32[1,32,8]{2,1,0:T(8,128)} %broadcast_multiply_fusion.bnd_hbm.refs_4_, f32[1536,128]{1,0:T(8,128)} %get-tuple-element.28.labk_hbm), custom_call_target="tpu_custom_call" | custom-call | tf_op jit(solution)/shard_map/errors/pallas_call | solution.py:526
  77.1 3.6 %all-to-all-start.1 = ((f32[32,1,1280]{2,1,0:T(1,128)}), f32[32,1,1280]{2,1,0:T(1,128)S(1)}, u32[]{:S(2)}, u32[]{:S(2)}) async-start(f32[32,1,1280]{2,1,0:T(1,128)} %bitcast.8), calls=%async_computation.1 | async-start | bytes 327680 | tf_op jit(solution)/shard_map/all_to_all | solution.py:539
  80.8 5.8 %near.6 = (f32[1536,256]{1,0:T(8,128)S(1)}, f32[8,128]{1,0:T(8,128)S(1)}) custom-call(f32[3072,128]{1,0:T(8,128)} %get-tuple-element.32.v_hbm.e_hbm, f32[3072,128]{1,0:T(8,128)} %get-tuple-element.32.v_hbm.e_hbm, bf16[1536,256]{1,0:T(8,128)(2,1)} %get-tuple-element.33.nh_hbm, bf16[1536,256]{1,0:T(8,128)(2,1)} %get-tuple-element.34.nl_hbm, s32[48]{0:T(128)S(1)} %copy-done.1, ...), custom_call_target="tpu_custom_call" | custom-call | flops 1000000000 | bytes 8000000 | tf_op jit(solution)/shard_map/near/pallas_call | solution.py:526
  86.6 2.8 %all-to-all-done.1 = f32[32,1,1280]{2,1,0:T(1,128)S(1)} async-done(((f32[32,1,1280]{2,1,0:T(1,128)}), f32[32,1,1280]{2,1,0:T(1,128)S(1)}, u32[]{:S(2)}, u32[]{:S(2)}) %all-to-all-start.1) | async-done | bytes 163872 | tf_op jit(solution)/shard_map/all_to_all | solution.py:539
  89.4 2.6 %far_step.3 = (f32[3072,128]{1,0:T(8,128)}, f32[320,128]{1,0:T(8,128)}) custom-call(f32[320,128]{1,0:T(8,128)S(1)} %bitcast.23, bf16[1536,256]{1,0:T(8,128)(2,1)S(1)} %get-tuple-element.30.refs_1_, bf16[1536,256]{1,0:T(8,128)(2,1)S(1)} %get-tuple-element.31.refs_2_, f32[1536,256]{1,0:T(8,128)S(1)} %get-tuple-element.36.refs_3_, ...), custom_call_target="tpu_custom_call" | custom-call | tf_op jit(solution)/shard_map/far_step/pallas_call | solution.py:526
  92.0 3.0 %all-to-all-start.2 = ((f32[32,1,1280]{2,1,0:T(1,128)}), f32[32,1,1280]{2,1,0:T(1,128)S(1)}, u32[]{:S(2)}, u32[]{:S(2)}) async-start(f32[32,1,1280]{2,1,0:T(1,128)} %bitcast.10), calls=%async_computation.2 | async-start | bytes 327680 | tf_op jit(solution)/shard_map/all_to_all | solution.py:539
  95.0 5.7 %near.7.refs_3_ = f32[1536,256]{1,0:T(8,128)S(1)} custom-call(f32[3072,128]{1,0:T(8,128)} %get-tuple-element.38.v_hbm, f32[3072,128]{1,0:T(8,128)} %get-tuple-element.32.v_hbm.e_hbm, bf16[1536,256]{1,0:T(8,128)(2,1)} %get-tuple-element.33.nh_hbm, bf16[1536,256]{1,0:T(8,128)(2,1)} %get-tuple-element.34.nl_hbm, s32[48]{0:T(128)S(1)} %copy-done.1), custom_call_target="tpu_custom_call" | custom-call | flops 1000000000 | bytes 8000000 | tf_op jit(solution)/shard_map/near/pallas_call | solution.py:526
  100.7 2.9 %all-to-all-done.2 = f32[32,1,1280]{2,1,0:T(1,128)S(1)} async-done(((f32[32,1,1280]{2,1,0:T(1,128)}), f32[32,1,1280]{2,1,0:T(1,128)S(1)}, u32[]{:S(2)}, u32[]{:S(2)}) %all-to-all-start.2) | async-done | bytes 163872 | tf_op jit(solution)/shard_map/all_to_all | solution.py:539
  103.7 2.6 %far_sums.1 = (f32[3072,128]{1,0:T(8,128)}, f32[320,128]{1,0:T(8,128)}) custom-call(f32[320,128]{1,0:T(8,128)S(1)} %bitcast.24, bf16[1536,256]{1,0:T(8,128)(2,1)S(1)} %get-tuple-element.30.refs_1_, bf16[1536,256]{1,0:T(8,128)(2,1)S(1)} %get-tuple-element.31.refs_2_, f32[1536,256]{1,0:T(8,128)S(1)} %near.7.refs_3_, ...), custom_call_target="tpu_custom_call" | custom-call | tf_op jit(solution)/shard_map/far_sums/pallas_call | solution.py:526
  106.2 3.1 %all-to-all-start.3 = ((f32[32,1,1280]{2,1,0:T(1,128)}), f32[32,1,1280]{2,1,0:T(1,128)S(1)}, u32[]{:S(2)}, u32[]{:S(2)}) async-start(f32[32,1,1280]{2,1,0:T(1,128)} %bitcast.12), calls=%async_computation.3 | async-start | bytes 327680 | tf_op jit(solution)/shard_map/all_to_all | solution.py:539
  109.3 5.7 %near.8.refs_3_ = f32[1536,256]{1,0:T(8,128)S(1)} custom-call(f32[3072,128]{1,0:T(8,128)} %get-tuple-element.41.v_hbm, f32[3072,128]{1,0:T(8,128)} %get-tuple-element.32.v_hbm.e_hbm, bf16[1536,256]{1,0:T(8,128)(2,1)} %get-tuple-element.33.nh_hbm, bf16[1536,256]{1,0:T(8,128)(2,1)} %get-tuple-element.34.nl_hbm, s32[48]{0:T(128)S(1)} %copy-done.1), custom_call_target="tpu_custom_call" | custom-call | flops 1000000000 | bytes 8000000 | tf_op jit(solution)/shard_map/near/pallas_call | solution.py:526
  115.0 2.8 %all-to-all-done.3 = f32[32,1,1280]{2,1,0:T(1,128)S(1)} async-done(((f32[32,1,1280]{2,1,0:T(1,128)}), f32[32,1,1280]{2,1,0:T(1,128)S(1)}, u32[]{:S(2)}, u32[]{:S(2)}) %all-to-all-start.3) | async-done | bytes 163872 | tf_op jit(solution)/shard_map/all_to_all | solution.py:539
  117.8 3.9 %far_turn.1 = (f32[3072,128]{1,0:T(8,128)}, f32[320,128]{1,0:T(8,128)}) custom-call(f32[320,128]{1,0:T(8,128)S(1)} %bitcast.21, bf16[1536,256]{1,0:T(8,128)(2,1)S(1)} %get-tuple-element.30.refs_1_, bf16[1536,256]{1,0:T(8,128)(2,1)S(1)} %get-tuple-element.31.refs_2_, f32[1536,256]{1,0:T(8,128)S(1)} %near.8.refs_3_, ...), custom_call_target="tpu_custom_call" | custom-call | tf_op jit(solution)/shard_map/far_turn/pallas_call | solution.py:526
  121.6 2.9 %all-to-all-start.4 = ((f32[32,1,1280]{2,1,0:T(1,128)}), f32[32,1,1280]{2,1,0:T(1,128)S(1)}, u32[]{:S(2)}, u32[]{:S(2)}) async-start(f32[32,1,1280]{2,1,0:T(1,128)} %bitcast.14), calls=%async_computation.4 | async-start | bytes 327680 | tf_op jit(solution)/shard_map/all_to_all | solution.py:539
  124.6 5.7 %near.9.refs_3_ = f32[1536,256]{1,0:T(8,128)S(1)} custom-call(f32[3072,128]{1,0:T(8,128)} %get-tuple-element.44.v_hbm.e_hbm, f32[3072,128]{1,0:T(8,128)} %get-tuple-element.44.v_hbm.e_hbm, bf16[1536,256]{1,0:T(8,128)(2,1)} %get-tuple-element.33.nh_hbm, bf16[1536,256]{1,0:T(8,128)(2,1)} %get-tuple-element.34.nl_hbm, s32[48]{0:T(128)S(1)} %copy-done.1), custom_call_target="tpu_custom_call" | custom-call | flops 1000000000 | bytes 8000000 | tf_op jit(solution)/shard_map/near/pallas_call | solution.py:526
  130.2 3.0 %all-to-all-done.4 = f32[32,1,1280]{2,1,0:T(1,128)S(1)} async-done(((f32[32,1,1280]{2,1,0:T(1,128)}), f32[32,1,1280]{2,1,0:T(1,128)S(1)}, u32[]{:S(2)}, u32[]{:S(2)}) %all-to-all-start.4) | async-done | bytes 163872 | tf_op jit(solution)/shard_map/all_to_all | solution.py:539
  133.2 2.6 %far_step.4 = (f32[3072,128]{1,0:T(8,128)}, f32[320,128]{1,0:T(8,128)}) custom-call(f32[320,128]{1,0:T(8,128)S(1)} %bitcast.26, bf16[1536,256]{1,0:T(8,128)(2,1)S(1)} %get-tuple-element.30.refs_1_, bf16[1536,256]{1,0:T(8,128)(2,1)S(1)} %get-tuple-element.31.refs_2_, f32[1536,256]{1,0:T(8,128)S(1)} %near.9.refs_3_, ...), custom_call_target="tpu_custom_call" | custom-call | tf_op jit(solution)/shard_map/far_step/pallas_call | solution.py:526
  135.8 2.9 %all-to-all-start.5 = ((f32[32,1,1280]{2,1,0:T(1,128)}), f32[32,1,1280]{2,1,0:T(1,128)S(1)}, u32[]{:S(2)}, u32[]{:S(2)}) async-start(f32[32,1,1280]{2,1,0:T(1,128)} %bitcast.16), calls=%async_computation.5 | async-start | bytes 327680 | tf_op jit(solution)/shard_map/all_to_all | solution.py:539
  138.7 5.7 %near.10.refs_3_ = f32[1536,256]{1,0:T(8,128)S(1)} custom-call(f32[3072,128]{1,0:T(8,128)} %get-tuple-element.46.v_hbm, f32[3072,128]{1,0:T(8,128)} %get-tuple-element.44.v_hbm.e_hbm, bf16[1536,256]{1,0:T(8,128)(2,1)} %get-tuple-element.33.nh_hbm, bf16[1536,256]{1,0:T(8,128)(2,1)} %get-tuple-element.34.nl_hbm, s32[48]{0:T(128)S(1)} %copy-done.1), custom_call_target="tpu_custom_call" | custom-call | flops 1000000000 | bytes 8000000 | tf_op jit(solution)/shard_map/near/pallas_call | solution.py:526
  144.4 2.9 %all-to-all-done.5 = f32[32,1,1280]{2,1,0:T(1,128)S(1)} async-done(((f32[32,1,1280]{2,1,0:T(1,128)}), f32[32,1,1280]{2,1,0:T(1,128)S(1)}, u32[]{:S(2)}, u32[]{:S(2)}) %all-to-all-start.5) | async-done | bytes 163872 | tf_op jit(solution)/shard_map/all_to_all | solution.py:539
  147.3 2.6 %far_step.5 = (f32[3072,128]{1,0:T(8,128)}, f32[320,128]{1,0:T(8,128)}) custom-call(f32[320,128]{1,0:T(8,128)S(1)} %bitcast.25, bf16[1536,256]{1,0:T(8,128)(2,1)S(1)} %get-tuple-element.30.refs_1_, bf16[1536,256]{1,0:T(8,128)(2,1)S(1)} %get-tuple-element.31.refs_2_, f32[1536,256]{1,0:T(8,128)S(1)} %near.10.refs_3_, ...), custom_call_target="tpu_custom_call" | custom-call | tf_op jit(solution)/shard_map/far_step/pallas_call | solution.py:526
  149.9 2.9 %all-to-all-start.6 = ((f32[32,1,1280]{2,1,0:T(1,128)}), f32[32,1,1280]{2,1,0:T(1,128)S(1)}, u32[]{:S(2)}, u32[]{:S(2)}) async-start(f32[32,1,1280]{2,1,0:T(1,128)} %bitcast.18), calls=%async_computation.6 | async-start | bytes 327680 | tf_op jit(solution)/shard_map/all_to_all | solution.py:539
  152.8 5.7 %near.11.refs_3_ = f32[1536,256]{1,0:T(8,128)S(1)} custom-call(f32[3072,128]{1,0:T(8,128)} %get-tuple-element.48.v_hbm, f32[3072,128]{1,0:T(8,128)} %get-tuple-element.44.v_hbm.e_hbm, bf16[1536,256]{1,0:T(8,128)(2,1)} %get-tuple-element.33.nh_hbm, bf16[1536,256]{1,0:T(8,128)(2,1)} %get-tuple-element.34.nl_hbm, s32[48]{0:T(128)S(1)} %copy-done.1), custom_call_target="tpu_custom_call" | custom-call | flops 1000000000 | bytes 8000000 | tf_op jit(solution)/shard_map/near/pallas_call | solution.py:526
  158.5 2.9 %all-to-all-done.6 = f32[32,1,1280]{2,1,0:T(1,128)S(1)} async-done(((f32[32,1,1280]{2,1,0:T(1,128)}), f32[32,1,1280]{2,1,0:T(1,128)S(1)}, u32[]{:S(2)}, u32[]{:S(2)}) %all-to-all-start.6) | async-done | bytes 163872 | tf_op jit(solution)/shard_map/all_to_all | solution.py:539
  161.4 2.5 %far_last.1 = f32[153,1536]{1,0:T(8,128)} custom-call(f32[320,128]{1,0:T(8,128)S(1)} %bitcast.22, bf16[1536,256]{1,0:T(8,128)(2,1)S(1)} %get-tuple-element.30.refs_1_, bf16[1536,256]{1,0:T(8,128)(2,1)S(1)} %get-tuple-element.31.refs_2_, f32[1536,256]{1,0:T(8,128)S(1)} %near.11.refs_3_), custom_call_target="tpu_custom_call" | custom-call | tf_op jit(solution)/shard_map/far_last/pallas_call | solution.py:526
Async XLA Ops:
  29.5 7.4 %copy-start.5 = (s32[1,32,8]{1,2,0:T(8,128)S(1)}, s32[1,32,8]{1,2,0:T(8,128)}, u32[]{:S(2)}) copy-start(s32[1,32,8]{1,2,0:T(8,128)} %param.27) | copy-start | bytes 3076
  29.6 7.5 %copy-start.1 = (s32[48]{0:T(128)S(1)}, s32[48]{0:T(128)}, u32[]{:S(2)}) copy-start(s32[48]{0:T(128)} %cols.13) | copy-start | bytes 580
  29.6 7.5 %copy-start.3 = (s32[1536]{0:T(1024)S(1)}, s32[1536]{0:T(1024)}, u32[]{:S(2)}) copy-start(s32[1536]{0:T(1024)} %param.25) | copy-start | bytes 18436
  29.6 7.4 %copy-start.4 = (s32[1536]{0:T(1024)S(1)}, s32[1536]{0:T(1024)}, u32[]{:S(2)}) copy-start(s32[1536]{0:T(1024)} %param.26) | copy-start | bytes 18436
  29.6 42.2 %all-to-all-start = ((f32[32,88,128]{2,1,0:T(8,128)}), f32[32,88,128]{2,1,0:T(8,128)S(1)}, u32[]{:S(2)}, u32[]{:S(2)}) async-start(f32[32,88,128]{2,1,0:T(8,128)} %get-tuple-element.27), calls=%async_computation | async-start | bytes 2883584 | tf_op jit(solution)/shard_map/all_to_all | solution.py:539
  37.0 1.9 %copy-start = (f32[48,128,128]{2,1,0:T(8,128)S(1)}, f32[48,128,128]{2,1,0:T(8,128)}, u32[]{:S(2)}) copy-start(f32[48,128,128]{2,1,0:T(8,128)} %tiles.3) | copy-start | bytes 9437188
  38.9 32.9 %copy-start.2 = (s32[1,32,72]{2,1,0:T(8,128)S(1)}, s32[1,32,72]{2,1,0:T(8,128)}, u32[]{:S(2)}) copy-start(s32[1,32,72]{2,1,0:T(8,128)} %recv.1) | copy-start | bytes 27652
  77.1 12.3 %all-to-all-start.1 = ((f32[32,1,1280]{2,1,0:T(1,128)}), f32[32,1,1280]{2,1,0:T(1,128)S(1)}, u32[]{:S(2)}, u32[]{:S(2)}) async-start(f32[32,1,1280]{2,1,0:T(1,128)} %bitcast.8), calls=%async_computation.1 | async-start | bytes 327680 | tf_op jit(solution)/shard_map/all_to_all | solution.py:539
  92.0 11.7 %all-to-all-start.2 = ((f32[32,1,1280]{2,1,0:T(1,128)}), f32[32,1,1280]{2,1,0:T(1,128)S(1)}, u32[]{:S(2)}, u32[]{:S(2)}) async-start(f32[32,1,1280]{2,1,0:T(1,128)} %bitcast.10), calls=%async_computation.2 | async-start | bytes 327680 | tf_op jit(solution)/shard_map/all_to_all | solution.py:539
  106.2 11.5 %all-to-all-start.3 = ((f32[32,1,1280]{2,1,0:T(1,128)}), f32[32,1,1280]{2,1,0:T(1,128)S(1)}, u32[]{:S(2)}, u32[]{:S(2)}) async-start(f32[32,1,1280]{2,1,0:T(1,128)} %bitcast.12), calls=%async_computation.3 | async-start | bytes 327680 | tf_op jit(solution)/shard_map/all_to_all | solution.py:539
  121.6 11.5 %all-to-all-start.4 = ((f32[32,1,1280]{2,1,0:T(1,128)}), f32[32,1,1280]{2,1,0:T(1,128)S(1)}, u32[]{:S(2)}, u32[]{:S(2)}) async-start(f32[32,1,1280]{2,1,0:T(1,128)} %bitcast.14), calls=%async_computation.4 | async-start | bytes 327680 | tf_op jit(solution)/shard_map/all_to_all | solution.py:539
  135.8 11.5 %all-to-all-start.5 = ((f32[32,1,1280]{2,1,0:T(1,128)}), f32[32,1,1280]{2,1,0:T(1,128)S(1)}, u32[]{:S(2)}, u32[]{:S(2)}) async-start(f32[32,1,1280]{2,1,0:T(1,128)} %bitcast.16), calls=%async_computation.5 | async-start | bytes 327680 | tf_op jit(solution)/shard_map/all_to_all | solution.py:539
  149.9 11.5 %all-to-all-start.6 = ((f32[32,1,1280]{2,1,0:T(1,128)}), f32[32,1,1280]{2,1,0:T(1,128)S(1)}, u32[]{:S(2)}, u32[]{:S(2)}) async-start(f32[32,1,1280]{2,1,0:T(1,128)} %bitcast.18), calls=%async_computation.6 | async-start | bytes 327680 | tf_op jit(solution)/shard_map/all_to_all | solution.py:539
